TPU v7x, 128 devices: a whole 4x4x4 slice. The times are simulated.
128 devices in a mesh: row: 8 (over y, x_lo), col: 16 (over x_hi, z, core).
Axes of the slice: x: 4 (x_hi: 2, x_lo: 2; x = x_hi * 2 + x_lo), y: 4, z: 4, core: 2. Of those that a mesh axis runs over, the one named last changes fastest.
Arguments:
- activations: bfloat16 [2048, 8192], P('col', 'row'), may hold values from -6 to 6
- output_grad: bfloat16 [2048, 8192], P('col', 'row'), may hold values from -1.5 to 1.5
- tile_counts: int32 [32], replicated, may hold values from 16 to 64, as said below
- w_gate: bfloat16 [8192, 15360], P('row', 'col'), may hold values from -0.0625 to 0.0625
- w_up: bfloat16 [8192, 15360], P('row', 'col'), may hold values from -0.0625 to 0.0625
- w_down: bfloat16 [15360, 8192], P('col', 'row'), may hold values from -0.046875 to 0.046875
Outputs:
- input_grad: bfloat16 [2048, 8192], P('col', 'row')
- grad_gate: bfloat16 [8192, 15360], P('row', 'col')
- grad_up: bfloat16 [8192, 15360], P('row', 'col')
- grad_down: bfloat16 [15360, 8192], P('col', 'row')
Inputs may be any that keep to these rules, and one draw needn't show every extreme that they name: `tile_counts`: number of live tokens at the start of each tile of 64 positions; some tile is full and some holds 16.
All inputs are finite; a program needn't handle non-finite values.
Results may differ from a plain program's by a relative error of at most 0.03.
Values may be sent and summed in bfloat16 or wider, within the bound.
No kernel may reach another device: no remote copies, remote signals or barrier semaphores. Data moves between devices by JAX's collectives and lax.ppermute only.
A program may use at most 128 MiB of HBM per device.

v0:
```python
import jax
import jax.numpy as jnp
from jax import lax
from jax.experimental import pallas as pl
from jax.experimental.pallas import tpu as pltpu
from jax.sharding import Mesh, PartitionSpec as P

TILE = 64
HEAD = 16
CAP = 1024
BF = jnp.bfloat16
F32 = jnp.float32


def dot(left, right, dims):
    return lax.dot_general(left, right, ((dims[:1], dims[1:]), ((), ())), preferred_element_type=F32)


def shift(value, axis, size, step):
    return lax.ppermute(value, axis, [(i, (i + step) % size) for i in range(size)])


def move(place, sources, shapes, copies):
    count = len(copies(0, 0))

    def kernel(place_ref, *refs):
        ins, outs, sems = refs[: len(sources)], refs[len(sources) : -1], refs[-1]
        jobs = [
            pltpu.make_async_copy(ins[i].at[src], outs[o].at[dst], sems.at[n])
            for n, (o, dst, i, src) in enumerate(copies(place_ref[0], place_ref[1]))
        ]
        for job in jobs:
            job.start()
        for job in jobs:
            job.wait()

    anywhere = pl.BlockSpec(memory_space=pl.ANY)
    return pl.pallas_call(
        kernel,
        out_shape=[jax.ShapeDtypeStruct(s, BF) for s in shapes],
        in_specs=[pl.BlockSpec(memory_space=pltpu.SMEM)] + [anywhere] * len(sources),
        out_specs=[pl.BlockSpec(memory_space=pltpu.VMEM)] * len(shapes),
        scratch_shapes=[pltpu.SemaphoreType.DMA((count,))],
    )(place, *sources)


def after(token, *values):
    return lax.optimization_barrier((*values, token))[:-1]


def blank(shapes):
    return pl.pallas_call(
        lambda *refs: None,
        out_shape=[jax.ShapeDtypeStruct(s, BF) for s in shapes],
        out_specs=[pl.BlockSpec(memory_space=pl.ANY)] * len(shapes),
    )()


def span(start, size):
    return pl.ds(start if isinstance(start, int) else pl.multiple_of(start, 8), size)


def join(place, blocks):
    rows, width = blocks[0].shape
    return move(place, blocks, [(len(blocks) * rows, width)], lambda y, xl: [(0, span(n * rows, rows), n, span(0, rows)) for n in range(len(blocks))])[0]


def by_core(place, moved, rows):
    return move(
        place, moved, [(8 * rows, moved[0].shape[1])],
        lambda y, xl: [(0, span((4 * d + n) * rows, rows), n, span(d * rows, rows)) for n in range(4) for d in (0, 1)],
    )[0]


def over_z(value):
    return [value] + [shift(value, "z", 4, -k) for k in (1, 2, 3)]


def project(place, sources, weights, rows, y_first):
    units, width = weights[0].shape
    wide = -(-units // 128) * 128
    compact = len(sources) > 2
    total = 8 * rows
    if y_first:
        cuts = [(k * 2 * rows, 2 * rows) for k in range(4)]
    else:
        cuts = [(n * 4 * rows, 4 * rows) for n in range(2)]
    shapes = [(3, size, wide) for _, size in cuts]
    if compact:
        shapes = [(total, width)] * 2 + shapes
    n_in = len(sources) + 3

    def kernel(place_ref, *refs):
        ins, w_refs, outs = refs[: len(sources)], refs[len(sources) : n_in], refs[n_in : n_in + len(shapes)]
        bufs, sems = refs[n_in + len(shapes) : -1], refs[-1]
        jobs = []

        def start(src, dst):
            job = pltpu.make_async_copy(src, dst, sems.at[len(jobs)])
            job.start()
            jobs.append(job)
            return job

        if compact:
            rank = ins[0][...]
            feeds = [start(ins[1 + i], bufs[3 + i]) for i in range(4)]
        else:
            feeds = []
            for i in (0, 1):
                for k in range(4):
                    for d in (0, 1):
                        block = ((place_ref[0] + k) % 4) * 2 + (place_ref[1] + d) % 2
                        feeds.append(start(ins[i].at[span(block * rows, rows)], bufs[3 + i].at[span((2 * k + d) * rows, rows)]))
        loads = [start(w_refs[i], bufs[i]) for i in range(3)]
        if compact:
            pick = (lax.broadcasted_iota(jnp.int32, (total, rank.shape[1]), 0) == rank).astype(F32).astype(BF)
            half = rank.shape[1] // 2
            for i in (0, 1):
                feeds[2 * i].wait()
                feeds[2 * i + 1].wait()
                outs[i][...] = (dot(pick[:, :half], bufs[3 + 2 * i][...], (1, 0)) + dot(pick[:, half:], bufs[4 + 2 * i][...], (1, 0))).astype(BF)
            lefts = outs[:2]
            packs = outs[2:]
        else:
            for feed in feeds:
                feed.wait()
            lefts = bufs[3:5]
            packs = outs
        for i in range(3):
            loads[i].wait()
            for (low, size), out in zip(cuts, packs):
                left = lefts[i // 2][low : low + size]
                out[i, :, :units] = dot(left, bufs[i][...], (1, 1)).astype(BF)
                out[i, :, units:] = jnp.zeros((size, wide - units), BF)

    anywhere = pl.BlockSpec(memory_space=pl.ANY)
    vmem = pl.BlockSpec(memory_space=pltpu.VMEM)
    smem = pl.BlockSpec(memory_space=pltpu.SMEM)
    scratch = [pltpu.VMEM(w.shape, BF) for w in weights]
    scratch += [pltpu.VMEM(s.shape, BF) for s in (sources[1:] if compact else sources)]
    return pl.pallas_call(
        kernel,
        out_shape=[jax.ShapeDtypeStruct(s, BF) for s in shapes],
        in_specs=[smem] + ([vmem] if compact else []) + [anywhere] * (n_in - compact),
        out_specs=[vmem] * len(shapes),
        scratch_shapes=scratch + [pltpu.SemaphoreType.DMA((19,))],
    )(place, *sources, *weights)


def unproject(place, pieces, jobs_of, total, weights, rank_col):
    units, width = weights[0].shape
    wide = pieces[0].shape[-1]
    arrays = list(pieces)
    expand = rank_col is not None
    half = (rank_col.shape[0] if expand else total) // 2
    count = len(jobs_of(0, 0))

    def kernel(place_ref, *refs):
        ins, w_refs = refs[: len(arrays)], refs[len(arrays) : len(arrays) + 2]
        rest = refs[len(arrays) + 2 :]
        if expand:
            rank, rest = rest[0][...], rest[1:]
        outs, bufs, sems = rest[:4], rest[4:6], rest[6]
        jobs = [
            pltpu.make_async_copy(ins[i].at[src], outs[o].at[dst], sems.at[n])
            for n, (o, dst, i, src) in enumerate(jobs_of(place_ref[0], place_ref[1]))
        ]
        jobs += [pltpu.make_async_copy(w_refs[i], bufs[i], sems.at[count + i]) for i in (0, 1)]
        for job in jobs:
            job.start()
        for job in jobs:
            job.wait()
        if expand:
            part = (dot(outs[0][:, :units], bufs[0][...], (1, 0)) + dot(outs[1][:, :units], bufs[1][...], (1, 0))).astype(BF)
            pick = (rank == lax.broadcasted_iota(jnp.int32, (rank.shape[0], total), 1)).astype(F32).astype(BF)
            for n in (0, 1):
                outs[2 + n][...] = dot(pick[n * half : (n + 1) * half], part, (1, 0)).astype(BF)
        else:
            for n in (0, 1):
                rows = slice(n * half, (n + 1) * half)
                outs[2 + n][...] = (dot(outs[0][rows, :units], bufs[0][...], (1, 0)) + dot(outs[1][rows, :units], bufs[1][...], (1, 0))).astype(BF)

    anywhere = pl.BlockSpec(memory_space=pl.ANY)
    vmem = pl.BlockSpec(memory_space=pltpu.VMEM)
    shapes = [(total, wide)] * 2 + [(half, width)] * 2
    return pl.pallas_call(
        kernel,
        out_shape=[jax.ShapeDtypeStruct(s, BF) for s in shapes],
        in_specs=[pl.BlockSpec(memory_space=pltpu.SMEM)] + [anywhere] * (len(arrays) + 2) + [vmem] * expand,
        out_specs=[vmem] * 4,
        scratch_shapes=[pltpu.VMEM((units, width), BF)] * 2 + [pltpu.SemaphoreType.DMA((count + 2,))],
    )(place, *arrays, *weights, *([rank_col] if expand else []))


def over_y(blocks, step):
    return [blocks[0]] + [shift(blocks[k], "y", 4, step * k) for k in (1, 2, 3)]


def add(blocks):
    return sum(b.astype(F32) for b in blocks[1:]) + blocks[0].astype(F32)


def pack_rows(place, blocks):
    n, rows, width = blocks[0].shape
    return move(
        place, blocks, [(n, len(blocks) * rows, width)],
        lambda y, xl: [(0, (i, span(k * rows, rows)), k, (i, span(0, rows))) for k in range(len(blocks)) for i in range(n)],
    )[0]


def swiglu_back(totals):
    gate_sum, up_sum, back_sum = totals[0], totals[1], totals[2]
    sigmoid_gate = jax.nn.sigmoid(gate_sum)
    hidden = gate_sum * sigmoid_gate * up_sum
    d_gate = back_sum * up_sum * sigmoid_gate * (1.0 + gate_sum * (1.0 - sigmoid_gate))
    d_up = back_sum * gate_sum * sigmoid_gate
    return hidden.astype(BF), jnp.stack([d_gate.astype(BF), d_up.astype(BF)])


def pipeline(cap, place, rank, x0, g0, received0, mine_x, other_x, mine_g, other_g, w_gate, w_up, w_down, sums):
    r0, r1 = x0.shape[0] // 8, cap // 16
    weights = (w_gate, w_up, w_down)
    units = w_gate.shape[0]
    block = (rank % (8 * r1)) // r1
    dxl, dy = (block + place[1]) % 2, (block // 2 + 4 - place[0]) % 4
    at = jnp.where(rank >= 8 * r1, dy * 2 + dxl + 8, dxl * 4 + dy) * r1 + rank % r1
    rank = jnp.where(rank < 0, -1, at)

    def near_far(total, rows):
        return total[:, :rows], shift(total[:, rows:].astype(BF), "xl", 2, 1).astype(F32)

    halves = (mine_x, other_x, mine_g, other_g)
    xa, ga, near_a, far_a = project(place, (rank[None, :], *halves), weights, r1, False)
    far_a = shift(far_a, "xl", 2, 1)
    near0, far0 = near_far(add(after(xa, *received0)), r0)
    (rank_b,) = after(near0, rank)
    xb, gb, *parts_b = project(place, (rank_b[None, :] - 8 * r1, *halves), weights, r1, True)
    received_b = over_y(parts_b, 1)
    total_a = add(after(xb, near_a, far_a))
    received_a = over_y([total_a[:, :r1]] + [total_a[:, k * r1 : (k + 1) * r1].astype(BF) for k in (1, 2, 3)], 1)
    near_b, far_b = near_far(add(after(received_a[0], *received_b)), r1)
    near0, far0 = after(near_b, near0, far0)
    h0, s0 = swiglu_back(near0 + far0)
    swap_s0 = shift(s0, "xl", 2, 1)
    ha, sa = swiglu_back(add(after(s0, *received_a)))
    all_a = over_y([sa] * 4, -1)
    pair0 = pack_rows(place, after(sa, s0, swap_s0))
    near_b, far_b = after(pair0, near_b, far_b)
    hb, sb = swiglu_back(near_b + far_b)
    swap_b = shift(sb, "xl", 2, 1)
    h_all = jnp.concatenate([h0, ha, hb], axis=0)[None]
    swap_h = shift(h_all, "xl", 2, 1)
    pair_h = pack_rows(place, after(sb, h_all, swap_h))
    all_a = pack_rows(place, after(pair_h, *all_a))
    pieces_a = [all_a, shift(all_a, "xl", 2, 1)]
    pair_b = pack_rows(place, after(all_a, sb, swap_b))
    all_b = over_y([pair_b] * 4, -1)
    pieces0 = over_y([pair0] * 4, -1)
    all_h = over_y([pair_h] * 4, -1)

    def jobs0(y, xl):
        return [
            (i, span((((y + k) % 4) * 2 + (xl + d) % 2) * r0, r0), k, (i, span(d * r0, r0)))
            for d in (0, 1) for k in range(4) for i in (0, 1)
        ]

    def jobs1(y, xl):
        jobs = [(i, span(n * 4 * r1, 4 * r1), n, (i, span(0, 4 * r1))) for n in range(2) for i in (0, 1)]
        return jobs + [(i, span((8 + 2 * n) * r1, 2 * r1), 2 + n, (i, span(0, 2 * r1))) for n in range(4) for i in (0, 1)]

    dgd, dud, *halves = unproject(place, after(pair_b, *pieces0[1:], *pieces_a, *all_b)[3:], jobs1, cap, weights[:2], rank[:, None])
    swap1 = shift(halves[1], "c", 2, 1)
    dg0, du0, *halves0 = unproject(place, after(dgd, *pieces0), jobs0, 8 * r0, weights[:2], None)
    swap0 = shift(halves0[1], "c", 2, 1)
    xd, gd = jnp.concatenate([xa, xb], axis=0), jnp.concatenate([ga, gb], axis=0)

    def outer(total, first, late, other_first, other_late):
        return (total + dot(first[:, :units], other_first, (0, 0)) + dot(late[:, :units], other_late, (0, 0))).astype(BF)

    rows0, rows1, width = r0 // 2, halves[0].shape[0] // 8, x0.shape[1]
    own1, swap1 = after(dg0, halves[0], swap1)
    total1 = (own1.astype(F32) + swap1.astype(F32)).reshape(2, 4, rows1, width)
    left, right = total1[..., : width // 2], total1[..., width // 2 :]
    far_left = shift(left[1].astype(BF), "xh", 2, 1)
    far_right = [shift(right[:, k].astype(BF), "z", 4, k) for k in (1, 2, 3)]
    (xd_late,) = after(total1, xd)
    grad_gate = outer(sums[2], dg0, dgd, x0, xd_late)
    own0, swap0, far_left, *far_right = after(grad_gate, halves0[0], swap0, far_left, *far_right)
    total0 = own0.astype(F32) + swap0.astype(F32)
    far0 = shift(total0[4 * rows0 :].astype(BF), "xh", 2, 1)
    left = left[0] + far_left.astype(F32)
    right = right[:, 0] + sum(f.astype(F32) for f in far_right)
    far_left = [shift(left[k].astype(BF), "z", 4, k) for k in (1, 2, 3)]
    far_right = shift(right[1].astype(BF), "xh", 2, 1)
    (xd_late,) = after((left[0] + right[0]).astype(BF), xd_late)
    grad_up = outer(sums[3], du0, dud, x0, xd_late)
    far0, far_right, *far_left = after(grad_up, far0, far_right, *far_left)
    total0 = total0[: 4 * rows0] + far0.astype(F32)
    out0 = total0[:rows0] + sum(shift(total0[k * rows0 : (k + 1) * rows0].astype(BF), "z", 4, k).astype(F32) for k in (1, 2, 3))
    out1 = jnp.concatenate([left[0] + sum(f.astype(F32) for f in far_left), right[0] + far_right.astype(F32)], axis=1)
    pieces = after(grad_up, *all_h)
    total = r0 + 2 * r1

    def copies(y, xl):
        jobs = []
        for k in range(4):
            for d in (0, 1):
                here = ((y + k) % 4) * 2 + (xl + d) % 2
                low = d * total
                jobs.append((0, span(here * r0, r0), k, (0, span(low, r0))))
                jobs.append((1, span((4 * d + k) * r1, r1), k, (0, span(low + r0, r1))))
                jobs.append((1, span((8 + 2 * k + d) * r1, r1), k, (0, span(low + r0 + r1, r1))))
        return jobs

    hidden0, hidden_d = move(place, pieces, [(8 * r0, h0.shape[1]), (cap, h0.shape[1])], copies)
    grad_down = outer(sums[4], hidden0, hidden_d, g0, gd)
    return (sums[0] + out0).astype(BF), (sums[1] + out1).astype(BF), grad_gate, grad_up, grad_down


def shards(activations, output_grad, tile_counts, w_gate, w_up, w_down):
    own_rows, width = activations.shape
    tiles, n_tiles = own_rows // TILE, tile_counts.shape[0]
    tail = TILE - HEAD
    y, xl = lax.axis_index("y"), lax.axis_index("xl")
    xh, z, c = lax.axis_index("xh"), lax.axis_index("z"), lax.axis_index("c")
    place = jnp.stack([y, xl]).astype(jnp.int32)
    live = jnp.sum(tile_counts) - HEAD * n_tiles

    w_gate, w_up = w_gate.T, w_up.T

    def one_pass(state):
        step, sums = state
        sums = [jnp.where(step > 0, value.astype(F32), 0.0) for value in sums]
        acts = activations.reshape(tiles, TILE, width)
        grads = output_grad.reshape(tiles, TILE, width)
        first = (step == 0).astype(BF) * jnp.concatenate([acts[:, :HEAD].reshape(-1, width), grads[:, :HEAD].reshape(-1, width)], axis=0)
        rows = tiles * HEAD
        far = shift(first, "xh", 2, 1)
        pair = join(place, [first, far])
        late_x, late_g = acts[:, HEAD:].reshape(-1, width), grads[:, HEAD:].reshape(-1, width)
        late_x, late_g = after(pair, late_x, late_g)
        moved_x = over_z(late_x)
        far_g = shift(late_g, "xh", 2, 1)
        mine = by_core(place, over_z(pair), 2 * rows)
        other = shift(mine, "c", 2, 1)
        pair_g = join(place, after(mine, late_g, far_g))
        moved_g = over_z(pair_g)
        mine, other = after(pair_g, mine, other)
        x0, g0 = move(
            place, [mine, other], [(16 * rows, width)] * 2,
            lambda y, xl: [(i, span((8 * d + n) * rows, rows), d, span((2 * n + i) * rows, rows)) for d in (0, 1) for n in range(8) for i in (0, 1)],
        )
        near_x = join(place, after(x0, *moved_x))
        far_x = shift(near_x, "xh", 2, 1)
        parts0 = project(place, after(near_x, x0, g0), (w_gate, w_up, w_down), x0.shape[0] // 8, True)
        received0 = over_y(parts0, 1)
        mine_g = by_core(place, after(parts0[0], received0[1], received0[3], *moved_g)[2:], late_x.shape[0])
        mine_x = join(place, after(mine_g, near_x, far_x))
        halves = (mine_x, shift(mine_x, "c", 2, 1), mine_g, shift(mine_g, "c", 2, 1))
        order = lax.iota(jnp.int32, n_tiles)
        dev, sub = order // tiles, order % tiles
        source = (((xh + (dev // 4) % 2) % 2) * 4 + (z + dev % 4) % 4) * 2 + (c + dev // 8) % 2
        wanted = source * tiles + sub
        counts = jnp.sum(jnp.where(wanted[:, None] == order[None, :], tile_counts[None, :], 0), axis=1)
        extra = counts - HEAD
        before = jnp.sum(jnp.where(order[None, :] < order[:, None], extra[None, :], 0), axis=1)
        slot = lax.iota(jnp.int32, tail)
        rank = jnp.where(slot[None, :] < extra[:, None], before[:, None] + slot[None, :], -1).reshape(-1)
        here = rank - step * CAP
        here = jnp.where((rank >= 0) & (here >= 0) & (here < CAP), here, -1)
        results = pipeline(CAP, place, here, x0, g0, received0, *halves, w_gate, w_up, w_down, sums)
        return step + 1, results

    rows = tiles * HEAD
    shapes = ((rows, width), (own_rows - rows, width), w_gate.shape, w_up.shape, w_down.shape)
    start = (jnp.int32(0), tuple(blank(shapes)))
    _, sums = lax.while_loop(lambda state: state[0] * CAP < jnp.maximum(live, 1), one_pass, start)
    out0, out1, grad_gate, grad_up, grad_down = sums
    input_grad = jnp.concatenate([out0.reshape(tiles, HEAD, width), out1.reshape(tiles, tail, width)], axis=1)
    return (input_grad.reshape(own_rows, width), grad_gate.T, grad_up.T, grad_down)


def solution(mesh):
    fine = Mesh(mesh.devices.reshape(4, 2, 2, 4, 2), ("y", "xl", "xh", "z", "c"))
    row, col = ("y", "xl"), ("xh", "z", "c")
    in_specs = (P(col, row), P(col, row), P(), P(row, col), P(row, col), P(col, row))
    out_specs = (P(col, row), P(row, col), P(row, col), P(col, row))
    return jax.shard_map(shards, mesh=fine, in_specs=in_specs, out_specs=out_specs, check_vma=False)
```

profile of v0, /device:TPU:0, one launch (start us, length us, event | category | flops | bytes accessed | tf_op | source)
XLA Modules:
  0.0 369.5 jit_solution(16894233868176454698)
XLA Ops:
  4.4 363.3 %while.21 = (s32[]{:T(128)}, bf16[32,1024]{1,0:T(8,128)(2,1)}, bf16[96,1024]{1,0:T(8,128)(2,1)}, bf16[960,1024]{1,0:T(8,128)(2,1)}, bf16[960,1024]{1,0:T(8,128)(...) while((s32[]{:T(128)}, bf16[32,1024]{1,0:T(8,128)(2,1)}, ...), condition=%wide.region_4.5_spmd, body=%wide.region_1.4_spmd.sunk | while | flops 9105185792 | bytes 403179456 | solution.py:377
  4.7 3.2 collective-permute-start
  7.9 3.5 collective-permute-done.refs_1_
  14.3 4.3 %collective-permute-start.1 = (bf16[128,1024]{1,0:T(8,128)(2,1)}, bf16[128,1024]{1,0:T(8,128)(2,1)S(1)}, u32[]{:S(2)}, u32[]{:S(2)}) collective-permute-start(bf16[128,1024]{1,0:T(8,128)(2,1)} %body.73.refs_0_), channel_id=1, source_target_pairs={{0,6},{2,0},{4,2},{6,4},{1,7},{3,1},{5,3},{7,5},{8,14},{10,8},{12,... | collective-permute-start | bytes 786440 | tf_op jit(solution)/shard_map/while/body/ppermute | solution.py:20
  19.8 9.4 %collective-permute-done.1.refs_1_ = bf16[128,1024]{1,0:T(8,128)(2,1)S(1)} collective-permute-done((bf16[128,1024]{1,0:T(8,128)(2,1)}, bf16[128,1024]{1,0:T(8,128)(2,1)S(1)}, u32[]{:S(2)}, u32[]{:S(2)}) %collective-permute-start.1) | collective-permute-done | bytes 262176 | tf_op jit(solution)/shard_map/while/body/ppermute | solution.py:20
  29.5 3.0 collective-permute-done.3.refs_3_
  33.2 2.9 body.74.refs_0_
  36.3 3.1 collective-permute-start.5
  41.4 3.8 %collective-permute-done.5.refs_1_ = bf16[96,1024]{1,0:T(8,128)(2,1)} collective-permute-done((bf16[96,1024]{1,0:T(8,128)(2,1)S(1)}, bf16[96,1024]{1,0:T(8,128)(2,1)}, u32[]{:S(2)}, u32[]{:S(2)}) %collective-permute-start.5) | collective-permute-done | bytes 196640 | tf_op jit(solution)/shard_map/while/body/ppermute | solution.py:20
  49.7 3.7 body.76
  53.5 2.7 body.77.refs_0_
  56.2 10.9 %body.78 = (bf16[3,128,1024]{2,1,0:T(8,128)(2,1)}, bf16[3,128,1024]{2,1,0:T(8,128)(2,1)}, bf16[3,128,1024]{2,1,0:T(8,128)(2,1)}, bf16[3,128,1024]{2,1,0:T(8,128)(2,1)}) custom-call(s32[2]{0:T(128)S(1)} %get-tuple-element.943.place_ref, bf16[512,1024]{1,0:T(8,128)(2,1)} %get-tuple-element.774.refs_0_, bf16[512,1024]{1,0:T(8,128)(2,1)} %get-tuple-element.775.refs_1_, ...), custom_call_target="tpu_custom_call" | custom-call | tf_op jit(solution)/shard_map/while/body/pallas_call | solution.py:141
  67.1 3.1 collective-permute-start.11
  70.2 3.0 collective-permute-start.12
  74.3 12.5 %collective-permute-done.14.refs_2_ = bf16[192,1024]{1,0:T(8,128)(2,1)S(1)} collective-permute-done((bf16[192,1024]{1,0:T(8,128)(2,1)S(1)}, bf16[192,1024]{1,0:T(8,128)(2,1)S(1)}, u32[]{:S(2)}, u32[]{:S(2)}) %collective-permute-start.14) | collective-permute-done | bytes 393248 | tf_op jit(solution)/shard_map/while/body/ppermute | solution.py:20
  86.8 6.3 %collective-permute-done.15.refs_3_ = bf16[192,1024]{1,0:T(8,128)(2,1)S(1)} collective-permute-done((bf16[192,1024]{1,0:T(8,128)(2,1)S(1)}, bf16[192,1024]{1,0:T(8,128)(2,1)S(1)}, u32[]{:S(2)}, u32[]{:S(2)}) %collective-permute-start.15) | collective-permute-done | bytes 393248 | tf_op jit(solution)/shard_map/while/body/ppermute | solution.py:20
  93.8 3.2 body.79.refs_3_
  97.1 3.1 body.80.refs_1_
  109.3 11.4 %body.81 = (bf16[512,1024]{1,0:T(8,128)(2,1)}, bf16[512,1024]{1,0:T(8,128)(2,1)}, bf16[3,256,1024]{2,1,0:T(8,128)(2,1)}, bf16[3,256,1024]{2,1,0:T(8,128)(2,1)}) custom-call(s32[2]{0:T(128)} %copy-done.30, s32[1,1536]{1,0:T(1,128)} %fusion.143.refs_0_, bf16[768,1024]{1,0:T(8,128)(2,1)} %body.80.refs_1_, bf16[768,1024]{1,0:T(8,128)(2,1)} %collective-permute-done.16.refs_2_, ...), custom_call_target="tpu_custom_call" | custom-call | tf_op jit(solution)/shard_map/while/body/pallas_call | solution.py:141
  122.3 5.0 %collective-permute-done.10 = bf16[3,128,1024]{2,1,0:T(8,128)(2,1)} collective-permute-done((bf16[3,128,1024]{2,1,0:T(8,128)(2,1)}, bf16[3,128,1024]{2,1,0:T(8,128)(2,1)}, u32[]{:S(2)}, u32[]{:S(2)}) %collective-permute-start.10) | collective-permute-done | bytes 786464 | tf_op jit(solution)/shard_map/while/body/ppermute | solution.py:20
  132.3 15.0 %body.82 = (bf16[512,1024]{1,0:T(8,128)(2,1)}, bf16[512,1024]{1,0:T(8,128)(2,1)}, bf16[3,128,1024]{2,1,0:T(8,128)(2,1)}, bf16[3,128,1024]{2,1,0:T(8,128)(2,1)}, ...) custom-call(s32[2]{0:T(128)} %copy-done.30, s32[1,1536]{1,0:T(1,128)} %sub.274.refs_0_, ...), custom_call_target="tpu_custom_call" | custom-call | tf_op jit(solution)/shard_map/while/body/pallas_call | solution.py:141
  147.9 3.8 %collective-permute-start.20 = (bf16[3,128,1024]{2,1,0:T(8,128)(2,1)}, bf16[3,128,1024]{2,1,0:T(8,128)(2,1)S(1)}, u32[]{:S(2)}, u32[]{:S(2)}) collective-permute-start(bf16[3,128,1024]{2,1,0:T(8,128)(2,1)} %get-tuple-element.794), channel_id=1, source_target_pairs={{0,64},{32,96},{64,0},{96,32},{1,65},{33,97},{65,1},{97,33},{2,66}... | collective-permute-start | bytes 2359304 | tf_op jit(solution)/shard_map/while/body/ppermute | solution.py:20
  151.9 13.7 %collective-permute-done.18 = bf16[3,64,1024]{2,1,0:T(8,128)(2,1)} collective-permute-done((bf16[3,64,1024]{2,1,0:T(8,128)(2,1)}, bf16[3,64,1024]{2,1,0:T(8,128)(2,1)}, u32[]{:S(2)}, u32[]{:S(2)}) %collective-permute-start.18) | collective-permute-done | bytes 393248 | tf_op jit(solution)/shard_map/while/body/ppermute | solution.py:20
  166.7 2.7 fusion.145
  169.5 15.8 %collective-permute-done.20 = bf16[3,128,1024]{2,1,0:T(8,128)(2,1)S(1)} collective-permute-done((bf16[3,128,1024]{2,1,0:T(8,128)(2,1)}, bf16[3,128,1024]{2,1,0:T(8,128)(2,1)S(1)}, u32[]{:S(2)}, u32[]{:S(2)}) %collective-permute-start.20) | collective-permute-done | bytes 786464 | tf_op jit(solution)/shard_map/while/body/ppermute | solution.py:20
  186.7 2.9 collective-permute-start.25
  194.1 3.3 collective-permute-done.24
  197.5 9.6 %collective-permute-done.25 = bf16[3,64,1024]{2,1,0:T(8,128)(2,1)S(1)} collective-permute-done((bf16[3,64,1024]{2,1,0:T(8,128)(2,1)S(1)}, bf16[3,64,1024]{2,1,0:T(8,128)(2,1)S(1)}, u32[]{:S(2)}, u32[]{:S(2)}) %collective-permute-start.25) | collective-permute-done | bytes 393248 | tf_op jit(solution)/shard_map/while/body/ppermute | solution.py:20
  217.4 3.0 collective-permute-start.27
  222.3 3.6 collective-permute-done.34.refs_1_
  227.3 2.7 body.84.refs_0_
  230.0 3.2 collective-permute-done.32.refs_3_
  233.2 3.0 body.85.refs_0_
  240.4 3.3 collective-permute-start.37
  244.5 5.7 %collective-permute-start.39 = (bf16[2,128,1024]{2,1,0:T(8,128)(2,1)}, bf16[2,128,1024]{2,1,0:T(8,128)(2,1)}, u32[]{:S(2)}, u32[]{:S(2)}) collective-permute-start(bf16[2,128,1024]{2,1,0:T(8,128)(2,1)} %body.86.refs_2_), channel_id=1, source_target_pairs={{0,32},{32,64},{64,96},{96,0},{1,33},{33,65},{65,97},{97,1},{2,34}... | collective-permute-start | bytes 1572872 | tf_op jit(solution)/shard_map/while/body/ppermute | solution.py:20
  250.2 3.3 fusion.149.refs_8_
  253.5 11.9 %collective-permute-done.29.refs_3_ = bf16[2,128,1024]{2,1,0:T(8,128)(2,1)} collective-permute-done((bf16[2,128,1024]{2,1,0:T(8,128)(2,1)}, bf16[2,128,1024]{2,1,0:T(8,128)(2,1)}, u32[]{:S(2)}, u32[]{:S(2)}) %collective-permute-start.29) | collective-permute-done | bytes 524320 | tf_op jit(solution)/shard_map/while/body/ppermute | solution.py:20
  267.0 9.7 %collective-permute-done.39.refs_5_ = bf16[2,128,1024]{2,1,0:T(8,128)(2,1)} collective-permute-done((bf16[2,128,1024]{2,1,0:T(8,128)(2,1)}, bf16[2,128,1024]{2,1,0:T(8,128)(2,1)}, u32[]{:S(2)}, u32[]{:S(2)}) %collective-permute-start.39) | collective-permute-done | bytes 524320 | tf_op jit(solution)/shard_map/while/body/ppermute | solution.py:20
  276.7 13.1 %body.87 = (bf16[1024,1024]{1,0:T(8,128)(2,1)}, bf16[1024,1024]{1,0:T(8,128)(2,1)}, bf16[768,1024]{1,0:T(8,128)(2,1)}, bf16[768,1024]{1,0:T(8,128)(2,1)}) custom-call(s32[2]{0:T(128)} %copy-done.30, bf16[2,256,1024]{2,1,0:T(8,128)(2,1)} %body.85.refs_0_, bf16[2,256,1024]{2,1,0:T(8,128)(2,1)} %collective-permute-done.35.refs_1_, ...), custom_call_target="tpu_custom_call" | custom-call | tf_op jit(solution)/shard_map/while/body/pallas_call | solution.py:186
  289.9 3.1 pad_maximum_fusion.13
  295.1 6.2 %body.88 = (bf16[512,1024]{1,0:T(8,128)(2,1)}, bf16[512,1024]{1,0:T(8,128)(2,1)}, bf16[256,1024]{1,0:T(8,128)(2,1)}, bf16[256,1024]{1,0:T(8,128)(2,1)}) custom-call(s32[2]{0:T(128)S(1)} %copy-done.31, bf16[2,128,1024]{2,1,0:T(8,128)(2,1)} %body.83.refs_0_, bf16[2,128,1024]{2,1,0:T(8,128)(2,1)} %collective-permute-done.27.refs_1_, ...), custom_call_target="tpu_custom_call" | custom-call | tf_op jit(solution)/shard_map/while/body/pallas_call | solution.py:186
  302.8 2.7 convert_add_fusion.11
  320.1 11.8 %collective-permute-done.56.refs_3_ = bf16[1,384,1024]{2,1,0:T(8,128)(2,1)} collective-permute-done((bf16[1,384,1024]{2,1,0:T(8,128)(2,1)}, bf16[1,384,1024]{2,1,0:T(8,128)(2,1)}, u32[]{:S(2)}, u32[]{:S(2)}) %collective-permute-start.56) | collective-permute-done | bytes 786464 | tf_op jit(solution)/shard_map/while/body/ppermute | solution.py:20
  332.4 4.4 %body.89 = (bf16[512,1024]{1,0:T(8,128)(2,1)}, bf16[1024,1024]{1,0:T(8,128)(2,1)}) custom-call(s32[2]{0:T(128)S(1)} %copy-done.31, bf16[1,384,1024]{2,1,0:T(8,128)(2,1)} %body.84.refs_0_, bf16[1,384,1024]{2,1,0:T(8,128)(2,1)} %collective-permute-done.54.refs_1_, bf16[1,384,1024]{2,1,0:T(8,128)(2,1)} %collective-permute-done.55.refs_2_, ...), custom_call_target="tpu_custom_call" | custom-call | tf_op jit(solution)/shard_map/while/body/pallas_call | solution.py:38
  336.8 2.8 fusion.161
  350.8 3.0 add_convert_fusion.8
  353.9 3.7 %collective-permute-done.46 = bf16[128,1024]{1,0:T(8,128)(2,1)S(1)} collective-permute-done((bf16[128,1024]{1,0:T(8,128)(2,1)S(1)}, bf16[128,1024]{1,0:T(8,128)(2,1)S(1)}, u32[]{:S(2)}, u32[]{:S(2)}) %collective-permute-start.46) | collective-permute-done | bytes 262176 | tf_op jit(solution)/shard_map/while/body/ppermute | solution.py:20
  362.1 2.8 collective-permute-done.52
  (262 shorter events, 97.9 us)
Async XLA Ops:
  14.3 15.0 %collective-permute-start.1 = (bf16[128,1024]{1,0:T(8,128)(2,1)}, bf16[128,1024]{1,0:T(8,128)(2,1)S(1)}, u32[]{:S(2)}, u32[]{:S(2)}) collective-permute-start(bf16[128,1024]{1,0:T(8,128)(2,1)} %body.73.refs_0_), channel_id=1, source_target_pairs={{0,6},{2,0},{4,2},{6,4},{1,7},{3,1},{5,3},{7,5},{8,14},{10,8},{12,... | collective-permute-start | bytes 786440 | tf_op jit(solution)/shard_map/while/body/ppermute | solution.py:20
  18.6 11.0 %collective-permute-start.2 = (bf16[128,1024]{1,0:T(8,128)(2,1)}, bf16[128,1024]{1,0:T(8,128)(2,1)S(1)}, u32[]{:S(2)}, u32[]{:S(2)}) collective-permute-start(bf16[128,1024]{1,0:T(8,128)(2,1)} %body.73.refs_0_), channel_id=1, source_target_pairs={{0,4},{2,6},{4,0},{6,2},{1,5},{3,7},{5,1},{7,3},{8,12},{10,14},{12... | collective-permute-start | bytes 786440 | tf_op jit(solution)/shard_map/while/body/ppermute | solution.py:20
  18.6 13.9 %collective-permute-start.3 = (bf16[128,1024]{1,0:T(8,128)(2,1)}, bf16[128,1024]{1,0:T(8,128)(2,1)S(1)}, u32[]{:S(2)}, u32[]{:S(2)}) collective-permute-start(bf16[128,1024]{1,0:T(8,128)(2,1)} %body.73.refs_0_), channel_id=1, source_target_pairs={{0,2},{2,4},{4,6},{6,0},{1,3},{3,5},{5,7},{7,1},{8,10},{10,12},{12... | collective-permute-start | bytes 786440 | tf_op jit(solution)/shard_map/while/body/ppermute | solution.py:20
  36.1 12.7 %collective-permute-start.4 = (bf16[512,1024]{1,0:T(8,128)(2,1)}, bf16[512,1024]{1,0:T(8,128)(2,1)S(1)}, u32[]{:S(2)}, u32[]{:S(2)}) collective-permute-start(bf16[512,1024]{1,0:T(8,128)(2,1)} %body.74.refs_0_), channel_id=1, source_target_pairs={{0,1},{1,0},{2,3},{3,2},{4,5},{5,4},{6,7},{7,6},{8,9},{9,8},{10,11... | collective-permute-start | bytes 3145736 | tf_op jit(solution)/shard_map/while/body/ppermute | solution.py:20
  39.4 14.0 %collective-permute-start.6 = (bf16[96,1024]{1,0:T(8,128)(2,1)S(1)}, bf16[96,1024]{1,0:T(8,128)(2,1)}, u32[]{:S(2)}, u32[]{:S(2)}) collective-permute-start(bf16[96,1024]{1,0:T(8,128)(2,1)S(1)} %bitcast.161), channel_id=1, source_target_pairs={{0,6},{2,0},{4,2},{6,4},{1,7},{3,1},{5,3},{7,5},{8,14},{10,8},{12,... | collective-permute-start | bytes 589832 | tf_op jit(solution)/shard_map/while/body/ppermute | solution.py:20
  40.5 13.0 %collective-permute-start.7 = (bf16[96,1024]{1,0:T(8,128)(2,1)S(1)}, bf16[96,1024]{1,0:T(8,128)(2,1)}, u32[]{:S(2)}, u32[]{:S(2)}) collective-permute-start(bf16[96,1024]{1,0:T(8,128)(2,1)S(1)} %bitcast.162), channel_id=1, source_target_pairs={{0,4},{2,6},{4,0},{6,2},{1,5},{3,7},{5,1},{7,3},{8,12},{10,14},{12... | collective-permute-start | bytes 589832 | tf_op jit(solution)/shard_map/while/body/ppermute | solution.py:20
  40.6 12.8 %collective-permute-start.8 = (bf16[96,1024]{1,0:T(8,128)(2,1)S(1)}, bf16[96,1024]{1,0:T(8,128)(2,1)}, u32[]{:S(2)}, u32[]{:S(2)}) collective-permute-start(bf16[96,1024]{1,0:T(8,128)(2,1)S(1)} %bitcast.163), channel_id=1, source_target_pairs={{0,2},{2,4},{4,6},{6,0},{1,3},{3,5},{5,7},{7,1},{8,10},{10,12},{12... | collective-permute-start | bytes 589832 | tf_op jit(solution)/shard_map/while/body/ppermute | solution.py:20
  47.6 25.8 %collective-permute-start.13 = (bf16[192,1024]{1,0:T(8,128)(2,1)}, bf16[192,1024]{1,0:T(8,128)(2,1)}, u32[]{:S(2)}, u32[]{:S(2)}) collective-permute-start(bf16[192,1024]{1,0:T(8,128)(2,1)} %body.75.refs_0_), channel_id=1, source_target_pairs={{0,6},{2,0},{4,2},{6,4},{1,7},{3,1},{5,3},{7,5},{8,14},{10,8},{12,... | collective-permute-start | bytes 1179656 | tf_op jit(solution)/shard_map/while/body/ppermute | solution.py:20
  67.1 25.9 %collective-permute-start.11 = (bf16[3,128,1024]{2,1,0:T(8,128)(2,1)}, bf16[3,128,1024]{2,1,0:T(8,128)(2,1)}, u32[]{:S(2)}, u32[]{:S(2)}) collective-permute-start(bf16[3,128,1024]{2,1,0:T(8,128)(2,1)} %get-tuple-element.779), channel_id=1, source_target_pairs={{0,96},{32,0},{64,32},{96,64},{1,97},{33,1},{65,33},{97,65},{2,98}... | collective-permute-start | bytes 2359304 | tf_op jit(solution)/shard_map/while/body/ppermute | solution.py:20
  70.2 22.8 %collective-permute-start.9 = (bf16[3,128,1024]{2,1,0:T(8,128)(2,1)}, bf16[3,128,1024]{2,1,0:T(8,128)(2,1)}, u32[]{:S(2)}, u32[]{:S(2)}) collective-permute-start(bf16[3,128,1024]{2,1,0:T(8,128)(2,1)} %get-tuple-element.777), channel_id=1, source_target_pairs={{0,32},{32,64},{64,96},{96,0},{1,33},{33,65},{65,97},{97,1},{2,34}... | collective-permute-start | bytes 2359304 | tf_op jit(solution)/shard_map/while/body/ppermute | solution.py:20
  70.2 26.8 %collective-permute-start.12 = (bf16[384,1024]{1,0:T(8,128)(2,1)}, bf16[384,1024]{1,0:T(8,128)(2,1)}, u32[]{:S(2)}, u32[]{:S(2)}) collective-permute-start(bf16[384,1024]{1,0:T(8,128)(2,1)} %body.77.refs_0_), channel_id=1, source_target_pairs={{0,8},{8,0},{1,9},{9,1},{2,10},{10,2},{3,11},{11,3},{4,12},{12,4},... | collective-permute-start | bytes 2359304 | tf_op jit(solution)/shard_map/while/body/ppermute | solution.py:20
  73.2 13.6 %collective-permute-start.14 = (bf16[192,1024]{1,0:T(8,128)(2,1)S(1)}, bf16[192,1024]{1,0:T(8,128)(2,1)S(1)}, u32[]{:S(2)}, u32[]{:S(2)}) collective-permute-start(bf16[192,1024]{1,0:T(8,128)(2,1)S(1)} %copy-done.7), channel_id=1, source_target_pairs={{0,4},{2,6},{4,0},{6,2},{1,5},{3,7},{5,1},{7,3},{8,12},{10,14},{12... | collective-permute-start | bytes 1179656 | tf_op jit(solution)/shard_map/while/body/ppermute | solution.py:20
  73.4 19.7 %collective-permute-start.15 = (bf16[192,1024]{1,0:T(8,128)(2,1)S(1)}, bf16[192,1024]{1,0:T(8,128)(2,1)S(1)}, u32[]{:S(2)}, u32[]{:S(2)}) collective-permute-start(bf16[192,1024]{1,0:T(8,128)(2,1)S(1)} %copy-done.7), channel_id=1, source_target_pairs={{0,2},{2,4},{4,6},{6,0},{1,3},{3,5},{5,7},{7,1},{8,10},{10,12},{12... | collective-permute-start | bytes 1179656 | tf_op jit(solution)/shard_map/while/body/ppermute | solution.py:20
  105.6 21.7 %collective-permute-start.10 = (bf16[3,128,1024]{2,1,0:T(8,128)(2,1)}, bf16[3,128,1024]{2,1,0:T(8,128)(2,1)}, u32[]{:S(2)}, u32[]{:S(2)}) collective-permute-start(bf16[3,128,1024]{2,1,0:T(8,128)(2,1)} %get-tuple-element.778), channel_id=1, source_target_pairs={{0,64},{32,96},{64,0},{96,32},{1,65},{33,97},{65,1},{97,33},{2,66}... | collective-permute-start | bytes 2359304 | tf_op jit(solution)/shard_map/while/body/ppermute | solution.py:20
  120.7 46.0 %collective-permute-start.22 = (bf16[3,256,1024]{2,1,0:T(8,128)(2,1)}, bf16[3,256,1024]{2,1,0:T(8,128)(2,1)}, u32[]{:S(2)}, u32[]{:S(2)}) collective-permute-start(bf16[3,256,1024]{2,1,0:T(8,128)(2,1)} %get-tuple-element.797), channel_id=1, source_target_pairs={{0,16},{16,0},{1,17},{17,1},{2,18},{18,2},{3,19},{19,3},{4,20},{20... | collective-permute-start | bytes 4718600 | tf_op jit(solution)/shard_map/while/body/ppermute | solution.py:20
  130.6 35.1 %collective-permute-start.18 = (bf16[3,64,1024]{2,1,0:T(8,128)(2,1)}, bf16[3,64,1024]{2,1,0:T(8,128)(2,1)}, u32[]{:S(2)}, u32[]{:S(2)}) collective-permute-start(bf16[3,64,1024]{2,1,0:T(8,128)(2,1)} %slice.533), channel_id=1, source_target_pairs={{0,16},{16,0},{1,17},{17,1},{2,18},{18,2},{3,19},{19,3},{4,20},{20... | collective-permute-start | bytes 1179656 | tf_op jit(solution)/shard_map/while/body/ppermute | solution.py:20
  147.3 22.2 %collective-permute-start.19 = (bf16[3,128,1024]{2,1,0:T(8,128)(2,1)}, bf16[3,128,1024]{2,1,0:T(8,128)(2,1)S(1)}, u32[]{:S(2)}, u32[]{:S(2)}) collective-permute-start(bf16[3,128,1024]{2,1,0:T(8,128)(2,1)} %get-tuple-element.793), channel_id=1, source_target_pairs={{0,32},{32,64},{64,96},{96,0},{1,33},{33,65},{65,97},{97,1},{2,34}... | collective-permute-start | bytes 2359304 | tf_op jit(solution)/shard_map/while/body/ppermute | solution.py:20
  147.9 37.3 %collective-permute-start.20 = (bf16[3,128,1024]{2,1,0:T(8,128)(2,1)}, bf16[3,128,1024]{2,1,0:T(8,128)(2,1)S(1)}, u32[]{:S(2)}, u32[]{:S(2)}) collective-permute-start(bf16[3,128,1024]{2,1,0:T(8,128)(2,1)} %get-tuple-element.794), channel_id=1, source_target_pairs={{0,64},{32,96},{64,0},{96,32},{1,65},{33,97},{65,1},{97,33},{2,66}... | collective-permute-start | bytes 2359304 | tf_op jit(solution)/shard_map/while/body/ppermute | solution.py:20
  151.8 33.5 %collective-permute-start.21 = (bf16[3,128,1024]{2,1,0:T(8,128)(2,1)}, bf16[3,128,1024]{2,1,0:T(8,128)(2,1)S(1)}, u32[]{:S(2)}, u32[]{:S(2)}) collective-permute-start(bf16[3,128,1024]{2,1,0:T(8,128)(2,1)} %get-tuple-element.795), channel_id=1, source_target_pairs={{0,96},{32,0},{64,32},{96,64},{1,97},{33,1},{65,33},{97,65},{2,98}... | collective-permute-start | bytes 2359304 | tf_op jit(solution)/shard_map/while/body/ppermute | solution.py:20
  185.9 11.5 %collective-permute-start.24 = (bf16[3,64,1024]{2,1,0:T(8,128)(2,1)S(1)}, bf16[3,64,1024]{2,1,0:T(8,128)(2,1)S(1)}, u32[]{:S(2)}, u32[]{:S(2)}) collective-permute-start(bf16[3,64,1024]{2,1,0:T(8,128)(2,1)S(1)} %get-tuple-element.811), channel_id=1, source_target_pairs={{0,32},{32,64},{64,96},{96,0},{1,33},{33,65},{65,97},{97,1},{2,34}... | collective-permute-start | bytes 1179656 | tf_op jit(solution)/shard_map/while/body/ppermute | solution.py:20
  186.7 20.3 %collective-permute-start.25 = (bf16[3,64,1024]{2,1,0:T(8,128)(2,1)S(1)}, bf16[3,64,1024]{2,1,0:T(8,128)(2,1)S(1)}, u32[]{:S(2)}, u32[]{:S(2)}) collective-permute-start(bf16[3,64,1024]{2,1,0:T(8,128)(2,1)S(1)} %get-tuple-element.812), channel_id=1, source_target_pairs={{0,64},{32,96},{64,0},{96,32},{1,65},{33,97},{65,1},{97,33},{2,66}... | collective-permute-start | bytes 1179656 | tf_op jit(solution)/shard_map/while/body/ppermute | solution.py:20
  189.6 17.4 %collective-permute-start.26 = (bf16[3,64,1024]{2,1,0:T(8,128)(2,1)S(1)}, bf16[3,64,1024]{2,1,0:T(8,128)(2,1)S(1)}, u32[]{:S(2)}, u32[]{:S(2)}) collective-permute-start(bf16[3,64,1024]{2,1,0:T(8,128)(2,1)S(1)} %get-tuple-element.813), channel_id=1, source_target_pairs={{0,96},{32,0},{64,32},{96,64},{1,97},{33,1},{65,33},{97,65},{2,98}... | collective-permute-start | bytes 1179656 | tf_op jit(solution)/shard_map/while/body/ppermute | solution.py:20
  191.1 19.3 %collective-permute-start.23 = (bf16[2,64,1024]{2,1,0:T(8,128)(2,1)S(1)}, bf16[2,64,1024]{2,1,0:T(8,128)(2,1)}, u32[]{:S(2)}, u32[]{:S(2)}) collective-permute-start(bf16[2,64,1024]{2,1,0:T(8,128)(2,1)S(1)} %pad_maximum_fusion.10.refs_0_), channel_id=1, source_target_pairs={{0,16},{16,0},{1,17},{17,1},{2,18},{18,2},{3,19},{19,3},{4,20},{20... | collective-permute-start | bytes 786440 | tf_op jit(solution)/shard_map/while/body/ppermute | solution.py:20
  192.8 20.2 %collective-permute-start.33 = (bf16[3,64,1024]{2,1,0:T(8,128)(2,1)}, bf16[3,64,1024]{2,1,0:T(8,128)(2,1)}, u32[]{:S(2)}, u32[]{:S(2)}) collective-permute-start(bf16[3,64,1024]{2,1,0:T(8,128)(2,1)} %slice.536), channel_id=1, source_target_pairs={{0,16},{16,0},{1,17},{17,1},{2,18},{18,2},{3,19},{19,3},{4,20},{20... | collective-permute-start | bytes 1179656 | tf_op jit(solution)/shard_map/while/body/ppermute | solution.py:20
  208.2 12.2 %collective-permute-start.30 = (bf16[2,64,1024]{2,1,0:T(8,128)(2,1)}, bf16[2,64,1024]{2,1,0:T(8,128)(2,1)}, u32[]{:S(2)}, u32[]{:S(2)}) collective-permute-start(bf16[2,64,1024]{2,1,0:T(8,128)(2,1)} %pad_maximum_fusion.11.refs_0_), channel_id=1, source_target_pairs={{0,96},{32,0},{64,32},{96,64},{1,97},{33,1},{65,33},{97,65},{2,98}... | collective-permute-start | bytes 786440 | tf_op jit(solution)/shard_map/while/body/ppermute | solution.py:20
  215.0 10.8 %collective-permute-start.34 = (bf16[1,192,1024]{2,1,0:T(8,128)(2,1)S(1)}, bf16[1,192,1024]{2,1,0:T(8,128)(2,1)S(1)}, u32[]{:S(2)}, u32[]{:S(2)}) collective-permute-start(bf16[1,192,1024]{2,1,0:T(8,128)(2,1)S(1)} %maximum_bitcast_fusion.2.refs_0_), channel_id=1, source_target_pairs={{0,16},{16,0},{1,17},{17,1},{2,18},{18,2},{3,19},{19,3},{4,20},{20... | collective-permute-start | bytes 1179656 | tf_op jit(solution)/shard_map/while/body/ppermute | solution.py:20
  216.5 13.5 %collective-permute-start.31 = (bf16[2,64,1024]{2,1,0:T(8,128)(2,1)}, bf16[2,64,1024]{2,1,0:T(8,128)(2,1)}, u32[]{:S(2)}, u32[]{:S(2)}) collective-permute-start(bf16[2,64,1024]{2,1,0:T(8,128)(2,1)} %pad_maximum_fusion.11.refs_0_), channel_id=1, source_target_pairs={{0,64},{32,96},{64,0},{96,32},{1,65},{33,97},{65,1},{97,33},{2,66}... | collective-permute-start | bytes 786440 | tf_op jit(solution)/shard_map/while/body/ppermute | solution.py:20
  217.2 16.0 %collective-permute-start.32 = (bf16[2,64,1024]{2,1,0:T(8,128)(2,1)}, bf16[2,64,1024]{2,1,0:T(8,128)(2,1)}, u32[]{:S(2)}, u32[]{:S(2)}) collective-permute-start(bf16[2,64,1024]{2,1,0:T(8,128)(2,1)} %pad_maximum_fusion.11.refs_0_), channel_id=1, source_target_pairs={{0,32},{32,64},{64,96},{96,0},{1,33},{33,65},{65,97},{97,1},{2,34}... | collective-permute-start | bytes 786440 | tf_op jit(solution)/shard_map/while/body/ppermute | solution.py:20
  217.4 26.3 %collective-permute-start.27 = (bf16[2,128,1024]{2,1,0:T(8,128)(2,1)}, bf16[2,128,1024]{2,1,0:T(8,128)(2,1)}, u32[]{:S(2)}, u32[]{:S(2)}) collective-permute-start(bf16[2,128,1024]{2,1,0:T(8,128)(2,1)} %body.83.refs_0_), channel_id=1, source_target_pairs={{0,96},{32,0},{64,32},{96,64},{1,97},{33,1},{65,33},{97,65},{2,98}... | collective-permute-start | bytes 1572872 | tf_op jit(solution)/shard_map/while/body/ppermute | solution.py:20
  220.4 24.1 %collective-permute-start.28 = (bf16[2,128,1024]{2,1,0:T(8,128)(2,1)}, bf16[2,128,1024]{2,1,0:T(8,128)(2,1)}, u32[]{:S(2)}, u32[]{:S(2)}) collective-permute-start(bf16[2,128,1024]{2,1,0:T(8,128)(2,1)} %body.83.refs_0_), channel_id=1, source_target_pairs={{0,64},{32,96},{64,0},{96,32},{1,65},{33,97},{65,1},{97,33},{2,66}... | collective-permute-start | bytes 1572872 | tf_op jit(solution)/shard_map/while/body/ppermute | solution.py:20
  225.9 11.9 %collective-permute-start.36 = (bf16[2,64,1024]{2,1,0:T(8,128)(2,1)S(1)}, bf16[2,64,1024]{2,1,0:T(8,128)(2,1)}, u32[]{:S(2)}, u32[]{:S(2)}) collective-permute-start(bf16[2,64,1024]{2,1,0:T(8,128)(2,1)S(1)} %pad_maximum_fusion.12.refs_0_), channel_id=1, source_target_pairs={{0,16},{16,0},{1,17},{17,1},{2,18},{18,2},{3,19},{19,3},{4,20},{20... | collective-permute-start | bytes 786440 | tf_op jit(solution)/shard_map/while/body/ppermute | solution.py:20
  236.2 40.5 %collective-permute-start.35 = (bf16[2,256,1024]{2,1,0:T(8,128)(2,1)}, bf16[2,256,1024]{2,1,0:T(8,128)(2,1)}, u32[]{:S(2)}, u32[]{:S(2)}) collective-permute-start(bf16[2,256,1024]{2,1,0:T(8,128)(2,1)} %body.85.refs_0_), channel_id=1, source_target_pairs={{0,16},{16,0},{1,17},{17,1},{2,18},{18,2},{3,19},{19,3},{4,20},{20... | collective-permute-start | bytes 3145736 | tf_op jit(solution)/shard_map/while/body/ppermute | solution.py:20
  237.7 27.7 %collective-permute-start.29 = (bf16[2,128,1024]{2,1,0:T(8,128)(2,1)}, bf16[2,128,1024]{2,1,0:T(8,128)(2,1)}, u32[]{:S(2)}, u32[]{:S(2)}) collective-permute-start(bf16[2,128,1024]{2,1,0:T(8,128)(2,1)} %body.83.refs_0_), channel_id=1, source_target_pairs={{0,32},{32,64},{64,96},{96,0},{1,33},{33,65},{65,97},{97,1},{2,34}... | collective-permute-start | bytes 1572872 | tf_op jit(solution)/shard_map/while/body/ppermute | solution.py:20
  240.4 25.0 %collective-permute-start.37 = (bf16[2,128,1024]{2,1,0:T(8,128)(2,1)}, bf16[2,128,1024]{2,1,0:T(8,128)(2,1)}, u32[]{:S(2)}, u32[]{:S(2)}) collective-permute-start(bf16[2,128,1024]{2,1,0:T(8,128)(2,1)} %body.86.refs_2_), channel_id=1, source_target_pairs={{0,96},{32,0},{64,32},{96,64},{1,97},{33,1},{65,33},{97,65},{2,98}... | collective-permute-start | bytes 1572872 | tf_op jit(solution)/shard_map/while/body/ppermute | solution.py:20
  243.7 23.3 %collective-permute-start.38 = (bf16[2,128,1024]{2,1,0:T(8,128)(2,1)}, bf16[2,128,1024]{2,1,0:T(8,128)(2,1)}, u32[]{:S(2)}, u32[]{:S(2)}) collective-permute-start(bf16[2,128,1024]{2,1,0:T(8,128)(2,1)} %body.86.refs_2_), channel_id=1, source_target_pairs={{0,64},{32,96},{64,0},{96,32},{1,65},{33,97},{65,1},{97,33},{2,66}... | collective-permute-start | bytes 1572872 | tf_op jit(solution)/shard_map/while/body/ppermute | solution.py:20
  244.5 32.2 %collective-permute-start.39 = (bf16[2,128,1024]{2,1,0:T(8,128)(2,1)}, bf16[2,128,1024]{2,1,0:T(8,128)(2,1)}, u32[]{:S(2)}, u32[]{:S(2)}) collective-permute-start(bf16[2,128,1024]{2,1,0:T(8,128)(2,1)} %body.86.refs_2_), channel_id=1, source_target_pairs={{0,32},{32,64},{64,96},{96,0},{1,33},{33,65},{65,97},{97,1},{2,34}... | collective-permute-start | bytes 1572872 | tf_op jit(solution)/shard_map/while/body/ppermute | solution.py:20
  289.8 11.8 %collective-permute-start.41 = (bf16[768,1024]{1,0:T(8,128)(2,1)}, bf16[768,1024]{1,0:T(8,128)(2,1)S(1)}, u32[]{:S(2)}, u32[]{:S(2)}) collective-permute-start(bf16[768,1024]{1,0:T(8,128)(2,1)} %get-tuple-element.850), channel_id=1, source_target_pairs={{0,1},{1,0},{2,3},{3,2},{4,5},{5,4},{6,7},{7,6},{8,9},{9,8},{10,11... | collective-permute-start | bytes 4718600 | tf_op jit(solution)/shard_map/while/body/ppermute | solution.py:20
  293.0 25.0 %collective-permute-start.54 = (bf16[1,384,1024]{2,1,0:T(8,128)(2,1)}, bf16[1,384,1024]{2,1,0:T(8,128)(2,1)}, u32[]{:S(2)}, u32[]{:S(2)}) collective-permute-start(bf16[1,384,1024]{2,1,0:T(8,128)(2,1)} %body.84.refs_0_), channel_id=1, source_target_pairs={{0,96},{32,0},{64,32},{96,64},{1,97},{33,1},{65,33},{97,65},{2,98}... | collective-permute-start | bytes 2359304 | tf_op jit(solution)/shard_map/while/body/ppermute | solution.py:20
  293.5 24.5 %collective-permute-start.55 = (bf16[1,384,1024]{2,1,0:T(8,128)(2,1)}, bf16[1,384,1024]{2,1,0:T(8,128)(2,1)}, u32[]{:S(2)}, u32[]{:S(2)}) collective-permute-start(bf16[1,384,1024]{2,1,0:T(8,128)(2,1)} %body.84.refs_0_), channel_id=1, source_target_pairs={{0,64},{32,96},{64,0},{96,32},{1,65},{33,97},{65,1},{97,33},{2,66}... | collective-permute-start | bytes 2359304 | tf_op jit(solution)/shard_map/while/body/ppermute | solution.py:20
  294.2 37.6 %collective-permute-start.56 = (bf16[1,384,1024]{2,1,0:T(8,128)(2,1)}, bf16[1,384,1024]{2,1,0:T(8,128)(2,1)}, u32[]{:S(2)}, u32[]{:S(2)}) collective-permute-start(bf16[1,384,1024]{2,1,0:T(8,128)(2,1)} %body.84.refs_0_), channel_id=1, source_target_pairs={{0,32},{32,64},{64,96},{96,0},{1,33},{33,65},{65,97},{97,1},{2,34}... | collective-permute-start | bytes 2359304 | tf_op jit(solution)/shard_map/while/body/ppermute | solution.py:20
  301.3 38.3 %collective-permute-start.40 = (bf16[256,1024]{1,0:T(8,128)(2,1)}, bf16[256,1024]{1,0:T(8,128)(2,1)}, u32[]{:S(2)}, u32[]{:S(2)}) collective-permute-start(bf16[256,1024]{1,0:T(8,128)(2,1)} %get-tuple-element.848), channel_id=1, source_target_pairs={{0,1},{1,0},{2,3},{3,2},{4,5},{5,4},{6,7},{7,6},{8,9},{9,8},{10,11... | collective-permute-start | bytes 1572872 | tf_op jit(solution)/shard_map/while/body/ppermute | solution.py:20
  309.1 30.6 %collective-permute-start.42 = (bf16[4,96,512]{2,1,0:T(8,128)(2,1)}, bf16[4,96,512]{2,1,0:T(8,128)(2,1)S(1)}, u32[]{:S(2)}, u32[]{:S(2)}) collective-permute-start(bf16[4,96,512]{2,1,0:T(8,128)(2,1)} %slice_bitcast_fusion.14), channel_id=1, source_target_pairs={{0,8},{8,0},{1,9},{9,1},{2,10},{10,2},{3,11},{11,3},{4,12},{12,4},... | collective-permute-start | bytes 1179656 | tf_op jit(solution)/shard_map/while/body/ppermute | solution.py:20
  318.0 21.6 %collective-permute-start.43 = (bf16[2,96,512]{2,1,0:T(8,128)(2,1)}, bf16[2,96,512]{2,1,0:T(8,128)(2,1)}, u32[]{:S(2)}, u32[]{:S(2)}) collective-permute-start(bf16[2,96,512]{2,1,0:T(8,128)(2,1)} %get-tuple-element.854), channel_id=1, source_target_pairs={{0,2},{2,4},{4,6},{6,0},{1,3},{3,5},{5,7},{7,1},{8,10},{10,12},{12... | collective-permute-start | bytes 589832 | tf_op jit(solution)/shard_map/while/body/ppermute | solution.py:20
  318.0 21.6 %collective-permute-start.44 = (bf16[2,96,512]{2,1,0:T(8,128)(2,1)}, bf16[2,96,512]{2,1,0:T(8,128)(2,1)}, u32[]{:S(2)}, u32[]{:S(2)}) collective-permute-start(bf16[2,96,512]{2,1,0:T(8,128)(2,1)} %get-tuple-element.855), channel_id=1, source_target_pairs={{0,4},{2,6},{4,0},{6,2},{1,5},{3,7},{5,1},{7,3},{8,12},{10,14},{12... | collective-permute-start | bytes 589832 | tf_op jit(solution)/shard_map/while/body/ppermute | solution.py:20
  339.8 14.0 %collective-permute-start.48 = (bf16[96,512]{1,0:T(8,128)(2,1)S(1)}, bf16[96,512]{1,0:T(8,128)(2,1)S(1)}, u32[]{:S(2)}, u32[]{:S(2)}) collective-permute-start(bf16[96,512]{1,0:T(8,128)(2,1)S(1)} %get-tuple-element.865), channel_id=1, source_target_pairs={{0,2},{2,4},{4,6},{6,0},{1,3},{3,5},{5,7},{7,1},{8,10},{10,12},{12... | collective-permute-start | bytes 294920 | tf_op jit(solution)/shard_map/while/body/ppermute | solution.py:20
  341.3 12.5 %collective-permute-start.49 = (bf16[96,512]{1,0:T(8,128)(2,1)S(1)}, bf16[96,512]{1,0:T(8,128)(2,1)S(1)}, u32[]{:S(2)}, u32[]{:S(2)}) collective-permute-start(bf16[96,512]{1,0:T(8,128)(2,1)S(1)} %get-tuple-element.866), channel_id=1, source_target_pairs={{0,4},{2,6},{4,0},{6,2},{1,5},{3,7},{5,1},{7,3},{8,12},{10,14},{12... | collective-permute-start | bytes 294920 | tf_op jit(solution)/shard_map/while/body/ppermute | solution.py:20
  342.5 11.3 %collective-permute-start.50 = (bf16[96,512]{1,0:T(8,128)(2,1)S(1)}, bf16[96,512]{1,0:T(8,128)(2,1)S(1)}, u32[]{:S(2)}, u32[]{:S(2)}) collective-permute-start(bf16[96,512]{1,0:T(8,128)(2,1)S(1)} %get-tuple-element.867), channel_id=1, source_target_pairs={{0,6},{2,0},{4,2},{6,4},{1,7},{3,1},{5,3},{7,5},{8,14},{10,8},{12,... | collective-permute-start | bytes 294920 | tf_op jit(solution)/shard_map/while/body/ppermute | solution.py:20
  348.3 9.3 %collective-permute-start.46 = (bf16[128,1024]{1,0:T(8,128)(2,1)S(1)}, bf16[128,1024]{1,0:T(8,128)(2,1)S(1)}, u32[]{:S(2)}, u32[]{:S(2)}) collective-permute-start(bf16[128,1024]{1,0:T(8,128)(2,1)S(1)} %slice.537), channel_id=1, source_target_pairs={{0,8},{8,0},{1,9},{9,1},{2,10},{10,2},{3,11},{11,3},{4,12},{12,4},... | collective-permute-start | bytes 786440 | tf_op jit(solution)/shard_map/while/body/ppermute | solution.py:20
  (63 other events, 555.3 us)
where the time goes:
time: 374 us; the launch traced here: 370 us
  waiting for transfers between devices  137 us (37%)
  Pallas kernels  91.9 us (25%)
  starting transfers between devices  76.7 us (21%)
  other arithmetic  28.5 us (8%)
  local copies, waits for them, and re-layouts  17.3 us (5%)
  matrix products  14 us (4%)
    ppermute x57, waiting for transfers between devices, shift(): lax.ppermute(value, axis, [(i, (i + step) % size) for i in range(size)])  137 us
    ppermute x57, starting transfers between devices, shift(): lax.ppermute(value, axis, [(i, (i + step) % size) for i in range(size)])  76.7 us
    pallas_call x3, Pallas kernels, project(): pl.pallas_call(kernel, out_shape=[jax.ShapeDtypeStruct(s, BF) for s in sh...  37.3 us
    pallas_call x12, Pallas kernels, move(): pl.pallas_call(kernel, out_shape=[jax.ShapeDtypeStruct(s, BF) for s in sh...  35.3 us
    pallas_call x2, Pallas kernels, unproject(): pl.pallas_call(kernel, out_shape=[jax.ShapeDtypeStruct(s, BF) for s in sh...  19.3 us
    dot_general x6, matrix products, dot(): lax.dot_general(left, right, ((dims[:1], dims[1:]), ((), ())), preferred_...  14 us
    while x104, local copies, waits for them, and re-layouts  7.65 us
  transfers between devices with their start and end apart: 57, of which 23 were waited for; matrix products, arithmetic and copies ran while one was open for 13% of the time, Pallas kernels for 19%

commit v1 on v0

--- a/solution.py
+++ b/solution.py
@@ -298,7 +298,7 @@
     total0 = total0[: 4 * rows0] + far0.astype(F32)
     out0 = total0[:rows0] + sum(shift(total0[k * rows0 : (k + 1) * rows0].astype(BF), "z", 4, k).astype(F32) for k in (1, 2, 3))
     out1 = jnp.concatenate([left[0] + sum(f.astype(F32) for f in far_left), right[0] + far_right.astype(F32)], axis=1)
-    pieces = after(grad_up, *all_h)
+    pieces = after(total0.astype(BF), *all_h)
     total = r0 + 2 * r1
 
     def copies(y, xl):

time: 374 us -> 377 us (level)
  waiting for transfers between devices: 137 us -> 143 us
    ppermute x57, waiting for transfers between devices: 137 us -> 143 us  [shift(): lax.ppermute(value, axis, [(i, (i + step) % size) for i in range(size)])]
    while x104 -> x110, local copies, waits for them, and re-layouts: 7.65 us -> 10.2 us
  transfers between devices with their start and end apart: 57 -> 57, of which waited for: 23 -> 28; matrix products, arithmetic and copies ran while one was open for 13% -> 11% of each run, Pallas kernels for 19% -> 22%
where the time goes in v1:
time: 377 us; the launch traced here: 375 us
  waiting for transfers between devices  143 us (38%)
  Pallas kernels  92.2 us (24%)
  starting transfers between devices  78.5 us (21%)
  other arithmetic  26.6 us (7%)
  local copies, waits for them, and re-layouts  17.6 us (5%)
  matrix products  13.8 us (4%)
    ppermute x57, waiting for transfers between devices, shift(): lax.ppermute(value, axis, [(i, (i + step) % size) for i in range(size)])  143 us
    ppermute x57, starting transfers between devices, shift(): lax.ppermute(value, axis, [(i, (i + step) % size) for i in range(size)])  78.5 us
    pallas_call x3, Pallas kernels, project(): pl.pallas_call(kernel, out_shape=[jax.ShapeDtypeStruct(s, BF) for s in sh...  37.3 us
    pallas_call x12, Pallas kernels, move(): pl.pallas_call(kernel, out_shape=[jax.ShapeDtypeStruct(s, BF) for s in sh...  35.5 us
    pallas_call x2, Pallas kernels, unproject(): pl.pallas_call(kernel, out_shape=[jax.ShapeDtypeStruct(s, BF) for s in sh...  19.4 us
    dot_general x6, matrix products, dot(): lax.dot_general(left, right, ((dims[:1], dims[1:]), ((), ())), preferred_...  13.8 us
    while x110, local copies, waits for them, and re-layouts  10.2 us
  transfers between devices with their start and end apart: 57, of which 28 were waited for; matrix products, arithmetic and copies ran while one was open for 11% of the time, Pallas kernels for 22%

profile of v1, /device:TPU:0, one launch (start us, length us, event | category | flops | bytes accessed | tf_op | source)
XLA Modules:
  0.0 375.1 jit_solution(2029504061504169372)
XLA Ops:
  5.0 368.2 %while.21 = (s32[]{:T(128)}, bf16[32,1024]{1,0:T(8,128)(2,1)}, bf16[96,1024]{1,0:T(8,128)(2,1)}, bf16[960,1024]{1,0:T(8,128)(2,1)}, bf16[960,1024]{1,0:T(8,128)(...) while((s32[]{:T(128)}, bf16[32,1024]{1,0:T(8,128)(2,1)}, ...), condition=%wide.region_4.5_spmd, body=%wide.region_1.4_spmd.sunk | while | flops 9105185792 | bytes 413671456 | solution.py:377
  6.0 3.2 collective-permute-start
  9.2 3.5 collective-permute-done.refs_1_
  17.8 3.6 collective-permute-start.2
  22.4 4.1 %collective-permute-done.3.refs_3_ = bf16[128,1024]{1,0:T(8,128)(2,1)S(1)} collective-permute-done((bf16[128,1024]{1,0:T(8,128)(2,1)}, bf16[128,1024]{1,0:T(8,128)(2,1)S(1)}, u32[]{:S(2)}, u32[]{:S(2)}) %collective-permute-start.3) | collective-permute-done | bytes 262176 | tf_op jit(solution)/shard_map/while/body/ppermute | solution.py:20
  26.4 5.9 %collective-permute-done.2.refs_2_ = bf16[128,1024]{1,0:T(8,128)(2,1)S(1)} collective-permute-done((bf16[128,1024]{1,0:T(8,128)(2,1)}, bf16[128,1024]{1,0:T(8,128)(2,1)S(1)}, u32[]{:S(2)}, u32[]{:S(2)}) %collective-permute-start.2) | collective-permute-done | bytes 262176 | tf_op jit(solution)/shard_map/while/body/ppermute | solution.py:20
  33.8 2.9 body.74.refs_0_
  36.9 3.1 collective-permute-start.5
  49.8 3.7 body.76
  53.5 2.7 body.77.refs_0_
  56.3 11.0 %body.78 = (bf16[3,128,1024]{2,1,0:T(8,128)(2,1)}, bf16[3,128,1024]{2,1,0:T(8,128)(2,1)}, bf16[3,128,1024]{2,1,0:T(8,128)(2,1)}, bf16[3,128,1024]{2,1,0:T(8,128)(2,1)}) custom-call(s32[2]{0:T(128)S(1)} %get-tuple-element.943.place_ref, bf16[512,1024]{1,0:T(8,128)(2,1)} %get-tuple-element.774.refs_0_, bf16[512,1024]{1,0:T(8,128)(2,1)} %get-tuple-element.775.refs_1_, ...), custom_call_target="tpu_custom_call" | custom-call | tf_op jit(solution)/shard_map/while/body/pallas_call | solution.py:141
  70.6 3.0 collective-permute-start.12
  77.2 7.6 %collective-permute-done.14.refs_2_ = bf16[192,1024]{1,0:T(8,128)(2,1)S(1)} collective-permute-done((bf16[192,1024]{1,0:T(8,128)(2,1)S(1)}, bf16[192,1024]{1,0:T(8,128)(2,1)S(1)}, u32[]{:S(2)}, u32[]{:S(2)}) %collective-permute-start.14) | collective-permute-done | bytes 393248 | tf_op jit(solution)/shard_map/while/body/ppermute | solution.py:20
  84.9 8.5 %collective-permute-done.13.refs_1_ = bf16[192,1024]{1,0:T(8,128)(2,1)S(1)} collective-permute-done((bf16[192,1024]{1,0:T(8,128)(2,1)S(1)}, bf16[192,1024]{1,0:T(8,128)(2,1)S(1)}, u32[]{:S(2)}, u32[]{:S(2)}) %collective-permute-start.13) | collective-permute-done | bytes 393248 | tf_op jit(solution)/shard_map/while/body/ppermute | solution.py:20
  94.1 3.2 body.79.refs_3_
  97.4 3.1 body.80.refs_1_
  108.7 11.4 %body.81 = (bf16[512,1024]{1,0:T(8,128)(2,1)}, bf16[512,1024]{1,0:T(8,128)(2,1)}, bf16[3,256,1024]{2,1,0:T(8,128)(2,1)}, bf16[3,256,1024]{2,1,0:T(8,128)(2,1)}) custom-call(s32[2]{0:T(128)} %copy-done.32, s32[1,1536]{1,0:T(1,128)} %fusion.143.refs_0_, bf16[768,1024]{1,0:T(8,128)(2,1)} %body.80.refs_1_, bf16[768,1024]{1,0:T(8,128)(2,1)} %collective-permute-done.16.refs_2_, ...), custom_call_target="tpu_custom_call" | custom-call | tf_op jit(solution)/shard_map/while/body/pallas_call | solution.py:141
  121.7 5.1 %collective-permute-done.10 = bf16[3,128,1024]{2,1,0:T(8,128)(2,1)} collective-permute-done((bf16[3,128,1024]{2,1,0:T(8,128)(2,1)}, bf16[3,128,1024]{2,1,0:T(8,128)(2,1)}, u32[]{:S(2)}, u32[]{:S(2)}) %collective-permute-start.10) | collective-permute-done | bytes 786464 | tf_op jit(solution)/shard_map/while/body/ppermute | solution.py:20
  131.9 14.9 %body.82 = (bf16[512,1024]{1,0:T(8,128)(2,1)}, bf16[512,1024]{1,0:T(8,128)(2,1)}, bf16[3,128,1024]{2,1,0:T(8,128)(2,1)}, bf16[3,128,1024]{2,1,0:T(8,128)(2,1)}, ...) custom-call(s32[2]{0:T(128)} %copy-done.32, s32[1,1536]{1,0:T(1,128)} %sub.274.refs_0_, ...), custom_call_target="tpu_custom_call" | custom-call | tf_op jit(solution)/shard_map/while/body/pallas_call | solution.py:141
  147.1 2.9 collective-permute-start.20
  151.4 13.7 %collective-permute-done.18 = bf16[3,64,1024]{2,1,0:T(8,128)(2,1)} collective-permute-done((bf16[3,64,1024]{2,1,0:T(8,128)(2,1)}, bf16[3,64,1024]{2,1,0:T(8,128)(2,1)}, u32[]{:S(2)}, u32[]{:S(2)}) %collective-permute-start.18) | collective-permute-done | bytes 393248 | tf_op jit(solution)/shard_map/while/body/ppermute | solution.py:20
  166.2 2.7 fusion.145
  168.9 14.7 %collective-permute-done.19 = bf16[3,128,1024]{2,1,0:T(8,128)(2,1)S(1)} collective-permute-done((bf16[3,128,1024]{2,1,0:T(8,128)(2,1)}, bf16[3,128,1024]{2,1,0:T(8,128)(2,1)S(1)}, u32[]{:S(2)}, u32[]{:S(2)}) %collective-permute-start.19) | collective-permute-done | bytes 786464 | tf_op jit(solution)/shard_map/while/body/ppermute | solution.py:20
  186.2 2.9 collective-permute-start.25
  193.6 3.3 collective-permute-done.24
  196.9 9.6 %collective-permute-done.25 = bf16[3,64,1024]{2,1,0:T(8,128)(2,1)S(1)} collective-permute-done((bf16[3,64,1024]{2,1,0:T(8,128)(2,1)S(1)}, bf16[3,64,1024]{2,1,0:T(8,128)(2,1)S(1)}, u32[]{:S(2)}, u32[]{:S(2)}) %collective-permute-start.25) | collective-permute-done | bytes 393248 | tf_op jit(solution)/shard_map/while/body/ppermute | solution.py:20
  208.3 2.9 collective-permute-start.31
  218.6 9.8 %collective-permute-done.34.refs_1_ = bf16[1,192,1024]{2,1,0:T(8,128)(2,1)S(1)} collective-permute-done((bf16[1,192,1024]{2,1,0:T(8,128)(2,1)S(1)}, bf16[1,192,1024]{2,1,0:T(8,128)(2,1)S(1)}, u32[]{:S(2)}, u32[]{:S(2)}) %collective-permute-start.34) | collective-permute-done | bytes 393248 | tf_op jit(solution)/shard_map/while/body/ppermute | solution.py:20
  230.8 2.7 body.84.refs_0_
  236.8 3.0 body.85.refs_0_
  240.5 2.6 body.86.refs_2_
  245.6 5.0 %collective-permute-done.29.refs_3_ = bf16[2,128,1024]{2,1,0:T(8,128)(2,1)} collective-permute-done((bf16[2,128,1024]{2,1,0:T(8,128)(2,1)S(1)}, bf16[2,128,1024]{2,1,0:T(8,128)(2,1)}, u32[]{:S(2)}, u32[]{:S(2)}) %collective-permute-start.29) | collective-permute-done | bytes 524320 | tf_op jit(solution)/shard_map/while/body/ppermute | solution.py:20
  252.8 2.9 collective-permute-done.28.refs_2_
  255.7 4.6 %collective-permute-done.27.refs_1_ = bf16[2,128,1024]{2,1,0:T(8,128)(2,1)} collective-permute-done((bf16[2,128,1024]{2,1,0:T(8,128)(2,1)S(1)}, bf16[2,128,1024]{2,1,0:T(8,128)(2,1)}, u32[]{:S(2)}, u32[]{:S(2)}) %collective-permute-start.27) | collective-permute-done | bytes 524320 | tf_op jit(solution)/shard_map/while/body/ppermute | solution.py:20
  261.8 11.1 %collective-permute-done.39.refs_5_ = bf16[2,128,1024]{2,1,0:T(8,128)(2,1)} collective-permute-done((bf16[2,128,1024]{2,1,0:T(8,128)(2,1)}, bf16[2,128,1024]{2,1,0:T(8,128)(2,1)}, u32[]{:S(2)}, u32[]{:S(2)}) %collective-permute-start.39) | collective-permute-done | bytes 524320 | tf_op jit(solution)/shard_map/while/body/ppermute | solution.py:20
  273.0 5.2 %collective-permute-done.38.refs_4_ = bf16[2,128,1024]{2,1,0:T(8,128)(2,1)} collective-permute-done((bf16[2,128,1024]{2,1,0:T(8,128)(2,1)}, bf16[2,128,1024]{2,1,0:T(8,128)(2,1)}, u32[]{:S(2)}, u32[]{:S(2)}) %collective-permute-start.38) | collective-permute-done | bytes 524320 | tf_op jit(solution)/shard_map/while/body/ppermute | solution.py:20
  278.4 3.3 fusion.149.refs_8_
  282.7 13.2 %body.87 = (bf16[1024,1024]{1,0:T(8,128)(2,1)}, bf16[1024,1024]{1,0:T(8,128)(2,1)}, bf16[768,1024]{1,0:T(8,128)(2,1)}, bf16[768,1024]{1,0:T(8,128)(2,1)}) custom-call(s32[2]{0:T(128)} %copy-done.32, bf16[2,256,1024]{2,1,0:T(8,128)(2,1)} %body.85.refs_0_, bf16[2,256,1024]{2,1,0:T(8,128)(2,1)} %collective-permute-done.35.refs_1_, ...), custom_call_target="tpu_custom_call" | custom-call | tf_op jit(solution)/shard_map/while/body/pallas_call | solution.py:186
  296.3 2.7 pad_maximum_fusion.13
  299.0 8.9 %collective-permute-done.56.refs_3_ = bf16[1,384,1024]{2,1,0:T(8,128)(2,1)} collective-permute-done((bf16[1,384,1024]{2,1,0:T(8,128)(2,1)}, bf16[1,384,1024]{2,1,0:T(8,128)(2,1)}, u32[]{:S(2)}, u32[]{:S(2)}) %collective-permute-start.56) | collective-permute-done | bytes 786464 | tf_op jit(solution)/shard_map/while/body/ppermute | solution.py:20
  307.9 3.5 collective-permute-done.54.refs_1_
  311.4 4.4 %body.89 = (bf16[512,1024]{1,0:T(8,128)(2,1)}, bf16[1024,1024]{1,0:T(8,128)(2,1)}) custom-call(s32[2]{0:T(128)S(1)} %copy-done.33, bf16[1,384,1024]{2,1,0:T(8,128)(2,1)} %body.84.refs_0_, bf16[1,384,1024]{2,1,0:T(8,128)(2,1)} %collective-permute-done.54.refs_1_, bf16[1,384,1024]{2,1,0:T(8,128)(2,1)} %collective-permute-done.55.refs_2_, ...), custom_call_target="tpu_custom_call" | custom-call | tf_op jit(solution)/shard_map/while/body/pallas_call | solution.py:38
  319.0 3.0 add_convert_fusion.8
  323.3 6.2 %body.88 = (bf16[512,1024]{1,0:T(8,128)(2,1)}, bf16[512,1024]{1,0:T(8,128)(2,1)}, bf16[256,1024]{1,0:T(8,128)(2,1)}, bf16[256,1024]{1,0:T(8,128)(2,1)}) custom-call(s32[2]{0:T(128)S(1)} %copy-done.33, bf16[2,128,1024]{2,1,0:T(8,128)(2,1)} %body.83.refs_0_, bf16[2,128,1024]{2,1,0:T(8,128)(2,1)} %collective-permute-done.27.refs_1_, ...), custom_call_target="tpu_custom_call" | custom-call | tf_op jit(solution)/shard_map/while/body/pallas_call | solution.py:186
  337.7 3.2 collective-permute-start.44
  345.6 4.5 %collective-permute-done.44 = bf16[2,96,512]{2,1,0:T(8,128)(2,1)S(1)} collective-permute-done((bf16[2,96,512]{2,1,0:T(8,128)(2,1)S(1)}, bf16[2,96,512]{2,1,0:T(8,128)(2,1)S(1)}, u32[]{:S(2)}, u32[]{:S(2)}) %collective-permute-start.44) | collective-permute-done | bytes 196640 | tf_op jit(solution)/shard_map/while/body/ppermute | solution.py:20
  355.0 3.2 collective-permute-start.49
  367.6 3.4 collective-permute-done.52
  (268 shorter events, 111.9 us)
Async XLA Ops:
  15.6 10.9 %collective-permute-start.3 = (bf16[128,1024]{1,0:T(8,128)(2,1)}, bf16[128,1024]{1,0:T(8,128)(2,1)S(1)}, u32[]{:S(2)}, u32[]{:S(2)}) collective-permute-start(bf16[128,1024]{1,0:T(8,128)(2,1)} %body.73.refs_0_), channel_id=1, source_target_pairs={{0,2},{2,4},{4,6},{6,0},{1,3},{3,5},{5,7},{7,1},{8,10},{10,12},{12... | collective-permute-start | bytes 786440 | tf_op jit(solution)/shard_map/while/body/ppermute | solution.py:20
  17.8 14.6 %collective-permute-start.2 = (bf16[128,1024]{1,0:T(8,128)(2,1)}, bf16[128,1024]{1,0:T(8,128)(2,1)S(1)}, u32[]{:S(2)}, u32[]{:S(2)}) collective-permute-start(bf16[128,1024]{1,0:T(8,128)(2,1)} %body.73.refs_0_), channel_id=1, source_target_pairs={{0,4},{2,6},{4,0},{6,2},{1,5},{3,7},{5,1},{7,3},{8,12},{10,14},{12... | collective-permute-start | bytes 786440 | tf_op jit(solution)/shard_map/while/body/ppermute | solution.py:20
  21.4 11.0 %collective-permute-start.1 = (bf16[128,1024]{1,0:T(8,128)(2,1)}, bf16[128,1024]{1,0:T(8,128)(2,1)S(1)}, u32[]{:S(2)}, u32[]{:S(2)}) collective-permute-start(bf16[128,1024]{1,0:T(8,128)(2,1)} %body.73.refs_0_), channel_id=1, source_target_pairs={{0,6},{2,0},{4,2},{6,4},{1,7},{3,1},{5,3},{7,5},{8,14},{10,8},{12,... | collective-permute-start | bytes 786440 | tf_op jit(solution)/shard_map/while/body/ppermute | solution.py:20
  36.7 12.1 %collective-permute-start.4 = (bf16[512,1024]{1,0:T(8,128)(2,1)}, bf16[512,1024]{1,0:T(8,128)(2,1)S(1)}, u32[]{:S(2)}, u32[]{:S(2)}) collective-permute-start(bf16[512,1024]{1,0:T(8,128)(2,1)} %body.74.refs_0_), channel_id=1, source_target_pairs={{0,1},{1,0},{2,3},{3,2},{4,5},{5,4},{6,7},{7,6},{8,9},{9,8},{10,11... | collective-permute-start | bytes 3145736 | tf_op jit(solution)/shard_map/while/body/ppermute | solution.py:20
  36.9 9.0 %collective-permute-start.5 = (bf16[96,1024]{1,0:T(8,128)(2,1)S(1)}, bf16[96,1024]{1,0:T(8,128)(2,1)}, u32[]{:S(2)}, u32[]{:S(2)}) collective-permute-start(bf16[96,1024]{1,0:T(8,128)(2,1)S(1)} %bitcast.159), channel_id=1, source_target_pairs={{0,8},{8,0},{1,9},{9,1},{2,10},{10,2},{3,11},{11,3},{4,12},{12,4},... | collective-permute-start | bytes 589832 | tf_op jit(solution)/shard_map/while/body/ppermute | solution.py:20
  40.0 13.5 %collective-permute-start.8 = (bf16[96,1024]{1,0:T(8,128)(2,1)S(1)}, bf16[96,1024]{1,0:T(8,128)(2,1)}, u32[]{:S(2)}, u32[]{:S(2)}) collective-permute-start(bf16[96,1024]{1,0:T(8,128)(2,1)S(1)} %bitcast.161), channel_id=1, source_target_pairs={{0,2},{2,4},{4,6},{6,0},{1,3},{3,5},{5,7},{7,1},{8,10},{10,12},{12... | collective-permute-start | bytes 589832 | tf_op jit(solution)/shard_map/while/body/ppermute | solution.py:20
  40.5 13.0 %collective-permute-start.7 = (bf16[96,1024]{1,0:T(8,128)(2,1)S(1)}, bf16[96,1024]{1,0:T(8,128)(2,1)}, u32[]{:S(2)}, u32[]{:S(2)}) collective-permute-start(bf16[96,1024]{1,0:T(8,128)(2,1)S(1)} %bitcast.162), channel_id=1, source_target_pairs={{0,4},{2,6},{4,0},{6,2},{1,5},{3,7},{5,1},{7,3},{8,12},{10,14},{12... | collective-permute-start | bytes 589832 | tf_op jit(solution)/shard_map/while/body/ppermute | solution.py:20
  42.9 10.6 %collective-permute-start.6 = (bf16[96,1024]{1,0:T(8,128)(2,1)S(1)}, bf16[96,1024]{1,0:T(8,128)(2,1)}, u32[]{:S(2)}, u32[]{:S(2)}) collective-permute-start(bf16[96,1024]{1,0:T(8,128)(2,1)S(1)} %bitcast.163), channel_id=1, source_target_pairs={{0,6},{2,0},{4,2},{6,4},{1,7},{3,1},{5,3},{7,5},{8,14},{10,8},{12,... | collective-permute-start | bytes 589832 | tf_op jit(solution)/shard_map/while/body/ppermute | solution.py:20
  48.2 27.8 %collective-permute-start.15 = (bf16[192,1024]{1,0:T(8,128)(2,1)}, bf16[192,1024]{1,0:T(8,128)(2,1)}, u32[]{:S(2)}, u32[]{:S(2)}) collective-permute-start(bf16[192,1024]{1,0:T(8,128)(2,1)} %body.75.refs_0_), channel_id=1, source_target_pairs={{0,2},{2,4},{4,6},{6,0},{1,3},{3,5},{5,7},{7,1},{8,10},{10,12},{12... | collective-permute-start | bytes 1179656 | tf_op jit(solution)/shard_map/while/body/ppermute | solution.py:20
  67.3 26.1 %collective-permute-start.9 = (bf16[3,128,1024]{2,1,0:T(8,128)(2,1)}, bf16[3,128,1024]{2,1,0:T(8,128)(2,1)}, u32[]{:S(2)}, u32[]{:S(2)}) collective-permute-start(bf16[3,128,1024]{2,1,0:T(8,128)(2,1)} %get-tuple-element.777), channel_id=1, source_target_pairs={{0,32},{32,64},{64,96},{96,0},{1,33},{33,65},{65,97},{97,1},{2,34}... | collective-permute-start | bytes 2359304 | tf_op jit(solution)/shard_map/while/body/ppermute | solution.py:20
  68.9 24.5 %collective-permute-start.11 = (bf16[3,128,1024]{2,1,0:T(8,128)(2,1)}, bf16[3,128,1024]{2,1,0:T(8,128)(2,1)}, u32[]{:S(2)}, u32[]{:S(2)}) collective-permute-start(bf16[3,128,1024]{2,1,0:T(8,128)(2,1)} %get-tuple-element.779), channel_id=1, source_target_pairs={{0,96},{32,0},{64,32},{96,64},{1,97},{33,1},{65,33},{97,65},{2,98}... | collective-permute-start | bytes 2359304 | tf_op jit(solution)/shard_map/while/body/ppermute | solution.py:20
  70.6 26.8 %collective-permute-start.12 = (bf16[384,1024]{1,0:T(8,128)(2,1)}, bf16[384,1024]{1,0:T(8,128)(2,1)}, u32[]{:S(2)}, u32[]{:S(2)}) collective-permute-start(bf16[384,1024]{1,0:T(8,128)(2,1)} %body.77.refs_0_), channel_id=1, source_target_pairs={{0,8},{8,0},{1,9},{9,1},{2,10},{10,2},{3,11},{11,3},{4,12},{12,4},... | collective-permute-start | bytes 2359304 | tf_op jit(solution)/shard_map/while/body/ppermute | solution.py:20
  73.6 11.3 %collective-permute-start.14 = (bf16[192,1024]{1,0:T(8,128)(2,1)S(1)}, bf16[192,1024]{1,0:T(8,128)(2,1)S(1)}, u32[]{:S(2)}, u32[]{:S(2)}) collective-permute-start(bf16[192,1024]{1,0:T(8,128)(2,1)S(1)} %copy-done.9), channel_id=1, source_target_pairs={{0,4},{2,6},{4,0},{6,2},{1,5},{3,7},{5,1},{7,3},{8,12},{10,14},{12... | collective-permute-start | bytes 1179656 | tf_op jit(solution)/shard_map/while/body/ppermute | solution.py:20
  76.0 17.4 %collective-permute-start.13 = (bf16[192,1024]{1,0:T(8,128)(2,1)S(1)}, bf16[192,1024]{1,0:T(8,128)(2,1)S(1)}, u32[]{:S(2)}, u32[]{:S(2)}) collective-permute-start(bf16[192,1024]{1,0:T(8,128)(2,1)S(1)} %copy-done.9), channel_id=1, source_target_pairs={{0,6},{2,0},{4,2},{6,4},{1,7},{3,1},{5,3},{7,5},{8,14},{10,8},{12,... | collective-permute-start | bytes 1179656 | tf_op jit(solution)/shard_map/while/body/ppermute | solution.py:20
  105.1 21.7 %collective-permute-start.10 = (bf16[3,128,1024]{2,1,0:T(8,128)(2,1)}, bf16[3,128,1024]{2,1,0:T(8,128)(2,1)}, u32[]{:S(2)}, u32[]{:S(2)}) collective-permute-start(bf16[3,128,1024]{2,1,0:T(8,128)(2,1)} %get-tuple-element.778), channel_id=1, source_target_pairs={{0,64},{32,96},{64,0},{96,32},{1,65},{33,97},{65,1},{97,33},{2,66}... | collective-permute-start | bytes 2359304 | tf_op jit(solution)/shard_map/while/body/ppermute | solution.py:20
  120.1 46.0 %collective-permute-start.22 = (bf16[3,256,1024]{2,1,0:T(8,128)(2,1)}, bf16[3,256,1024]{2,1,0:T(8,128)(2,1)}, u32[]{:S(2)}, u32[]{:S(2)}) collective-permute-start(bf16[3,256,1024]{2,1,0:T(8,128)(2,1)} %get-tuple-element.797), channel_id=1, source_target_pairs={{0,16},{16,0},{1,17},{17,1},{2,18},{18,2},{3,19},{19,3},{4,20},{20... | collective-permute-start | bytes 4718600 | tf_op jit(solution)/shard_map/while/body/ppermute | solution.py:20
  130.1 35.0 %collective-permute-start.18 = (bf16[3,64,1024]{2,1,0:T(8,128)(2,1)}, bf16[3,64,1024]{2,1,0:T(8,128)(2,1)}, u32[]{:S(2)}, u32[]{:S(2)}) collective-permute-start(bf16[3,64,1024]{2,1,0:T(8,128)(2,1)} %slice.533), channel_id=1, source_target_pairs={{0,16},{16,0},{1,17},{17,1},{2,18},{18,2},{3,19},{19,3},{4,20},{20... | collective-permute-start | bytes 1179656 | tf_op jit(solution)/shard_map/while/body/ppermute | solution.py:20
  146.8 36.8 %collective-permute-start.19 = (bf16[3,128,1024]{2,1,0:T(8,128)(2,1)}, bf16[3,128,1024]{2,1,0:T(8,128)(2,1)S(1)}, u32[]{:S(2)}, u32[]{:S(2)}) collective-permute-start(bf16[3,128,1024]{2,1,0:T(8,128)(2,1)} %get-tuple-element.793), channel_id=1, source_target_pairs={{0,32},{32,64},{64,96},{96,0},{1,33},{33,65},{65,97},{97,1},{2,34}... | collective-permute-start | bytes 2359304 | tf_op jit(solution)/shard_map/while/body/ppermute | solution.py:20
  147.1 36.5 %collective-permute-start.20 = (bf16[3,128,1024]{2,1,0:T(8,128)(2,1)}, bf16[3,128,1024]{2,1,0:T(8,128)(2,1)S(1)}, u32[]{:S(2)}, u32[]{:S(2)}) collective-permute-start(bf16[3,128,1024]{2,1,0:T(8,128)(2,1)} %get-tuple-element.794), channel_id=1, source_target_pairs={{0,64},{32,96},{64,0},{96,32},{1,65},{33,97},{65,1},{97,33},{2,66}... | collective-permute-start | bytes 2359304 | tf_op jit(solution)/shard_map/while/body/ppermute | solution.py:20
  150.0 34.2 %collective-permute-start.21 = (bf16[3,128,1024]{2,1,0:T(8,128)(2,1)}, bf16[3,128,1024]{2,1,0:T(8,128)(2,1)S(1)}, u32[]{:S(2)}, u32[]{:S(2)}) collective-permute-start(bf16[3,128,1024]{2,1,0:T(8,128)(2,1)} %get-tuple-element.795), channel_id=1, source_target_pairs={{0,96},{32,0},{64,32},{96,64},{1,97},{33,1},{65,33},{97,65},{2,98}... | collective-permute-start | bytes 2359304 | tf_op jit(solution)/shard_map/while/body/ppermute | solution.py:20
  184.9 12.0 %collective-permute-start.24 = (bf16[3,64,1024]{2,1,0:T(8,128)(2,1)S(1)}, bf16[3,64,1024]{2,1,0:T(8,128)(2,1)S(1)}, u32[]{:S(2)}, u32[]{:S(2)}) collective-permute-start(bf16[3,64,1024]{2,1,0:T(8,128)(2,1)S(1)} %get-tuple-element.811), channel_id=1, source_target_pairs={{0,32},{32,64},{64,96},{96,0},{1,33},{33,65},{65,97},{97,1},{2,34}... | collective-permute-start | bytes 1179656 | tf_op jit(solution)/shard_map/while/body/ppermute | solution.py:20
  186.2 20.3 %collective-permute-start.25 = (bf16[3,64,1024]{2,1,0:T(8,128)(2,1)S(1)}, bf16[3,64,1024]{2,1,0:T(8,128)(2,1)S(1)}, u32[]{:S(2)}, u32[]{:S(2)}) collective-permute-start(bf16[3,64,1024]{2,1,0:T(8,128)(2,1)S(1)} %get-tuple-element.812), channel_id=1, source_target_pairs={{0,64},{32,96},{64,0},{96,32},{1,65},{33,97},{65,1},{97,33},{2,66}... | collective-permute-start | bytes 1179656 | tf_op jit(solution)/shard_map/while/body/ppermute | solution.py:20
  189.1 17.4 %collective-permute-start.26 = (bf16[3,64,1024]{2,1,0:T(8,128)(2,1)S(1)}, bf16[3,64,1024]{2,1,0:T(8,128)(2,1)S(1)}, u32[]{:S(2)}, u32[]{:S(2)}) collective-permute-start(bf16[3,64,1024]{2,1,0:T(8,128)(2,1)S(1)} %get-tuple-element.813), channel_id=1, source_target_pairs={{0,96},{32,0},{64,32},{96,64},{1,97},{33,1},{65,33},{97,65},{2,98}... | collective-permute-start | bytes 1179656 | tf_op jit(solution)/shard_map/while/body/ppermute | solution.py:20
  190.5 21.1 %collective-permute-start.23 = (bf16[2,64,1024]{2,1,0:T(8,128)(2,1)S(1)}, bf16[2,64,1024]{2,1,0:T(8,128)(2,1)}, u32[]{:S(2)}, u32[]{:S(2)}) collective-permute-start(bf16[2,64,1024]{2,1,0:T(8,128)(2,1)S(1)} %pad_maximum_fusion.10.refs_0_), channel_id=1, source_target_pairs={{0,16},{16,0},{1,17},{17,1},{2,18},{18,2},{3,19},{19,3},{4,20},{20... | collective-permute-start | bytes 786440 | tf_op jit(solution)/shard_map/while/body/ppermute | solution.py:20
  192.2 22.0 %collective-permute-start.33 = (bf16[3,64,1024]{2,1,0:T(8,128)(2,1)}, bf16[3,64,1024]{2,1,0:T(8,128)(2,1)}, u32[]{:S(2)}, u32[]{:S(2)}) collective-permute-start(bf16[3,64,1024]{2,1,0:T(8,128)(2,1)} %slice.536), channel_id=1, source_target_pairs={{0,16},{16,0},{1,17},{17,1},{2,18},{18,2},{3,19},{19,3},{4,20},{20... | collective-permute-start | bytes 1179656 | tf_op jit(solution)/shard_map/while/body/ppermute | solution.py:20
  207.6 25.9 %collective-permute-start.32 = (bf16[2,64,1024]{2,1,0:T(8,128)(2,1)}, bf16[2,64,1024]{2,1,0:T(8,128)(2,1)}, u32[]{:S(2)}, u32[]{:S(2)}) collective-permute-start(bf16[2,64,1024]{2,1,0:T(8,128)(2,1)} %pad_maximum_fusion.11.refs_0_), channel_id=1, source_target_pairs={{0,32},{32,64},{64,96},{96,0},{1,33},{33,65},{65,97},{97,1},{2,34}... | collective-permute-start | bytes 786440 | tf_op jit(solution)/shard_map/while/body/ppermute | solution.py:20
  208.3 25.9 %collective-permute-start.31 = (bf16[2,64,1024]{2,1,0:T(8,128)(2,1)}, bf16[2,64,1024]{2,1,0:T(8,128)(2,1)}, u32[]{:S(2)}, u32[]{:S(2)}) collective-permute-start(bf16[2,64,1024]{2,1,0:T(8,128)(2,1)} %pad_maximum_fusion.11.refs_0_), channel_id=1, source_target_pairs={{0,64},{32,96},{64,0},{96,32},{1,65},{33,97},{65,1},{97,33},{2,66}... | collective-permute-start | bytes 786440 | tf_op jit(solution)/shard_map/while/body/ppermute | solution.py:20
  211.2 25.5 %collective-permute-start.30 = (bf16[2,64,1024]{2,1,0:T(8,128)(2,1)}, bf16[2,64,1024]{2,1,0:T(8,128)(2,1)}, u32[]{:S(2)}, u32[]{:S(2)}) collective-permute-start(bf16[2,64,1024]{2,1,0:T(8,128)(2,1)} %pad_maximum_fusion.11.refs_0_), channel_id=1, source_target_pairs={{0,96},{32,0},{64,32},{96,64},{1,97},{33,1},{65,33},{97,65},{2,98}... | collective-permute-start | bytes 786440 | tf_op jit(solution)/shard_map/while/body/ppermute | solution.py:20
  216.3 12.1 %collective-permute-start.34 = (bf16[1,192,1024]{2,1,0:T(8,128)(2,1)S(1)}, bf16[1,192,1024]{2,1,0:T(8,128)(2,1)S(1)}, u32[]{:S(2)}, u32[]{:S(2)}) collective-permute-start(bf16[1,192,1024]{2,1,0:T(8,128)(2,1)S(1)} %maximum_bitcast_fusion.2.refs_0_), channel_id=1, source_target_pairs={{0,16},{16,0},{1,17},{17,1},{2,18},{18,2},{3,19},{19,3},{4,20},{20... | collective-permute-start | bytes 1179656 | tf_op jit(solution)/shard_map/while/body/ppermute | solution.py:20
  218.0 21.8 %collective-permute-start.36 = (bf16[2,64,1024]{2,1,0:T(8,128)(2,1)S(1)}, bf16[2,64,1024]{2,1,0:T(8,128)(2,1)S(1)}, u32[]{:S(2)}, u32[]{:S(2)}) collective-permute-start(bf16[2,64,1024]{2,1,0:T(8,128)(2,1)S(1)} %pad_maximum_fusion.12.refs_0_), channel_id=1, source_target_pairs={{0,16},{16,0},{1,17},{17,1},{2,18},{18,2},{3,19},{19,3},{4,20},{20... | collective-permute-start | bytes 786440 | tf_op jit(solution)/shard_map/while/body/ppermute | solution.py:20
  229.2 21.4 %collective-permute-start.29 = (bf16[2,128,1024]{2,1,0:T(8,128)(2,1)S(1)}, bf16[2,128,1024]{2,1,0:T(8,128)(2,1)}, u32[]{:S(2)}, u32[]{:S(2)}) collective-permute-start(bf16[2,128,1024]{2,1,0:T(8,128)(2,1)S(1)} %copy-done.6), channel_id=1, source_target_pairs={{0,32},{32,64},{64,96},{96,0},{1,33},{33,65},{65,97},{97,1},{2,34}... | collective-permute-start | bytes 1572872 | tf_op jit(solution)/shard_map/while/body/ppermute | solution.py:20
  233.5 22.1 %collective-permute-start.28 = (bf16[2,128,1024]{2,1,0:T(8,128)(2,1)S(1)}, bf16[2,128,1024]{2,1,0:T(8,128)(2,1)}, u32[]{:S(2)}, u32[]{:S(2)}) collective-permute-start(bf16[2,128,1024]{2,1,0:T(8,128)(2,1)S(1)} %copy-done.6), channel_id=1, source_target_pairs={{0,64},{32,96},{64,0},{96,32},{1,65},{33,97},{65,1},{97,33},{2,66}... | collective-permute-start | bytes 1572872 | tf_op jit(solution)/shard_map/while/body/ppermute | solution.py:20
  234.2 26.0 %collective-permute-start.27 = (bf16[2,128,1024]{2,1,0:T(8,128)(2,1)S(1)}, bf16[2,128,1024]{2,1,0:T(8,128)(2,1)}, u32[]{:S(2)}, u32[]{:S(2)}) collective-permute-start(bf16[2,128,1024]{2,1,0:T(8,128)(2,1)S(1)} %copy-done.6), channel_id=1, source_target_pairs={{0,96},{32,0},{64,32},{96,64},{1,97},{33,1},{65,33},{97,65},{2,98}... | collective-permute-start | bytes 1572872 | tf_op jit(solution)/shard_map/while/body/ppermute | solution.py:20
  243.1 29.9 %collective-permute-start.39 = (bf16[2,128,1024]{2,1,0:T(8,128)(2,1)}, bf16[2,128,1024]{2,1,0:T(8,128)(2,1)}, u32[]{:S(2)}, u32[]{:S(2)}) collective-permute-start(bf16[2,128,1024]{2,1,0:T(8,128)(2,1)} %body.86.refs_2_), channel_id=1, source_target_pairs={{0,32},{32,64},{64,96},{96,0},{1,33},{33,65},{65,97},{97,1},{2,34}... | collective-permute-start | bytes 1572872 | tf_op jit(solution)/shard_map/while/body/ppermute | solution.py:20
  243.2 35.0 %collective-permute-start.38 = (bf16[2,128,1024]{2,1,0:T(8,128)(2,1)}, bf16[2,128,1024]{2,1,0:T(8,128)(2,1)}, u32[]{:S(2)}, u32[]{:S(2)}) collective-permute-start(bf16[2,128,1024]{2,1,0:T(8,128)(2,1)} %body.86.refs_2_), channel_id=1, source_target_pairs={{0,64},{32,96},{64,0},{96,32},{1,65},{33,97},{65,1},{97,33},{2,66}... | collective-permute-start | bytes 1572872 | tf_op jit(solution)/shard_map/while/body/ppermute | solution.py:20
  250.5 32.2 %collective-permute-start.35 = (bf16[2,256,1024]{2,1,0:T(8,128)(2,1)}, bf16[2,256,1024]{2,1,0:T(8,128)(2,1)}, u32[]{:S(2)}, u32[]{:S(2)}) collective-permute-start(bf16[2,256,1024]{2,1,0:T(8,128)(2,1)} %body.85.refs_0_), channel_id=1, source_target_pairs={{0,16},{16,0},{1,17},{17,1},{2,18},{18,2},{3,19},{19,3},{4,20},{20... | collective-permute-start | bytes 3145736 | tf_op jit(solution)/shard_map/while/body/ppermute | solution.py:20
  255.7 27.1 %collective-permute-start.37 = (bf16[2,128,1024]{2,1,0:T(8,128)(2,1)}, bf16[2,128,1024]{2,1,0:T(8,128)(2,1)}, u32[]{:S(2)}, u32[]{:S(2)}) collective-permute-start(bf16[2,128,1024]{2,1,0:T(8,128)(2,1)} %body.86.refs_2_), channel_id=1, source_target_pairs={{0,96},{32,0},{64,32},{96,64},{1,97},{33,1},{65,33},{97,65},{2,98}... | collective-permute-start | bytes 1572872 | tf_op jit(solution)/shard_map/while/body/ppermute | solution.py:20
  260.2 47.7 %collective-permute-start.56 = (bf16[1,384,1024]{2,1,0:T(8,128)(2,1)}, bf16[1,384,1024]{2,1,0:T(8,128)(2,1)}, u32[]{:S(2)}, u32[]{:S(2)}) collective-permute-start(bf16[1,384,1024]{2,1,0:T(8,128)(2,1)} %body.84.refs_0_), channel_id=1, source_target_pairs={{0,32},{32,64},{64,96},{96,0},{1,33},{33,65},{65,97},{97,1},{2,34}... | collective-permute-start | bytes 2359304 | tf_op jit(solution)/shard_map/while/body/ppermute | solution.py:20
  273.0 35.0 %collective-permute-start.55 = (bf16[1,384,1024]{2,1,0:T(8,128)(2,1)}, bf16[1,384,1024]{2,1,0:T(8,128)(2,1)}, u32[]{:S(2)}, u32[]{:S(2)}) collective-permute-start(bf16[1,384,1024]{2,1,0:T(8,128)(2,1)} %body.84.refs_0_), channel_id=1, source_target_pairs={{0,64},{32,96},{64,0},{96,32},{1,65},{33,97},{65,1},{97,33},{2,66}... | collective-permute-start | bytes 2359304 | tf_op jit(solution)/shard_map/while/body/ppermute | solution.py:20
  278.2 33.2 %collective-permute-start.54 = (bf16[1,384,1024]{2,1,0:T(8,128)(2,1)}, bf16[1,384,1024]{2,1,0:T(8,128)(2,1)}, u32[]{:S(2)}, u32[]{:S(2)}) collective-permute-start(bf16[1,384,1024]{2,1,0:T(8,128)(2,1)} %body.84.refs_0_), channel_id=1, source_target_pairs={{0,96},{32,0},{64,32},{96,64},{1,97},{33,1},{65,33},{97,65},{2,98}... | collective-permute-start | bytes 2359304 | tf_op jit(solution)/shard_map/while/body/ppermute | solution.py:20
  295.9 33.7 %collective-permute-start.41 = (bf16[768,1024]{1,0:T(8,128)(2,1)}, bf16[768,1024]{1,0:T(8,128)(2,1)}, u32[]{:S(2)}, u32[]{:S(2)}) collective-permute-start(bf16[768,1024]{1,0:T(8,128)(2,1)} %get-tuple-element.850), channel_id=1, source_target_pairs={{0,1},{1,0},{2,3},{3,2},{4,5},{5,4},{6,7},{7,6},{8,9},{9,8},{10,11... | collective-permute-start | bytes 4718600 | tf_op jit(solution)/shard_map/while/body/ppermute | solution.py:20
  329.5 16.0 %collective-permute-start.40 = (bf16[256,1024]{1,0:T(8,128)(2,1)}, bf16[256,1024]{1,0:T(8,128)(2,1)S(1)}, u32[]{:S(2)}, u32[]{:S(2)}) collective-permute-start(bf16[256,1024]{1,0:T(8,128)(2,1)} %get-tuple-element.848), channel_id=1, source_target_pairs={{0,1},{1,0},{2,3},{3,2},{4,5},{5,4},{6,7},{7,6},{8,9},{9,8},{10,11... | collective-permute-start | bytes 1572872 | tf_op jit(solution)/shard_map/while/body/ppermute | solution.py:20
  334.7 15.4 %collective-permute-start.42 = (bf16[4,96,512]{2,1,0:T(8,128)(2,1)S(1)}, bf16[4,96,512]{2,1,0:T(8,128)(2,1)S(1)}, u32[]{:S(2)}, u32[]{:S(2)}) collective-permute-start(bf16[4,96,512]{2,1,0:T(8,128)(2,1)S(1)} %slice_bitcast_fusion.14), channel_id=1, source_target_pairs={{0,8},{8,0},{1,9},{9,1},{2,10},{10,2},{3,11},{11,3},{4,12},{12,4},... | collective-permute-start | bytes 1179656 | tf_op jit(solution)/shard_map/while/body/ppermute | solution.py:20
  336.8 8.8 %collective-permute-start.43 = (bf16[2,96,512]{2,1,0:T(8,128)(2,1)S(1)}, bf16[2,96,512]{2,1,0:T(8,128)(2,1)S(1)}, u32[]{:S(2)}, u32[]{:S(2)}) collective-permute-start(bf16[2,96,512]{2,1,0:T(8,128)(2,1)S(1)} %get-tuple-element.854), channel_id=1, source_target_pairs={{0,2},{2,4},{4,6},{6,0},{1,3},{3,5},{5,7},{7,1},{8,10},{10,12},{12... | collective-permute-start | bytes 589832 | tf_op jit(solution)/shard_map/while/body/ppermute | solution.py:20
  337.7 12.4 %collective-permute-start.44 = (bf16[2,96,512]{2,1,0:T(8,128)(2,1)S(1)}, bf16[2,96,512]{2,1,0:T(8,128)(2,1)S(1)}, u32[]{:S(2)}, u32[]{:S(2)}) collective-permute-start(bf16[2,96,512]{2,1,0:T(8,128)(2,1)S(1)} %get-tuple-element.855), channel_id=1, source_target_pairs={{0,4},{2,6},{4,0},{6,2},{1,5},{3,7},{5,1},{7,3},{8,12},{10,14},{12... | collective-permute-start | bytes 589832 | tf_op jit(solution)/shard_map/while/body/ppermute | solution.py:20
  340.9 9.2 %collective-permute-start.45 = (bf16[2,96,512]{2,1,0:T(8,128)(2,1)S(1)}, bf16[2,96,512]{2,1,0:T(8,128)(2,1)S(1)}, u32[]{:S(2)}, u32[]{:S(2)}) collective-permute-start(bf16[2,96,512]{2,1,0:T(8,128)(2,1)S(1)} %get-tuple-element.856), channel_id=1, source_target_pairs={{0,6},{2,0},{4,2},{6,4},{1,7},{3,1},{5,3},{7,5},{8,14},{10,8},{12,... | collective-permute-start | bytes 589832 | tf_op jit(solution)/shard_map/while/body/ppermute | solution.py:20
  350.3 12.5 %collective-permute-start.46 = (bf16[128,1024]{1,0:T(8,128)(2,1)S(1)}, bf16[128,1024]{1,0:T(8,128)(2,1)S(1)}, u32[]{:S(2)}, u32[]{:S(2)}) collective-permute-start(bf16[128,1024]{1,0:T(8,128)(2,1)S(1)} %slice.537), channel_id=1, source_target_pairs={{0,8},{8,0},{1,9},{9,1},{2,10},{10,2},{3,11},{11,3},{4,12},{12,4},... | collective-permute-start | bytes 786440 | tf_op jit(solution)/shard_map/while/body/ppermute | solution.py:20
  352.2 9.4 %collective-permute-start.47 = (bf16[96,512]{1,0:T(8,128)(2,1)S(1)}, bf16[96,512]{1,0:T(8,128)(2,1)S(1)}, u32[]{:S(2)}, u32[]{:S(2)}) collective-permute-start(bf16[96,512]{1,0:T(8,128)(2,1)S(1)} %fusion.152), channel_id=1, source_target_pairs={{0,8},{8,0},{1,9},{9,1},{2,10},{10,2},{3,11},{11,3},{4,12},{12,4},... | collective-permute-start | bytes 294920 | tf_op jit(solution)/shard_map/while/body/ppermute | solution.py:20
  (66 other events, 624.2 us)

commit v2 on v0

--- a/solution.py
+++ b/solution.py
@@ -110,7 +110,7 @@
                 for k in range(4):
                     for d in (0, 1):
                         block = ((place_ref[0] + k) % 4) * 2 + (place_ref[1] + d) % 2
-                        feeds.append(start(ins[i].at[span(block * rows, rows)], bufs[3 + i].at[span((2 * k + d) * rows, rows)]))
+                        feeds.append(start(ins[i].at[span(block * rows, rows)], bufs[3 + i].at[span((2 * k + d if y_first else 4 * d + k) * rows, rows)]))
         loads = [start(w_refs[i], bufs[i]) for i in range(3)]
         if compact:
             pick = (lax.broadcasted_iota(jnp.int32, (total, rank.shape[1]), 0) == rank).astype(F32).astype(BF)
@@ -229,23 +229,25 @@
     def near_far(total, rows):
         return total[:, :rows], shift(total[:, rows:].astype(BF), "xl", 2, 1).astype(F32)
 
+    total0 = add(received0)
+    received0 = over_y([total0[:, :r0]] + [total0[:, k * r0 : (k + 1) * r0].astype(BF) for k in (1, 2, 3)], 1)
+    (rank,) = after(received0[1], rank)
     halves = (mine_x, other_x, mine_g, other_g)
     xa, ga, near_a, far_a = project(place, (rank[None, :], *halves), weights, r1, False)
     far_a = shift(far_a, "xl", 2, 1)
-    near0, far0 = near_far(add(after(xa, *received0)), r0)
-    (rank_b,) = after(near0, rank)
+    h0, s0 = swiglu_back(add(after(xa, *received0)))
+    all0 = over_y([s0] * 4, -1)
+    (rank_b,) = after(s0, rank)
     xb, gb, *parts_b = project(place, (rank_b[None, :] - 8 * r1, *halves), weights, r1, True)
     received_b = over_y(parts_b, 1)
-    total_a = add(after(xb, near_a, far_a))
+    all0 = pack_rows(place, after(xb, *all0))
+    pieces0 = [all0, shift(all0, "xl", 2, 1)]
+    total_a = add(after(all0, near_a, far_a))
     received_a = over_y([total_a[:, :r1]] + [total_a[:, k * r1 : (k + 1) * r1].astype(BF) for k in (1, 2, 3)], 1)
     near_b, far_b = near_far(add(after(received_a[0], *received_b)), r1)
-    near0, far0 = after(near_b, near0, far0)
-    h0, s0 = swiglu_back(near0 + far0)
-    swap_s0 = shift(s0, "xl", 2, 1)
-    ha, sa = swiglu_back(add(after(s0, *received_a)))
+    ha, sa = swiglu_back(add(after(near_b, *received_a)))
     all_a = over_y([sa] * 4, -1)
-    pair0 = pack_rows(place, after(sa, s0, swap_s0))
-    near_b, far_b = after(pair0, near_b, far_b)
+    near_b, far_b = after(sa, near_b, far_b)
     hb, sb = swiglu_back(near_b + far_b)
     swap_b = shift(sb, "xl", 2, 1)
     h_all = jnp.concatenate([h0, ha, hb], axis=0)[None]
@@ -255,12 +257,11 @@
     pieces_a = [all_a, shift(all_a, "xl", 2, 1)]
     pair_b = pack_rows(place, after(all_a, sb, swap_b))
     all_b = over_y([pair_b] * 4, -1)
-    pieces0 = over_y([pair0] * 4, -1)
     all_h = over_y([pair_h] * 4, -1)
 
     def jobs0(y, xl):
         return [
-            (i, span((((y + k) % 4) * 2 + (xl + d) % 2) * r0, r0), k, (i, span(d * r0, r0)))
+            (i, span((((y + k) % 4) * 2 + (xl + d) % 2) * r0, r0), d, (i, span(k * r0, r0)))
             for d in (0, 1) for k in range(4) for i in (0, 1)
         ]
 
@@ -268,7 +269,7 @@
         jobs = [(i, span(n * 4 * r1, 4 * r1), n, (i, span(0, 4 * r1))) for n in range(2) for i in (0, 1)]
         return jobs + [(i, span((8 + 2 * n) * r1, 2 * r1), 2 + n, (i, span(0, 2 * r1))) for n in range(4) for i in (0, 1)]
 
-    dgd, dud, *halves = unproject(place, after(pair_b, *pieces0[1:], *pieces_a, *all_b)[3:], jobs1, cap, weights[:2], rank[:, None])
+    dgd, dud, *halves = unproject(place, after(pair_b, pieces0[1], *pieces_a, *all_b)[1:], jobs1, cap, weights[:2], rank[:, None])
     swap1 = shift(halves[1], "c", 2, 1)
     dg0, du0, *halves0 = unproject(place, after(dgd, *pieces0), jobs0, 8 * r0, weights[:2], None)
     swap0 = shift(halves0[1], "c", 2, 1)
@@ -352,9 +353,9 @@
         )
         near_x = join(place, after(x0, *moved_x))
         far_x = shift(near_x, "xh", 2, 1)
-        parts0 = project(place, after(near_x, x0, g0), (w_gate, w_up, w_down), x0.shape[0] // 8, True)
-        received0 = over_y(parts0, 1)
-        mine_g = by_core(place, after(parts0[0], received0[1], received0[3], *moved_g)[2:], late_x.shape[0])
+        parts0 = project(place, after(near_x, x0, g0), (w_gate, w_up, w_down), x0.shape[0] // 8, False)
+        received0 = (parts0[0], shift(parts0[1], "xl", 2, 1))
+        mine_g = by_core(place, after(parts0[0], *moved_g), late_x.shape[0])
         mine_x = join(place, after(mine_g, near_x, far_x))
         halves = (mine_x, shift(mine_x, "c", 2, 1), mine_g, shift(mine_g, "c", 2, 1))
         order = lax.iota(jnp.int32, n_tiles)

time: 374 us -> 443 us (1.18)
  waiting for transfers between devices: 137 us -> 218 us
  starting transfers between devices: 76.7 us -> 71.1 us
    ppermute x57, waiting for transfers between devices: 137 us -> 218 us  [shift(): lax.ppermute(value, axis, [(i, (i + step) % size) for i in range(size)])]
    ppermute x57, starting transfers between devices: 76.7 us -> 71.1 us  [shift(): lax.ppermute(value, axis, [(i, (i + step) % size) for i in range(size)])]
  transfers between devices with their start and end apart: 57 -> 57, of which waited for: 23 -> 28; matrix products, arithmetic and copies ran while one was open for 13% -> 10% of each run, Pallas kernels for 19% -> 11%
where the time goes in v2:
time: 443 us; the launch traced here: 440 us
  waiting for transfers between devices  218 us (49%)
  Pallas kernels  88.1 us (20%)
  starting transfers between devices  71.1 us (16%)
  other arithmetic  26.5 us (6%)
  local copies, waits for them, and re-layouts  18.2 us (4%)
  matrix products  14 us (3%)
    ppermute x57, waiting for transfers between devices, shift(): lax.ppermute(value, axis, [(i, (i + step) % size) for i in range(size)])  218 us
    ppermute x57, starting transfers between devices, shift(): lax.ppermute(value, axis, [(i, (i + step) % size) for i in range(size)])  71.1 us
    pallas_call x12, Pallas kernels, move(): pl.pallas_call(kernel, out_shape=[jax.ShapeDtypeStruct(s, BF) for s in sh...  35.2 us
    pallas_call x3, Pallas kernels, project(): pl.pallas_call(kernel, out_shape=[jax.ShapeDtypeStruct(s, BF) for s in sh...  33.6 us
    pallas_call x2, Pallas kernels, unproject(): pl.pallas_call(kernel, out_shape=[jax.ShapeDtypeStruct(s, BF) for s in sh...  19.3 us
    dot_general x6, matrix products, dot(): lax.dot_general(left, right, ((dims[:1], dims[1:]), ((), ())), preferred_...  14 us
  transfers between devices with their start and end apart: 57, of which 28 were waited for; matrix products, arithmetic and copies ran while one was open for 10% of the time, Pallas kernels for 11%

profile of v2, /device:TPU:0, one launch (start us, length us, event | category | flops | bytes accessed | tf_op | source)
XLA Modules:
  0.0 439.8 jit_solution(16296906281343961107)
XLA Ops:
  4.4 433.6 %while.21 = (s32[]{:T(128)}, bf16[32,1024]{1,0:T(8,128)(2,1)}, bf16[96,1024]{1,0:T(8,128)(2,1)}, bf16[960,1024]{1,0:T(8,128)(2,1)}, bf16[960,1024]{1,0:T(8,128)(...) while((s32[]{:T(128)}, bf16[32,1024]{1,0:T(8,128)(2,1)}, ...), condition=%wide.region_4.5_spmd, body=%wide.region_1.4_spmd.sunk | while | flops 9106092032 | bytes 408905504 | solution.py:378
  4.7 3.2 collective-permute-start
  7.9 3.5 collective-permute-done.refs_1_
  14.3 4.3 collective-permute-start.1
  19.8 9.4 %collective-permute-done.1.refs_1_ = bf16[128,1024]{1,0:T(8,128)(2,1)S(1)} collective-permute-done((bf16[128,1024]{1,0:T(8,128)(2,1)}, bf16[128,1024]{1,0:T(8,128)(2,1)S(1)}, u32[]{:S(2)}, u32[]{:S(2)}) %collective-permute-start.1) | collective-permute-done | bytes 262176 | tf_op jit(solution)/shard_map/while/body/ppermute | solution.py:20
  29.5 3.0 collective-permute-done.3.refs_3_
  33.2 2.9 body.74.refs_0_
  36.3 3.1 collective-permute-start.5
  41.4 3.8 collective-permute-done.5.refs_1_
  48.6 3.7 body.76
  53.0 2.7 body.77.refs_0_
  55.7 7.3 %body.78 = (bf16[3,256,1024]{2,1,0:T(8,128)(2,1)}, bf16[3,256,1024]{2,1,0:T(8,128)(2,1)}) custom-call(s32[2]{0:T(128)S(1)} %get-tuple-element.949.place_ref, bf16[512,1024]{1,0:T(8,128)(2,1)} %get-tuple-element.778.refs_0_, bf16[512,1024]{1,0:T(8,128)(2,1)} %get-tuple-element.779.refs_1_, bf16[960,1024]{1,0:T(8,128)(2,1)S(1)} %copy-done, ...), custom_call_target="tpu_custom_call" | custom-call | tf_op jit(solution)/shard_map/while/body/pallas_call | solution.py:141
  64.0 2.7 collective-permute-start.13
  68.9 9.8 %collective-permute-done.14.refs_1_ = bf16[192,1024]{1,0:T(8,128)(2,1)S(1)} collective-permute-done((bf16[192,1024]{1,0:T(8,128)(2,1)S(1)}, bf16[192,1024]{1,0:T(8,128)(2,1)S(1)}, u32[]{:S(2)}, u32[]{:S(2)}) %collective-permute-start.14) | collective-permute-done | bytes 393248 | tf_op jit(solution)/shard_map/while/body/ppermute | solution.py:20
  78.8 2.6 collective-permute-done.15.refs_2_
  81.3 6.3 %collective-permute-done.16.refs_3_ = bf16[192,1024]{1,0:T(8,128)(2,1)S(1)} collective-permute-done((bf16[192,1024]{1,0:T(8,128)(2,1)S(1)}, bf16[192,1024]{1,0:T(8,128)(2,1)S(1)}, u32[]{:S(2)}, u32[]{:S(2)}) %collective-permute-start.16) | collective-permute-done | bytes 393248 | tf_op jit(solution)/shard_map/while/body/ppermute | solution.py:20
  88.3 3.3 body.79.refs_3_
  91.7 26.1 %collective-permute-done.13.refs_1_ = bf16[384,1024]{1,0:T(8,128)(2,1)} collective-permute-done((bf16[384,1024]{1,0:T(8,128)(2,1)}, bf16[384,1024]{1,0:T(8,128)(2,1)}, u32[]{:S(2)}, u32[]{:S(2)}) %collective-permute-start.13) | collective-permute-done | bytes 786464 | tf_op jit(solution)/shard_map/while/body/ppermute | solution.py:20
  117.8 3.1 body.80.refs_1_
  123.2 4.3 fusion.126
  131.4 10.6 %collective-permute-done.10 = bf16[3,64,1024]{2,1,0:T(8,128)(2,1)} collective-permute-done((bf16[3,64,1024]{2,1,0:T(8,128)(2,1)}, bf16[3,64,1024]{2,1,0:T(8,128)(2,1)}, u32[]{:S(2)}, u32[]{:S(2)}) %collective-permute-start.10) | collective-permute-done | bytes 393248 | tf_op jit(solution)/shard_map/while/body/ppermute | solution.py:20
  143.8 11.4 %body.81 = (bf16[512,1024]{1,0:T(8,128)(2,1)}, bf16[512,1024]{1,0:T(8,128)(2,1)}, bf16[3,256,1024]{2,1,0:T(8,128)(2,1)}, bf16[3,256,1024]{2,1,0:T(8,128)(2,1)}) custom-call(s32[2]{0:T(128)S(1)} %get-tuple-element.949.place_ref, s32[1,1536]{1,0:T(1,128)} %broadcast_in_dim.131.refs_0_, bf16[768,1024]{1,0:T(8,128)(2,1)} %body.80.refs_1_, ...), custom_call_target="tpu_custom_call" | custom-call | tf_op jit(solution)/shard_map/while/body/pallas_call | solution.py:141
  159.6 8.2 %collective-permute-done.11 = bf16[3,64,1024]{2,1,0:T(8,128)(2,1)S(1)} collective-permute-done((bf16[3,64,1024]{2,1,0:T(8,128)(2,1)}, bf16[3,64,1024]{2,1,0:T(8,128)(2,1)S(1)}, u32[]{:S(2)}, u32[]{:S(2)}) %collective-permute-start.11) | collective-permute-done | bytes 393248 | tf_op jit(solution)/shard_map/while/body/ppermute | solution.py:20
  167.9 7.5 %collective-permute-done.12 = bf16[3,64,1024]{2,1,0:T(8,128)(2,1)S(1)} collective-permute-done((bf16[3,64,1024]{2,1,0:T(8,128)(2,1)}, bf16[3,64,1024]{2,1,0:T(8,128)(2,1)S(1)}, u32[]{:S(2)}, u32[]{:S(2)}) %collective-permute-start.12) | collective-permute-done | bytes 393248 | tf_op jit(solution)/shard_map/while/body/ppermute | solution.py:20
  176.7 2.7 collective-permute-start.19
  181.5 14.9 %body.82 = (bf16[512,1024]{1,0:T(8,128)(2,1)}, bf16[512,1024]{1,0:T(8,128)(2,1)}, bf16[3,128,1024]{2,1,0:T(8,128)(2,1)}, bf16[3,128,1024]{2,1,0:T(8,128)(2,1)}, ...) custom-call(s32[2]{0:T(128)S(1)} %get-tuple-element.949.place_ref, s32[1,1536]{1,0:T(1,128)} %sub.162.refs_0_, ...), custom_call_target="tpu_custom_call" | custom-call | tf_op jit(solution)/shard_map/while/body/pallas_call | solution.py:141
  196.5 2.6 collective-permute-start.27
  201.9 2.9 body.83.refs_0_
  204.8 2.7 fusion.132
  210.4 23.9 %collective-permute-done.27 = bf16[3,128,1024]{2,1,0:T(8,128)(2,1)} collective-permute-done((bf16[3,128,1024]{2,1,0:T(8,128)(2,1)}, bf16[3,128,1024]{2,1,0:T(8,128)(2,1)}, u32[]{:S(2)}, u32[]{:S(2)}) %collective-permute-start.27) | collective-permute-done | bytes 786464 | tf_op jit(solution)/shard_map/while/body/ppermute | solution.py:20
  242.9 8.7 %collective-permute-done.25 = bf16[3,64,1024]{2,1,0:T(8,128)(2,1)S(1)} collective-permute-done((bf16[3,64,1024]{2,1,0:T(8,128)(2,1)S(1)}, bf16[3,64,1024]{2,1,0:T(8,128)(2,1)S(1)}, u32[]{:S(2)}, u32[]{:S(2)}) %collective-permute-start.25) | collective-permute-done | bytes 393248 | tf_op jit(solution)/shard_map/while/body/ppermute | solution.py:20
  260.7 5.0 %collective-permute-done.34.refs_1_ = bf16[1,192,1024]{2,1,0:T(8,128)(2,1)} collective-permute-done((bf16[1,192,1024]{2,1,0:T(8,128)(2,1)S(1)}, bf16[1,192,1024]{2,1,0:T(8,128)(2,1)}, u32[]{:S(2)}, u32[]{:S(2)}) %collective-permute-start.34) | collective-permute-done | bytes 393248 | tf_op jit(solution)/shard_map/while/body/ppermute | solution.py:20
  269.6 3.7 collective-permute-done.32.refs_3_
  273.3 2.9 body.85.refs_0_
  278.3 35.3 %collective-permute-done.36.refs_1_ = bf16[2,64,1024]{2,1,0:T(8,128)(2,1)S(1)} collective-permute-done((bf16[2,64,1024]{2,1,0:T(8,128)(2,1)S(1)}, bf16[2,64,1024]{2,1,0:T(8,128)(2,1)S(1)}, u32[]{:S(2)}, u32[]{:S(2)}) %collective-permute-start.36) | collective-permute-done | bytes 262176 | tf_op jit(solution)/shard_map/while/body/ppermute | solution.py:20
  316.8 3.8 collective-permute-start.37
  322.7 19.8 %collective-permute-done.37.refs_3_ = bf16[2,128,1024]{2,1,0:T(8,128)(2,1)S(1)} collective-permute-done((bf16[2,128,1024]{2,1,0:T(8,128)(2,1)}, bf16[2,128,1024]{2,1,0:T(8,128)(2,1)S(1)}, u32[]{:S(2)}, u32[]{:S(2)}) %collective-permute-start.37) | collective-permute-done | bytes 524320 | tf_op jit(solution)/shard_map/while/body/ppermute | solution.py:20
  342.5 3.6 collective-permute-done.39.refs_5_
  346.2 13.1 %body.87 = (bf16[1024,1024]{1,0:T(8,128)(2,1)}, bf16[1024,1024]{1,0:T(8,128)(2,1)}, bf16[768,1024]{1,0:T(8,128)(2,1)}, bf16[768,1024]{1,0:T(8,128)(2,1)}) custom-call(s32[2]{0:T(128)S(1)} %get-tuple-element.949.place_ref, bf16[2,256,1024]{2,1,0:T(8,128)(2,1)} %body.85.refs_0_, bf16[2,256,1024]{2,1,0:T(8,128)(2,1)} %collective-permute-done.35.refs_1_, ...), custom_call_target="tpu_custom_call" | custom-call | tf_op jit(solution)/shard_map/while/body/pallas_call | solution.py:186
  359.4 3.0 pad_maximum_fusion.13
  364.7 6.2 %body.88 = (bf16[512,1024]{1,0:T(8,128)(2,1)}, bf16[512,1024]{1,0:T(8,128)(2,1)}, bf16[256,1024]{1,0:T(8,128)(2,1)}, bf16[256,1024]{1,0:T(8,128)(2,1)}) custom-call(s32[2]{0:T(128)S(1)} %get-tuple-element.949.place_ref, bf16[2,256,1024]{2,1,0:T(8,128)(2,1)} %body.83.refs_0_, bf16[2,256,1024]{2,1,0:T(8,128)(2,1)} %collective-permute-done.22.refs_1_, ...), custom_call_target="tpu_custom_call" | custom-call | tf_op jit(solution)/shard_map/while/body/pallas_call | solution.py:186
  372.1 2.7 convert_add_fusion.9
  390.0 11.5 %collective-permute-done.56.refs_3_ = bf16[1,384,1024]{2,1,0:T(8,128)(2,1)} collective-permute-done((bf16[1,384,1024]{2,1,0:T(8,128)(2,1)}, bf16[1,384,1024]{2,1,0:T(8,128)(2,1)}, u32[]{:S(2)}, u32[]{:S(2)}) %collective-permute-start.56) | collective-permute-done | bytes 786464 | tf_op jit(solution)/shard_map/while/body/ppermute | solution.py:20
  403.0 4.3 body.89
  407.3 2.8 fusion.147
  420.5 3.0 add_convert_fusion.8
  423.7 4.3 collective-permute-done.46
  432.4 2.9 collective-permute-done.52
  (252 shorter events, 107.1 us)
Async XLA Ops:
  14.3 15.0 %collective-permute-start.1 = (bf16[128,1024]{1,0:T(8,128)(2,1)}, bf16[128,1024]{1,0:T(8,128)(2,1)S(1)}, u32[]{:S(2)}, u32[]{:S(2)}) collective-permute-start(bf16[128,1024]{1,0:T(8,128)(2,1)} %body.73.refs_0_), channel_id=1, source_target_pairs={{0,6},{2,0},{4,2},{6,4},{1,7},{3,1},{5,3},{7,5},{8,14},{10,8},{12,... | collective-permute-start | bytes 786440 | tf_op jit(solution)/shard_map/while/body/ppermute | solution.py:20
  18.6 11.0 %collective-permute-start.2 = (bf16[128,1024]{1,0:T(8,128)(2,1)}, bf16[128,1024]{1,0:T(8,128)(2,1)S(1)}, u32[]{:S(2)}, u32[]{:S(2)}) collective-permute-start(bf16[128,1024]{1,0:T(8,128)(2,1)} %body.73.refs_0_), channel_id=1, source_target_pairs={{0,4},{2,6},{4,0},{6,2},{1,5},{3,7},{5,1},{7,3},{8,12},{10,14},{12... | collective-permute-start | bytes 786440 | tf_op jit(solution)/shard_map/while/body/ppermute | solution.py:20
  18.6 13.9 %collective-permute-start.3 = (bf16[128,1024]{1,0:T(8,128)(2,1)}, bf16[128,1024]{1,0:T(8,128)(2,1)S(1)}, u32[]{:S(2)}, u32[]{:S(2)}) collective-permute-start(bf16[128,1024]{1,0:T(8,128)(2,1)} %body.73.refs_0_), channel_id=1, source_target_pairs={{0,2},{2,4},{4,6},{6,0},{1,3},{3,5},{5,7},{7,1},{8,10},{10,12},{12... | collective-permute-start | bytes 786440 | tf_op jit(solution)/shard_map/while/body/ppermute | solution.py:20
  36.1 11.5 %collective-permute-start.4 = (bf16[512,1024]{1,0:T(8,128)(2,1)}, bf16[512,1024]{1,0:T(8,128)(2,1)S(1)}, u32[]{:S(2)}, u32[]{:S(2)}) collective-permute-start(bf16[512,1024]{1,0:T(8,128)(2,1)} %body.74.refs_0_), channel_id=1, source_target_pairs={{0,1},{1,0},{2,3},{3,2},{4,5},{5,4},{6,7},{7,6},{8,9},{9,8},{10,11... | collective-permute-start | bytes 3145736 | tf_op jit(solution)/shard_map/while/body/ppermute | solution.py:20
  39.4 12.9 %collective-permute-start.6 = (bf16[96,1024]{1,0:T(8,128)(2,1)S(1)}, bf16[96,1024]{1,0:T(8,128)(2,1)}, u32[]{:S(2)}, u32[]{:S(2)}) collective-permute-start(bf16[96,1024]{1,0:T(8,128)(2,1)S(1)} %bitcast.161), channel_id=1, source_target_pairs={{0,6},{2,0},{4,2},{6,4},{1,7},{3,1},{5,3},{7,5},{8,14},{10,8},{12,... | collective-permute-start | bytes 589832 | tf_op jit(solution)/shard_map/while/body/ppermute | solution.py:20
  40.5 11.9 %collective-permute-start.7 = (bf16[96,1024]{1,0:T(8,128)(2,1)S(1)}, bf16[96,1024]{1,0:T(8,128)(2,1)}, u32[]{:S(2)}, u32[]{:S(2)}) collective-permute-start(bf16[96,1024]{1,0:T(8,128)(2,1)S(1)} %bitcast.162), channel_id=1, source_target_pairs={{0,4},{2,6},{4,0},{6,2},{1,5},{3,7},{5,1},{7,3},{8,12},{10,14},{12... | collective-permute-start | bytes 589832 | tf_op jit(solution)/shard_map/while/body/ppermute | solution.py:20
  40.6 12.4 %collective-permute-start.8 = (bf16[96,1024]{1,0:T(8,128)(2,1)S(1)}, bf16[96,1024]{1,0:T(8,128)(2,1)}, u32[]{:S(2)}, u32[]{:S(2)}) collective-permute-start(bf16[96,1024]{1,0:T(8,128)(2,1)S(1)} %bitcast.163), channel_id=1, source_target_pairs={{0,2},{2,4},{4,6},{6,0},{1,3},{3,5},{5,7},{7,1},{8,10},{10,12},{12... | collective-permute-start | bytes 589832 | tf_op jit(solution)/shard_map/while/body/ppermute | solution.py:20
  63.1 60.2 %collective-permute-start.9 = (bf16[3,256,1024]{2,1,0:T(8,128)(2,1)}, bf16[3,256,1024]{2,1,0:T(8,128)(2,1)}, u32[]{:S(2)}, u32[]{:S(2)}) collective-permute-start(bf16[3,256,1024]{2,1,0:T(8,128)(2,1)} %get-tuple-element.781), channel_id=1, source_target_pairs={{0,16},{16,0},{1,17},{17,1},{2,18},{18,2},{3,19},{19,3},{4,20},{20... | collective-permute-start | bytes 4718600 | tf_op jit(solution)/shard_map/while/body/ppermute | solution.py:20
  64.0 53.9 %collective-permute-start.13 = (bf16[384,1024]{1,0:T(8,128)(2,1)}, bf16[384,1024]{1,0:T(8,128)(2,1)}, u32[]{:S(2)}, u32[]{:S(2)}) collective-permute-start(bf16[384,1024]{1,0:T(8,128)(2,1)} %body.77.refs_0_), channel_id=1, source_target_pairs={{0,8},{8,0},{1,9},{9,1},{2,10},{10,2},{3,11},{11,3},{4,12},{12,4},... | collective-permute-start | bytes 2359304 | tf_op jit(solution)/shard_map/while/body/ppermute | solution.py:20
  66.7 12.1 %collective-permute-start.14 = (bf16[192,1024]{1,0:T(8,128)(2,1)S(1)}, bf16[192,1024]{1,0:T(8,128)(2,1)S(1)}, u32[]{:S(2)}, u32[]{:S(2)}) collective-permute-start(bf16[192,1024]{1,0:T(8,128)(2,1)S(1)} %copy-done.7), channel_id=1, source_target_pairs={{0,6},{2,0},{4,2},{6,4},{1,7},{3,1},{5,3},{7,5},{8,14},{10,8},{12,... | collective-permute-start | bytes 1179656 | tf_op jit(solution)/shard_map/while/body/ppermute | solution.py:20
  67.8 13.6 %collective-permute-start.15 = (bf16[192,1024]{1,0:T(8,128)(2,1)S(1)}, bf16[192,1024]{1,0:T(8,128)(2,1)S(1)}, u32[]{:S(2)}, u32[]{:S(2)}) collective-permute-start(bf16[192,1024]{1,0:T(8,128)(2,1)S(1)} %copy-done.7), channel_id=1, source_target_pairs={{0,4},{2,6},{4,0},{6,2},{1,5},{3,7},{5,1},{7,3},{8,12},{10,14},{12... | collective-permute-start | bytes 1179656 | tf_op jit(solution)/shard_map/while/body/ppermute | solution.py:20
  67.9 19.7 %collective-permute-start.16 = (bf16[192,1024]{1,0:T(8,128)(2,1)S(1)}, bf16[192,1024]{1,0:T(8,128)(2,1)S(1)}, u32[]{:S(2)}, u32[]{:S(2)}) collective-permute-start(bf16[192,1024]{1,0:T(8,128)(2,1)S(1)} %copy-done.7), channel_id=1, source_target_pairs={{0,2},{2,4},{4,6},{6,0},{1,3},{3,5},{5,7},{7,1},{8,10},{10,12},{12... | collective-permute-start | bytes 1179656 | tf_op jit(solution)/shard_map/while/body/ppermute | solution.py:20
  91.6 51.0 %collective-permute-start.18 = (bf16[768,1024]{1,0:T(8,128)(2,1)}, bf16[768,1024]{1,0:T(8,128)(2,1)S(1)}, u32[]{:S(2)}, u32[]{:S(2)}) collective-permute-start(bf16[768,1024]{1,0:T(8,128)(2,1)} %body.79.refs_3_), channel_id=1, source_target_pairs={{0,1},{1,0},{2,3},{3,2},{4,5},{5,4},{6,7},{7,6},{8,9},{9,8},{10,11... | collective-permute-start | bytes 4718600 | tf_op jit(solution)/shard_map/while/body/ppermute | solution.py:20
  120.9 21.7 %collective-permute-start.17 = (bf16[768,1024]{1,0:T(8,128)(2,1)}, bf16[768,1024]{1,0:T(8,128)(2,1)}, u32[]{:S(2)}, u32[]{:S(2)}) collective-permute-start(bf16[768,1024]{1,0:T(8,128)(2,1)} %body.80.refs_1_), channel_id=1, source_target_pairs={{0,1},{1,0},{2,3},{3,2},{4,5},{5,4},{6,7},{7,6},{8,9},{9,8},{10,11... | collective-permute-start | bytes 4718600 | tf_op jit(solution)/shard_map/while/body/ppermute | solution.py:20
  128.6 13.4 %collective-permute-start.10 = (bf16[3,64,1024]{2,1,0:T(8,128)(2,1)}, bf16[3,64,1024]{2,1,0:T(8,128)(2,1)}, u32[]{:S(2)}, u32[]{:S(2)}) collective-permute-start(bf16[3,64,1024]{2,1,0:T(8,128)(2,1)} %get-tuple-element.784), channel_id=1, source_target_pairs={{0,32},{32,64},{64,96},{96,0},{1,33},{33,65},{65,97},{97,1},{2,34}... | collective-permute-start | bytes 1179656 | tf_op jit(solution)/shard_map/while/body/ppermute | solution.py:20
  155.2 49.6 %collective-permute-start.23 = (bf16[3,256,1024]{2,1,0:T(8,128)(2,1)}, bf16[3,256,1024]{2,1,0:T(8,128)(2,1)}, u32[]{:S(2)}, u32[]{:S(2)}) collective-permute-start(bf16[3,256,1024]{2,1,0:T(8,128)(2,1)} %get-tuple-element.808), channel_id=1, source_target_pairs={{0,16},{16,0},{1,17},{17,1},{2,18},{18,2},{3,19},{19,3},{4,20},{20... | collective-permute-start | bytes 4718600 | tf_op jit(solution)/shard_map/while/body/ppermute | solution.py:20
  155.5 12.4 %collective-permute-start.11 = (bf16[3,64,1024]{2,1,0:T(8,128)(2,1)}, bf16[3,64,1024]{2,1,0:T(8,128)(2,1)S(1)}, u32[]{:S(2)}, u32[]{:S(2)}) collective-permute-start(bf16[3,64,1024]{2,1,0:T(8,128)(2,1)} %get-tuple-element.785), channel_id=1, source_target_pairs={{0,64},{32,96},{64,0},{96,32},{1,65},{33,97},{65,1},{97,33},{2,66}... | collective-permute-start | bytes 1179656 | tf_op jit(solution)/shard_map/while/body/ppermute | solution.py:20
  157.4 17.9 %collective-permute-start.12 = (bf16[3,64,1024]{2,1,0:T(8,128)(2,1)}, bf16[3,64,1024]{2,1,0:T(8,128)(2,1)S(1)}, u32[]{:S(2)}, u32[]{:S(2)}) collective-permute-start(bf16[3,64,1024]{2,1,0:T(8,128)(2,1)} %get-tuple-element.786), channel_id=1, source_target_pairs={{0,96},{32,0},{64,32},{96,64},{1,97},{33,1},{65,33},{97,65},{2,98}... | collective-permute-start | bytes 1179656 | tf_op jit(solution)/shard_map/while/body/ppermute | solution.py:20
  176.7 22.4 %collective-permute-start.19 = (bf16[2,64,1024]{2,1,0:T(8,128)(2,1)S(1)}, bf16[2,64,1024]{2,1,0:T(8,128)(2,1)S(1)}, u32[]{:S(2)}, u32[]{:S(2)}) collective-permute-start(bf16[2,64,1024]{2,1,0:T(8,128)(2,1)S(1)} %pad_maximum_fusion.10.refs_0_), channel_id=1, source_target_pairs={{0,96},{32,0},{64,32},{96,64},{1,97},{33,1},{65,33},{97,65},{2,98}... | collective-permute-start | bytes 786440 | tf_op jit(solution)/shard_map/while/body/ppermute | solution.py:20
  179.4 21.5 %collective-permute-start.20 = (bf16[2,64,1024]{2,1,0:T(8,128)(2,1)S(1)}, bf16[2,64,1024]{2,1,0:T(8,128)(2,1)S(1)}, u32[]{:S(2)}, u32[]{:S(2)}) collective-permute-start(bf16[2,64,1024]{2,1,0:T(8,128)(2,1)S(1)} %pad_maximum_fusion.10.refs_0_), channel_id=1, source_target_pairs={{0,64},{32,96},{64,0},{96,32},{1,65},{33,97},{65,1},{97,33},{2,66}... | collective-permute-start | bytes 786440 | tf_op jit(solution)/shard_map/while/body/ppermute | solution.py:20
  180.1 21.8 %collective-permute-start.21 = (bf16[2,64,1024]{2,1,0:T(8,128)(2,1)S(1)}, bf16[2,64,1024]{2,1,0:T(8,128)(2,1)}, u32[]{:S(2)}, u32[]{:S(2)}) collective-permute-start(bf16[2,64,1024]{2,1,0:T(8,128)(2,1)S(1)} %pad_maximum_fusion.10.refs_0_), channel_id=1, source_target_pairs={{0,32},{32,64},{64,96},{96,0},{1,33},{33,65},{65,97},{97,1},{2,34}... | collective-permute-start | bytes 786440 | tf_op jit(solution)/shard_map/while/body/ppermute | solution.py:20
  196.5 37.8 %collective-permute-start.27 = (bf16[3,128,1024]{2,1,0:T(8,128)(2,1)}, bf16[3,128,1024]{2,1,0:T(8,128)(2,1)}, u32[]{:S(2)}, u32[]{:S(2)}) collective-permute-start(bf16[3,128,1024]{2,1,0:T(8,128)(2,1)} %get-tuple-element.817), channel_id=1, source_target_pairs={{0,32},{32,64},{64,96},{96,0},{1,33},{33,65},{65,97},{97,1},{2,34}... | collective-permute-start | bytes 2359304 | tf_op jit(solution)/shard_map/while/body/ppermute | solution.py:20
  199.1 37.5 %collective-permute-start.28 = (bf16[3,128,1024]{2,1,0:T(8,128)(2,1)}, bf16[3,128,1024]{2,1,0:T(8,128)(2,1)}, u32[]{:S(2)}, u32[]{:S(2)}) collective-permute-start(bf16[3,128,1024]{2,1,0:T(8,128)(2,1)} %get-tuple-element.818), channel_id=1, source_target_pairs={{0,64},{32,96},{64,0},{96,32},{1,65},{33,97},{65,1},{97,33},{2,66}... | collective-permute-start | bytes 2359304 | tf_op jit(solution)/shard_map/while/body/ppermute | solution.py:20
  200.9 35.7 %collective-permute-start.29 = (bf16[3,128,1024]{2,1,0:T(8,128)(2,1)}, bf16[3,128,1024]{2,1,0:T(8,128)(2,1)}, u32[]{:S(2)}, u32[]{:S(2)}) collective-permute-start(bf16[3,128,1024]{2,1,0:T(8,128)(2,1)} %get-tuple-element.819), channel_id=1, source_target_pairs={{0,96},{32,0},{64,32},{96,64},{1,97},{33,1},{65,33},{97,65},{2,98}... | collective-permute-start | bytes 2359304 | tf_op jit(solution)/shard_map/while/body/ppermute | solution.py:20
  207.6 35.4 %collective-permute-start.24 = (bf16[3,64,1024]{2,1,0:T(8,128)(2,1)S(1)}, bf16[3,64,1024]{2,1,0:T(8,128)(2,1)S(1)}, u32[]{:S(2)}, u32[]{:S(2)}) collective-permute-start(bf16[3,64,1024]{2,1,0:T(8,128)(2,1)S(1)} %get-tuple-element.813), channel_id=1, source_target_pairs={{0,32},{32,64},{64,96},{96,0},{1,33},{33,65},{65,97},{97,1},{2,34}... | collective-permute-start | bytes 1179656 | tf_op jit(solution)/shard_map/while/body/ppermute | solution.py:20
  208.7 42.9 %collective-permute-start.25 = (bf16[3,64,1024]{2,1,0:T(8,128)(2,1)S(1)}, bf16[3,64,1024]{2,1,0:T(8,128)(2,1)S(1)}, u32[]{:S(2)}, u32[]{:S(2)}) collective-permute-start(bf16[3,64,1024]{2,1,0:T(8,128)(2,1)S(1)} %get-tuple-element.814), channel_id=1, source_target_pairs={{0,64},{32,96},{64,0},{96,32},{1,65},{33,97},{65,1},{97,33},{2,66}... | collective-permute-start | bytes 1179656 | tf_op jit(solution)/shard_map/while/body/ppermute | solution.py:20
  234.2 17.4 %collective-permute-start.26 = (bf16[3,64,1024]{2,1,0:T(8,128)(2,1)S(1)}, bf16[3,64,1024]{2,1,0:T(8,128)(2,1)S(1)}, u32[]{:S(2)}, u32[]{:S(2)}) collective-permute-start(bf16[3,64,1024]{2,1,0:T(8,128)(2,1)S(1)} %get-tuple-element.815), channel_id=1, source_target_pairs={{0,96},{32,0},{64,32},{96,64},{1,97},{33,1},{65,33},{97,65},{2,98}... | collective-permute-start | bytes 1179656 | tf_op jit(solution)/shard_map/while/body/ppermute | solution.py:20
  238.9 13.9 %collective-permute-start.33 = (bf16[3,64,1024]{2,1,0:T(8,128)(2,1)S(1)}, bf16[3,64,1024]{2,1,0:T(8,128)(2,1)S(1)}, u32[]{:S(2)}, u32[]{:S(2)}) collective-permute-start(bf16[3,64,1024]{2,1,0:T(8,128)(2,1)S(1)} %slice.559), channel_id=1, source_target_pairs={{0,16},{16,0},{1,17},{17,1},{2,18},{18,2},{3,19},{19,3},{4,20},{20... | collective-permute-start | bytes 1179656 | tf_op jit(solution)/shard_map/while/body/ppermute | solution.py:20
  253.5 12.2 %collective-permute-start.34 = (bf16[1,192,1024]{2,1,0:T(8,128)(2,1)S(1)}, bf16[1,192,1024]{2,1,0:T(8,128)(2,1)}, u32[]{:S(2)}, u32[]{:S(2)}) collective-permute-start(bf16[1,192,1024]{2,1,0:T(8,128)(2,1)S(1)} %maximum_bitcast_fusion.2.refs_0_), channel_id=1, source_target_pairs={{0,16},{16,0},{1,17},{17,1},{2,18},{18,2},{3,19},{19,3},{4,20},{20... | collective-permute-start | bytes 1179656 | tf_op jit(solution)/shard_map/while/body/ppermute | solution.py:20
  255.2 67.5 %collective-permute-start.22 = (bf16[2,256,1024]{2,1,0:T(8,128)(2,1)S(1)}, bf16[2,256,1024]{2,1,0:T(8,128)(2,1)}, u32[]{:S(2)}, u32[]{:S(2)}) collective-permute-start(bf16[2,256,1024]{2,1,0:T(8,128)(2,1)S(1)} %copy-done.3), channel_id=1, source_target_pairs={{0,16},{16,0},{1,17},{17,1},{2,18},{18,2},{3,19},{19,3},{4,20},{20... | collective-permute-start | bytes 3145736 | tf_op jit(solution)/shard_map/while/body/ppermute | solution.py:20
  256.1 13.5 %collective-permute-start.30 = (bf16[2,64,1024]{2,1,0:T(8,128)(2,1)}, bf16[2,64,1024]{2,1,0:T(8,128)(2,1)}, u32[]{:S(2)}, u32[]{:S(2)}) collective-permute-start(bf16[2,64,1024]{2,1,0:T(8,128)(2,1)} %pad_maximum_fusion.11.refs_0_), channel_id=1, source_target_pairs={{0,96},{32,0},{64,32},{96,64},{1,97},{33,1},{65,33},{97,65},{2,98}... | collective-permute-start | bytes 786440 | tf_op jit(solution)/shard_map/while/body/ppermute | solution.py:20
  258.3 11.3 %collective-permute-start.31 = (bf16[2,64,1024]{2,1,0:T(8,128)(2,1)}, bf16[2,64,1024]{2,1,0:T(8,128)(2,1)}, u32[]{:S(2)}, u32[]{:S(2)}) collective-permute-start(bf16[2,64,1024]{2,1,0:T(8,128)(2,1)} %pad_maximum_fusion.11.refs_0_), channel_id=1, source_target_pairs={{0,64},{32,96},{64,0},{96,32},{1,65},{33,97},{65,1},{97,33},{2,66}... | collective-permute-start | bytes 786440 | tf_op jit(solution)/shard_map/while/body/ppermute | solution.py:20
  259.5 13.8 %collective-permute-start.32 = (bf16[2,64,1024]{2,1,0:T(8,128)(2,1)}, bf16[2,64,1024]{2,1,0:T(8,128)(2,1)}, u32[]{:S(2)}, u32[]{:S(2)}) collective-permute-start(bf16[2,64,1024]{2,1,0:T(8,128)(2,1)} %pad_maximum_fusion.11.refs_0_), channel_id=1, source_target_pairs={{0,32},{32,64},{64,96},{96,0},{1,33},{33,65},{65,97},{97,1},{2,34}... | collective-permute-start | bytes 786440 | tf_op jit(solution)/shard_map/while/body/ppermute | solution.py:20
  276.2 70.0 %collective-permute-start.35 = (bf16[2,256,1024]{2,1,0:T(8,128)(2,1)}, bf16[2,256,1024]{2,1,0:T(8,128)(2,1)}, u32[]{:S(2)}, u32[]{:S(2)}) collective-permute-start(bf16[2,256,1024]{2,1,0:T(8,128)(2,1)} %body.85.refs_0_), channel_id=1, source_target_pairs={{0,16},{16,0},{1,17},{17,1},{2,18},{18,2},{3,19},{19,3},{4,20},{20... | collective-permute-start | bytes 3145736 | tf_op jit(solution)/shard_map/while/body/ppermute | solution.py:20
  277.2 36.4 %collective-permute-start.36 = (bf16[2,64,1024]{2,1,0:T(8,128)(2,1)S(1)}, bf16[2,64,1024]{2,1,0:T(8,128)(2,1)S(1)}, u32[]{:S(2)}, u32[]{:S(2)}) collective-permute-start(bf16[2,64,1024]{2,1,0:T(8,128)(2,1)S(1)} %copy-done.11), channel_id=1, source_target_pairs={{0,16},{16,0},{1,17},{17,1},{2,18},{18,2},{3,19},{19,3},{4,20},{20... | collective-permute-start | bytes 786440 | tf_op jit(solution)/shard_map/while/body/ppermute | solution.py:20
  316.8 25.7 %collective-permute-start.37 = (bf16[2,128,1024]{2,1,0:T(8,128)(2,1)}, bf16[2,128,1024]{2,1,0:T(8,128)(2,1)S(1)}, u32[]{:S(2)}, u32[]{:S(2)}) collective-permute-start(bf16[2,128,1024]{2,1,0:T(8,128)(2,1)} %body.86.refs_2_), channel_id=1, source_target_pairs={{0,96},{32,0},{64,32},{96,64},{1,97},{33,1},{65,33},{97,65},{2,98}... | collective-permute-start | bytes 1572872 | tf_op jit(solution)/shard_map/while/body/ppermute | solution.py:20
  320.6 21.9 %collective-permute-start.38 = (bf16[2,128,1024]{2,1,0:T(8,128)(2,1)}, bf16[2,128,1024]{2,1,0:T(8,128)(2,1)}, u32[]{:S(2)}, u32[]{:S(2)}) collective-permute-start(bf16[2,128,1024]{2,1,0:T(8,128)(2,1)} %body.86.refs_2_), channel_id=1, source_target_pairs={{0,64},{32,96},{64,0},{96,32},{1,65},{33,97},{65,1},{97,33},{2,66}... | collective-permute-start | bytes 1572872 | tf_op jit(solution)/shard_map/while/body/ppermute | solution.py:20
  321.4 24.7 %collective-permute-start.39 = (bf16[2,128,1024]{2,1,0:T(8,128)(2,1)}, bf16[2,128,1024]{2,1,0:T(8,128)(2,1)}, u32[]{:S(2)}, u32[]{:S(2)}) collective-permute-start(bf16[2,128,1024]{2,1,0:T(8,128)(2,1)} %body.86.refs_2_), channel_id=1, source_target_pairs={{0,32},{32,64},{64,96},{96,0},{1,33},{33,65},{65,97},{97,1},{2,34}... | collective-permute-start | bytes 1572872 | tf_op jit(solution)/shard_map/while/body/ppermute | solution.py:20
  359.3 11.7 %collective-permute-start.41 = (bf16[768,1024]{1,0:T(8,128)(2,1)}, bf16[768,1024]{1,0:T(8,128)(2,1)S(1)}, u32[]{:S(2)}, u32[]{:S(2)}) collective-permute-start(bf16[768,1024]{1,0:T(8,128)(2,1)} %get-tuple-element.856), channel_id=1, source_target_pairs={{0,1},{1,0},{2,3},{3,2},{4,5},{5,4},{6,7},{7,6},{8,9},{9,8},{10,11... | collective-permute-start | bytes 4718600 | tf_op jit(solution)/shard_map/while/body/ppermute | solution.py:20
  362.4 26.0 %collective-permute-start.54 = (bf16[1,384,1024]{2,1,0:T(8,128)(2,1)}, bf16[1,384,1024]{2,1,0:T(8,128)(2,1)}, u32[]{:S(2)}, u32[]{:S(2)}) collective-permute-start(bf16[1,384,1024]{2,1,0:T(8,128)(2,1)} %body.84.refs_0_), channel_id=1, source_target_pairs={{0,96},{32,0},{64,32},{96,64},{1,97},{33,1},{65,33},{97,65},{2,98}... | collective-permute-start | bytes 2359304 | tf_op jit(solution)/shard_map/while/body/ppermute | solution.py:20
  363.2 25.3 %collective-permute-start.55 = (bf16[1,384,1024]{2,1,0:T(8,128)(2,1)}, bf16[1,384,1024]{2,1,0:T(8,128)(2,1)}, u32[]{:S(2)}, u32[]{:S(2)}) collective-permute-start(bf16[1,384,1024]{2,1,0:T(8,128)(2,1)} %body.84.refs_0_), channel_id=1, source_target_pairs={{0,64},{32,96},{64,0},{96,32},{1,65},{33,97},{65,1},{97,33},{2,66}... | collective-permute-start | bytes 2359304 | tf_op jit(solution)/shard_map/while/body/ppermute | solution.py:20
  363.6 37.9 %collective-permute-start.56 = (bf16[1,384,1024]{2,1,0:T(8,128)(2,1)}, bf16[1,384,1024]{2,1,0:T(8,128)(2,1)}, u32[]{:S(2)}, u32[]{:S(2)}) collective-permute-start(bf16[1,384,1024]{2,1,0:T(8,128)(2,1)} %body.84.refs_0_), channel_id=1, source_target_pairs={{0,32},{32,64},{64,96},{96,0},{1,33},{33,65},{65,97},{97,1},{2,34}... | collective-permute-start | bytes 2359304 | tf_op jit(solution)/shard_map/while/body/ppermute | solution.py:20
  370.9 39.2 %collective-permute-start.40 = (bf16[256,1024]{1,0:T(8,128)(2,1)}, bf16[256,1024]{1,0:T(8,128)(2,1)}, u32[]{:S(2)}, u32[]{:S(2)}) collective-permute-start(bf16[256,1024]{1,0:T(8,128)(2,1)} %get-tuple-element.854), channel_id=1, source_target_pairs={{0,1},{1,0},{2,3},{3,2},{4,5},{5,4},{6,7},{7,6},{8,9},{9,8},{10,11... | collective-permute-start | bytes 1572872 | tf_op jit(solution)/shard_map/while/body/ppermute | solution.py:20
  378.4 31.7 %collective-permute-start.42 = (bf16[4,96,512]{2,1,0:T(8,128)(2,1)}, bf16[4,96,512]{2,1,0:T(8,128)(2,1)S(1)}, u32[]{:S(2)}, u32[]{:S(2)}) collective-permute-start(bf16[4,96,512]{2,1,0:T(8,128)(2,1)} %slice_bitcast_fusion.14), channel_id=1, source_target_pairs={{0,8},{8,0},{1,9},{9,1},{2,10},{10,2},{3,11},{11,3},{4,12},{12,4},... | collective-permute-start | bytes 1179656 | tf_op jit(solution)/shard_map/while/body/ppermute | solution.py:20
  388.5 21.6 %collective-permute-start.43 = (bf16[2,96,512]{2,1,0:T(8,128)(2,1)}, bf16[2,96,512]{2,1,0:T(8,128)(2,1)}, u32[]{:S(2)}, u32[]{:S(2)}) collective-permute-start(bf16[2,96,512]{2,1,0:T(8,128)(2,1)} %get-tuple-element.860), channel_id=1, source_target_pairs={{0,2},{2,4},{4,6},{6,0},{1,3},{3,5},{5,7},{7,1},{8,10},{10,12},{12... | collective-permute-start | bytes 589832 | tf_op jit(solution)/shard_map/while/body/ppermute | solution.py:20
  388.5 21.6 %collective-permute-start.44 = (bf16[2,96,512]{2,1,0:T(8,128)(2,1)}, bf16[2,96,512]{2,1,0:T(8,128)(2,1)}, u32[]{:S(2)}, u32[]{:S(2)}) collective-permute-start(bf16[2,96,512]{2,1,0:T(8,128)(2,1)} %get-tuple-element.861), channel_id=1, source_target_pairs={{0,4},{2,6},{4,0},{6,2},{1,5},{3,7},{5,1},{7,3},{8,12},{10,14},{12... | collective-permute-start | bytes 589832 | tf_op jit(solution)/shard_map/while/body/ppermute | solution.py:20
  410.3 13.3 %collective-permute-start.48 = (bf16[96,512]{1,0:T(8,128)(2,1)S(1)}, bf16[96,512]{1,0:T(8,128)(2,1)S(1)}, u32[]{:S(2)}, u32[]{:S(2)}) collective-permute-start(bf16[96,512]{1,0:T(8,128)(2,1)S(1)} %get-tuple-element.871), channel_id=1, source_target_pairs={{0,2},{2,4},{4,6},{6,0},{1,3},{3,5},{5,7},{7,1},{8,10},{10,12},{12... | collective-permute-start | bytes 294920 | tf_op jit(solution)/shard_map/while/body/ppermute | solution.py:20
  411.3 12.3 %collective-permute-start.49 = (bf16[96,512]{1,0:T(8,128)(2,1)S(1)}, bf16[96,512]{1,0:T(8,128)(2,1)S(1)}, u32[]{:S(2)}, u32[]{:S(2)}) collective-permute-start(bf16[96,512]{1,0:T(8,128)(2,1)S(1)} %get-tuple-element.872), channel_id=1, source_target_pairs={{0,4},{2,6},{4,0},{6,2},{1,5},{3,7},{5,1},{7,3},{8,12},{10,14},{12... | collective-permute-start | bytes 294920 | tf_op jit(solution)/shard_map/while/body/ppermute | solution.py:20
  (60 other events, 452.4 us)

commit v3 on v0

--- a/solution.py
+++ b/solution.py
@@ -278,7 +278,7 @@
         return (total + dot(first[:, :units], other_first, (0, 0)) + dot(late[:, :units], other_late, (0, 0))).astype(BF)
 
     rows0, rows1, width = r0 // 2, halves[0].shape[0] // 8, x0.shape[1]
-    own1, swap1 = after(dg0, halves[0], swap1)
+    own1, swap1 = after(dgd, halves[0], swap1)
     total1 = (own1.astype(F32) + swap1.astype(F32)).reshape(2, 4, rows1, width)
     left, right = total1[..., : width // 2], total1[..., width // 2 :]
     far_left = shift(left[1].astype(BF), "xh", 2, 1)

time: 374 us -> 374 us (level)
  no operation moved by 1% of the time
where the time goes in v3:
time: 374 us; the launch traced here: 370 us
  waiting for transfers between devices  136 us (36%)
  Pallas kernels  91.9 us (25%)
  starting transfers between devices  76.7 us (21%)
  other arithmetic  28.5 us (8%)
  local copies, waits for them, and re-layouts  18 us (5%)
  matrix products  14 us (4%)
    ppermute x57, waiting for transfers between devices, shift(): lax.ppermute(value, axis, [(i, (i + step) % size) for i in range(size)])  136 us
    ppermute x57, starting transfers between devices, shift(): lax.ppermute(value, axis, [(i, (i + step) % size) for i in range(size)])  76.7 us
    pallas_call x3, Pallas kernels, project(): pl.pallas_call(kernel, out_shape=[jax.ShapeDtypeStruct(s, BF) for s in sh...  37.3 us
    pallas_call x12, Pallas kernels, move(): pl.pallas_call(kernel, out_shape=[jax.ShapeDtypeStruct(s, BF) for s in sh...  35.3 us
    pallas_call x2, Pallas kernels, unproject(): pl.pallas_call(kernel, out_shape=[jax.ShapeDtypeStruct(s, BF) for s in sh...  19.3 us
    dot_general x6, matrix products, dot(): lax.dot_general(left, right, ((dims[:1], dims[1:]), ((), ())), preferred_...  14 us
    while x104, local copies, waits for them, and re-layouts  8.41 us
  transfers between devices with their start and end apart: 57, of which 23 were waited for; matrix products, arithmetic and copies ran while one was open for 13% of the time, Pallas kernels for 19%

profile of v3, /device:TPU:0, one launch (start us, length us, event | category | flops | bytes accessed | tf_op | source)
XLA Modules:
  0.0 369.5 jit_solution(17819506008268428042)
XLA Ops:
  4.4 363.3 %while.21 = (s32[]{:T(128)}, bf16[32,1024]{1,0:T(8,128)(2,1)}, bf16[96,1024]{1,0:T(8,128)(2,1)}, bf16[960,1024]{1,0:T(8,128)(2,1)}, bf16[960,1024]{1,0:T(8,128)(...) while((s32[]{:T(128)}, bf16[32,1024]{1,0:T(8,128)(2,1)}, ...), condition=%wide.region_4.5_spmd, body=%wide.region_1.4_spmd.sunk | while | flops 9105185792 | bytes 403179456 | solution.py:377
  4.7 3.2 collective-permute-start
  7.9 3.5 collective-permute-done.refs_1_
  14.3 4.3 %collective-permute-start.1 = (bf16[128,1024]{1,0:T(8,128)(2,1)}, bf16[128,1024]{1,0:T(8,128)(2,1)S(1)}, u32[]{:S(2)}, u32[]{:S(2)}) collective-permute-start(bf16[128,1024]{1,0:T(8,128)(2,1)} %body.73.refs_0_), channel_id=1, source_target_pairs={{0,6},{2,0},{4,2},{6,4},{1,7},{3,1},{5,3},{7,5},{8,14},{10,8},{12,... | collective-permute-start | bytes 786440 | tf_op jit(solution)/shard_map/while/body/ppermute | solution.py:20
  19.8 9.4 %collective-permute-done.1.refs_1_ = bf16[128,1024]{1,0:T(8,128)(2,1)S(1)} collective-permute-done((bf16[128,1024]{1,0:T(8,128)(2,1)}, bf16[128,1024]{1,0:T(8,128)(2,1)S(1)}, u32[]{:S(2)}, u32[]{:S(2)}) %collective-permute-start.1) | collective-permute-done | bytes 262176 | tf_op jit(solution)/shard_map/while/body/ppermute | solution.py:20
  29.5 3.0 collective-permute-done.3.refs_3_
  33.2 2.9 body.74.refs_0_
  36.3 3.1 collective-permute-start.5
  41.4 3.8 %collective-permute-done.5.refs_1_ = bf16[96,1024]{1,0:T(8,128)(2,1)} collective-permute-done((bf16[96,1024]{1,0:T(8,128)(2,1)S(1)}, bf16[96,1024]{1,0:T(8,128)(2,1)}, u32[]{:S(2)}, u32[]{:S(2)}) %collective-permute-start.5) | collective-permute-done | bytes 196640 | tf_op jit(solution)/shard_map/while/body/ppermute | solution.py:20
  49.7 3.7 body.76
  53.5 2.7 body.77.refs_0_
  56.2 10.9 %body.78 = (bf16[3,128,1024]{2,1,0:T(8,128)(2,1)}, bf16[3,128,1024]{2,1,0:T(8,128)(2,1)}, bf16[3,128,1024]{2,1,0:T(8,128)(2,1)}, bf16[3,128,1024]{2,1,0:T(8,128)(2,1)}) custom-call(s32[2]{0:T(128)S(1)} %get-tuple-element.943.place_ref, bf16[512,1024]{1,0:T(8,128)(2,1)} %get-tuple-element.774.refs_0_, bf16[512,1024]{1,0:T(8,128)(2,1)} %get-tuple-element.775.refs_1_, ...), custom_call_target="tpu_custom_call" | custom-call | tf_op jit(solution)/shard_map/while/body/pallas_call | solution.py:141
  67.1 3.1 collective-permute-start.11
  70.2 3.0 collective-permute-start.12
  74.3 12.5 %collective-permute-done.14.refs_2_ = bf16[192,1024]{1,0:T(8,128)(2,1)S(1)} collective-permute-done((bf16[192,1024]{1,0:T(8,128)(2,1)S(1)}, bf16[192,1024]{1,0:T(8,128)(2,1)S(1)}, u32[]{:S(2)}, u32[]{:S(2)}) %collective-permute-start.14) | collective-permute-done | bytes 393248 | tf_op jit(solution)/shard_map/while/body/ppermute | solution.py:20
  86.8 6.3 %collective-permute-done.15.refs_3_ = bf16[192,1024]{1,0:T(8,128)(2,1)S(1)} collective-permute-done((bf16[192,1024]{1,0:T(8,128)(2,1)S(1)}, bf16[192,1024]{1,0:T(8,128)(2,1)S(1)}, u32[]{:S(2)}, u32[]{:S(2)}) %collective-permute-start.15) | collective-permute-done | bytes 393248 | tf_op jit(solution)/shard_map/while/body/ppermute | solution.py:20
  93.8 3.2 body.79.refs_3_
  97.1 3.1 body.80.refs_1_
  109.3 11.4 %body.81 = (bf16[512,1024]{1,0:T(8,128)(2,1)}, bf16[512,1024]{1,0:T(8,128)(2,1)}, bf16[3,256,1024]{2,1,0:T(8,128)(2,1)}, bf16[3,256,1024]{2,1,0:T(8,128)(2,1)}) custom-call(s32[2]{0:T(128)} %copy-done.30, s32[1,1536]{1,0:T(1,128)} %fusion.143.refs_0_, bf16[768,1024]{1,0:T(8,128)(2,1)} %body.80.refs_1_, bf16[768,1024]{1,0:T(8,128)(2,1)} %collective-permute-done.16.refs_2_, ...), custom_call_target="tpu_custom_call" | custom-call | tf_op jit(solution)/shard_map/while/body/pallas_call | solution.py:141
  122.3 5.0 %collective-permute-done.10 = bf16[3,128,1024]{2,1,0:T(8,128)(2,1)} collective-permute-done((bf16[3,128,1024]{2,1,0:T(8,128)(2,1)}, bf16[3,128,1024]{2,1,0:T(8,128)(2,1)}, u32[]{:S(2)}, u32[]{:S(2)}) %collective-permute-start.10) | collective-permute-done | bytes 786464 | tf_op jit(solution)/shard_map/while/body/ppermute | solution.py:20
  132.3 15.0 %body.82 = (bf16[512,1024]{1,0:T(8,128)(2,1)}, bf16[512,1024]{1,0:T(8,128)(2,1)}, bf16[3,128,1024]{2,1,0:T(8,128)(2,1)}, bf16[3,128,1024]{2,1,0:T(8,128)(2,1)}, ...) custom-call(s32[2]{0:T(128)} %copy-done.30, s32[1,1536]{1,0:T(1,128)} %sub.274.refs_0_, ...), custom_call_target="tpu_custom_call" | custom-call | tf_op jit(solution)/shard_map/while/body/pallas_call | solution.py:141
  147.9 3.8 %collective-permute-start.20 = (bf16[3,128,1024]{2,1,0:T(8,128)(2,1)}, bf16[3,128,1024]{2,1,0:T(8,128)(2,1)S(1)}, u32[]{:S(2)}, u32[]{:S(2)}) collective-permute-start(bf16[3,128,1024]{2,1,0:T(8,128)(2,1)} %get-tuple-element.794), channel_id=1, source_target_pairs={{0,64},{32,96},{64,0},{96,32},{1,65},{33,97},{65,1},{97,33},{2,66}... | collective-permute-start | bytes 2359304 | tf_op jit(solution)/shard_map/while/body/ppermute | solution.py:20
  151.9 13.7 %collective-permute-done.18 = bf16[3,64,1024]{2,1,0:T(8,128)(2,1)} collective-permute-done((bf16[3,64,1024]{2,1,0:T(8,128)(2,1)}, bf16[3,64,1024]{2,1,0:T(8,128)(2,1)}, u32[]{:S(2)}, u32[]{:S(2)}) %collective-permute-start.18) | collective-permute-done | bytes 393248 | tf_op jit(solution)/shard_map/while/body/ppermute | solution.py:20
  166.7 2.7 fusion.145
  169.5 15.8 %collective-permute-done.20 = bf16[3,128,1024]{2,1,0:T(8,128)(2,1)S(1)} collective-permute-done((bf16[3,128,1024]{2,1,0:T(8,128)(2,1)}, bf16[3,128,1024]{2,1,0:T(8,128)(2,1)S(1)}, u32[]{:S(2)}, u32[]{:S(2)}) %collective-permute-start.20) | collective-permute-done | bytes 786464 | tf_op jit(solution)/shard_map/while/body/ppermute | solution.py:20
  186.7 2.9 collective-permute-start.25
  194.1 3.3 collective-permute-done.24
  197.5 9.6 %collective-permute-done.25 = bf16[3,64,1024]{2,1,0:T(8,128)(2,1)S(1)} collective-permute-done((bf16[3,64,1024]{2,1,0:T(8,128)(2,1)S(1)}, bf16[3,64,1024]{2,1,0:T(8,128)(2,1)S(1)}, u32[]{:S(2)}, u32[]{:S(2)}) %collective-permute-start.25) | collective-permute-done | bytes 393248 | tf_op jit(solution)/shard_map/while/body/ppermute | solution.py:20
  217.4 3.0 collective-permute-start.27
  222.3 3.6 collective-permute-done.34.refs_1_
  227.3 2.7 body.84.refs_0_
  230.0 3.2 collective-permute-done.32.refs_3_
  233.2 3.0 body.85.refs_0_
  240.4 3.3 collective-permute-start.37
  244.5 5.7 %collective-permute-start.39 = (bf16[2,128,1024]{2,1,0:T(8,128)(2,1)}, bf16[2,128,1024]{2,1,0:T(8,128)(2,1)}, u32[]{:S(2)}, u32[]{:S(2)}) collective-permute-start(bf16[2,128,1024]{2,1,0:T(8,128)(2,1)} %body.86.refs_2_), channel_id=1, source_target_pairs={{0,32},{32,64},{64,96},{96,0},{1,33},{33,65},{65,97},{97,1},{2,34}... | collective-permute-start | bytes 1572872 | tf_op jit(solution)/shard_map/while/body/ppermute | solution.py:20
  250.2 3.3 fusion.149.refs_8_
  253.5 11.9 %collective-permute-done.29.refs_3_ = bf16[2,128,1024]{2,1,0:T(8,128)(2,1)} collective-permute-done((bf16[2,128,1024]{2,1,0:T(8,128)(2,1)}, bf16[2,128,1024]{2,1,0:T(8,128)(2,1)}, u32[]{:S(2)}, u32[]{:S(2)}) %collective-permute-start.29) | collective-permute-done | bytes 524320 | tf_op jit(solution)/shard_map/while/body/ppermute | solution.py:20
  267.0 9.7 %collective-permute-done.39.refs_5_ = bf16[2,128,1024]{2,1,0:T(8,128)(2,1)} collective-permute-done((bf16[2,128,1024]{2,1,0:T(8,128)(2,1)}, bf16[2,128,1024]{2,1,0:T(8,128)(2,1)}, u32[]{:S(2)}, u32[]{:S(2)}) %collective-permute-start.39) | collective-permute-done | bytes 524320 | tf_op jit(solution)/shard_map/while/body/ppermute | solution.py:20
  276.7 13.1 %body.87 = (bf16[1024,1024]{1,0:T(8,128)(2,1)}, bf16[1024,1024]{1,0:T(8,128)(2,1)}, bf16[768,1024]{1,0:T(8,128)(2,1)}, bf16[768,1024]{1,0:T(8,128)(2,1)}) custom-call(s32[2]{0:T(128)} %copy-done.30, bf16[2,256,1024]{2,1,0:T(8,128)(2,1)} %body.85.refs_0_, bf16[2,256,1024]{2,1,0:T(8,128)(2,1)} %collective-permute-done.35.refs_1_, ...), custom_call_target="tpu_custom_call" | custom-call | tf_op jit(solution)/shard_map/while/body/pallas_call | solution.py:186
  289.9 3.1 pad_maximum_fusion.13
  295.1 6.2 %body.88 = (bf16[512,1024]{1,0:T(8,128)(2,1)}, bf16[512,1024]{1,0:T(8,128)(2,1)}, bf16[256,1024]{1,0:T(8,128)(2,1)}, bf16[256,1024]{1,0:T(8,128)(2,1)}) custom-call(s32[2]{0:T(128)S(1)} %copy-done.31, bf16[2,128,1024]{2,1,0:T(8,128)(2,1)} %body.83.refs_0_, bf16[2,128,1024]{2,1,0:T(8,128)(2,1)} %collective-permute-done.27.refs_1_, ...), custom_call_target="tpu_custom_call" | custom-call | tf_op jit(solution)/shard_map/while/body/pallas_call | solution.py:186
  302.8 2.7 convert_add_fusion.11
  320.7 11.1 %collective-permute-done.56.refs_3_ = bf16[1,384,1024]{2,1,0:T(8,128)(2,1)} collective-permute-done((bf16[1,384,1024]{2,1,0:T(8,128)(2,1)}, bf16[1,384,1024]{2,1,0:T(8,128)(2,1)}, u32[]{:S(2)}, u32[]{:S(2)}) %collective-permute-start.56) | collective-permute-done | bytes 786464 | tf_op jit(solution)/shard_map/while/body/ppermute | solution.py:20
  332.4 4.4 %body.89 = (bf16[512,1024]{1,0:T(8,128)(2,1)}, bf16[1024,1024]{1,0:T(8,128)(2,1)}) custom-call(s32[2]{0:T(128)S(1)} %copy-done.31, bf16[1,384,1024]{2,1,0:T(8,128)(2,1)} %body.84.refs_0_, bf16[1,384,1024]{2,1,0:T(8,128)(2,1)} %collective-permute-done.54.refs_1_, bf16[1,384,1024]{2,1,0:T(8,128)(2,1)} %collective-permute-done.55.refs_2_, ...), custom_call_target="tpu_custom_call" | custom-call | tf_op jit(solution)/shard_map/while/body/pallas_call | solution.py:38
  336.8 2.8 fusion.161
  350.8 3.0 add_convert_fusion.8
  353.9 3.7 %collective-permute-done.46 = bf16[128,1024]{1,0:T(8,128)(2,1)S(1)} collective-permute-done((bf16[128,1024]{1,0:T(8,128)(2,1)S(1)}, bf16[128,1024]{1,0:T(8,128)(2,1)S(1)}, u32[]{:S(2)}, u32[]{:S(2)}) %collective-permute-start.46) | collective-permute-done | bytes 262176 | tf_op jit(solution)/shard_map/while/body/ppermute | solution.py:20
  362.1 2.8 collective-permute-done.52
  (262 shorter events, 98.6 us)
Async XLA Ops:
  14.3 15.0 %collective-permute-start.1 = (bf16[128,1024]{1,0:T(8,128)(2,1)}, bf16[128,1024]{1,0:T(8,128)(2,1)S(1)}, u32[]{:S(2)}, u32[]{:S(2)}) collective-permute-start(bf16[128,1024]{1,0:T(8,128)(2,1)} %body.73.refs_0_), channel_id=1, source_target_pairs={{0,6},{2,0},{4,2},{6,4},{1,7},{3,1},{5,3},{7,5},{8,14},{10,8},{12,... | collective-permute-start | bytes 786440 | tf_op jit(solution)/shard_map/while/body/ppermute | solution.py:20
  18.6 11.0 %collective-permute-start.2 = (bf16[128,1024]{1,0:T(8,128)(2,1)}, bf16[128,1024]{1,0:T(8,128)(2,1)S(1)}, u32[]{:S(2)}, u32[]{:S(2)}) collective-permute-start(bf16[128,1024]{1,0:T(8,128)(2,1)} %body.73.refs_0_), channel_id=1, source_target_pairs={{0,4},{2,6},{4,0},{6,2},{1,5},{3,7},{5,1},{7,3},{8,12},{10,14},{12... | collective-permute-start | bytes 786440 | tf_op jit(solution)/shard_map/while/body/ppermute | solution.py:20
  18.6 13.9 %collective-permute-start.3 = (bf16[128,1024]{1,0:T(8,128)(2,1)}, bf16[128,1024]{1,0:T(8,128)(2,1)S(1)}, u32[]{:S(2)}, u32[]{:S(2)}) collective-permute-start(bf16[128,1024]{1,0:T(8,128)(2,1)} %body.73.refs_0_), channel_id=1, source_target_pairs={{0,2},{2,4},{4,6},{6,0},{1,3},{3,5},{5,7},{7,1},{8,10},{10,12},{12... | collective-permute-start | bytes 786440 | tf_op jit(solution)/shard_map/while/body/ppermute | solution.py:20
  36.1 12.7 %collective-permute-start.4 = (bf16[512,1024]{1,0:T(8,128)(2,1)}, bf16[512,1024]{1,0:T(8,128)(2,1)S(1)}, u32[]{:S(2)}, u32[]{:S(2)}) collective-permute-start(bf16[512,1024]{1,0:T(8,128)(2,1)} %body.74.refs_0_), channel_id=1, source_target_pairs={{0,1},{1,0},{2,3},{3,2},{4,5},{5,4},{6,7},{7,6},{8,9},{9,8},{10,11... | collective-permute-start | bytes 3145736 | tf_op jit(solution)/shard_map/while/body/ppermute | solution.py:20
  39.4 14.0 %collective-permute-start.6 = (bf16[96,1024]{1,0:T(8,128)(2,1)S(1)}, bf16[96,1024]{1,0:T(8,128)(2,1)}, u32[]{:S(2)}, u32[]{:S(2)}) collective-permute-start(bf16[96,1024]{1,0:T(8,128)(2,1)S(1)} %bitcast.161), channel_id=1, source_target_pairs={{0,6},{2,0},{4,2},{6,4},{1,7},{3,1},{5,3},{7,5},{8,14},{10,8},{12,... | collective-permute-start | bytes 589832 | tf_op jit(solution)/shard_map/while/body/ppermute | solution.py:20
  40.5 13.0 %collective-permute-start.7 = (bf16[96,1024]{1,0:T(8,128)(2,1)S(1)}, bf16[96,1024]{1,0:T(8,128)(2,1)}, u32[]{:S(2)}, u32[]{:S(2)}) collective-permute-start(bf16[96,1024]{1,0:T(8,128)(2,1)S(1)} %bitcast.162), channel_id=1, source_target_pairs={{0,4},{2,6},{4,0},{6,2},{1,5},{3,7},{5,1},{7,3},{8,12},{10,14},{12... | collective-permute-start | bytes 589832 | tf_op jit(solution)/shard_map/while/body/ppermute | solution.py:20
  40.6 12.8 %collective-permute-start.8 = (bf16[96,1024]{1,0:T(8,128)(2,1)S(1)}, bf16[96,1024]{1,0:T(8,128)(2,1)}, u32[]{:S(2)}, u32[]{:S(2)}) collective-permute-start(bf16[96,1024]{1,0:T(8,128)(2,1)S(1)} %bitcast.163), channel_id=1, source_target_pairs={{0,2},{2,4},{4,6},{6,0},{1,3},{3,5},{5,7},{7,1},{8,10},{10,12},{12... | collective-permute-start | bytes 589832 | tf_op jit(solution)/shard_map/while/body/ppermute | solution.py:20
  47.6 25.8 %collective-permute-start.13 = (bf16[192,1024]{1,0:T(8,128)(2,1)}, bf16[192,1024]{1,0:T(8,128)(2,1)}, u32[]{:S(2)}, u32[]{:S(2)}) collective-permute-start(bf16[192,1024]{1,0:T(8,128)(2,1)} %body.75.refs_0_), channel_id=1, source_target_pairs={{0,6},{2,0},{4,2},{6,4},{1,7},{3,1},{5,3},{7,5},{8,14},{10,8},{12,... | collective-permute-start | bytes 1179656 | tf_op jit(solution)/shard_map/while/body/ppermute | solution.py:20
  67.1 25.9 %collective-permute-start.11 = (bf16[3,128,1024]{2,1,0:T(8,128)(2,1)}, bf16[3,128,1024]{2,1,0:T(8,128)(2,1)}, u32[]{:S(2)}, u32[]{:S(2)}) collective-permute-start(bf16[3,128,1024]{2,1,0:T(8,128)(2,1)} %get-tuple-element.779), channel_id=1, source_target_pairs={{0,96},{32,0},{64,32},{96,64},{1,97},{33,1},{65,33},{97,65},{2,98}... | collective-permute-start | bytes 2359304 | tf_op jit(solution)/shard_map/while/body/ppermute | solution.py:20
  70.2 22.8 %collective-permute-start.9 = (bf16[3,128,1024]{2,1,0:T(8,128)(2,1)}, bf16[3,128,1024]{2,1,0:T(8,128)(2,1)}, u32[]{:S(2)}, u32[]{:S(2)}) collective-permute-start(bf16[3,128,1024]{2,1,0:T(8,128)(2,1)} %get-tuple-element.777), channel_id=1, source_target_pairs={{0,32},{32,64},{64,96},{96,0},{1,33},{33,65},{65,97},{97,1},{2,34}... | collective-permute-start | bytes 2359304 | tf_op jit(solution)/shard_map/while/body/ppermute | solution.py:20
  70.2 26.8 %collective-permute-start.12 = (bf16[384,1024]{1,0:T(8,128)(2,1)}, bf16[384,1024]{1,0:T(8,128)(2,1)}, u32[]{:S(2)}, u32[]{:S(2)}) collective-permute-start(bf16[384,1024]{1,0:T(8,128)(2,1)} %body.77.refs_0_), channel_id=1, source_target_pairs={{0,8},{8,0},{1,9},{9,1},{2,10},{10,2},{3,11},{11,3},{4,12},{12,4},... | collective-permute-start | bytes 2359304 | tf_op jit(solution)/shard_map/while/body/ppermute | solution.py:20
  73.2 13.6 %collective-permute-start.14 = (bf16[192,1024]{1,0:T(8,128)(2,1)S(1)}, bf16[192,1024]{1,0:T(8,128)(2,1)S(1)}, u32[]{:S(2)}, u32[]{:S(2)}) collective-permute-start(bf16[192,1024]{1,0:T(8,128)(2,1)S(1)} %copy-done.7), channel_id=1, source_target_pairs={{0,4},{2,6},{4,0},{6,2},{1,5},{3,7},{5,1},{7,3},{8,12},{10,14},{12... | collective-permute-start | bytes 1179656 | tf_op jit(solution)/shard_map/while/body/ppermute | solution.py:20
  73.4 19.7 %collective-permute-start.15 = (bf16[192,1024]{1,0:T(8,128)(2,1)S(1)}, bf16[192,1024]{1,0:T(8,128)(2,1)S(1)}, u32[]{:S(2)}, u32[]{:S(2)}) collective-permute-start(bf16[192,1024]{1,0:T(8,128)(2,1)S(1)} %copy-done.7), channel_id=1, source_target_pairs={{0,2},{2,4},{4,6},{6,0},{1,3},{3,5},{5,7},{7,1},{8,10},{10,12},{12... | collective-permute-start | bytes 1179656 | tf_op jit(solution)/shard_map/while/body/ppermute | solution.py:20
  105.6 21.7 %collective-permute-start.10 = (bf16[3,128,1024]{2,1,0:T(8,128)(2,1)}, bf16[3,128,1024]{2,1,0:T(8,128)(2,1)}, u32[]{:S(2)}, u32[]{:S(2)}) collective-permute-start(bf16[3,128,1024]{2,1,0:T(8,128)(2,1)} %get-tuple-element.778), channel_id=1, source_target_pairs={{0,64},{32,96},{64,0},{96,32},{1,65},{33,97},{65,1},{97,33},{2,66}... | collective-permute-start | bytes 2359304 | tf_op jit(solution)/shard_map/while/body/ppermute | solution.py:20
  120.7 46.0 %collective-permute-start.22 = (bf16[3,256,1024]{2,1,0:T(8,128)(2,1)}, bf16[3,256,1024]{2,1,0:T(8,128)(2,1)}, u32[]{:S(2)}, u32[]{:S(2)}) collective-permute-start(bf16[3,256,1024]{2,1,0:T(8,128)(2,1)} %get-tuple-element.797), channel_id=1, source_target_pairs={{0,16},{16,0},{1,17},{17,1},{2,18},{18,2},{3,19},{19,3},{4,20},{20... | collective-permute-start | bytes 4718600 | tf_op jit(solution)/shard_map/while/body/ppermute | solution.py:20
  130.6 35.1 %collective-permute-start.18 = (bf16[3,64,1024]{2,1,0:T(8,128)(2,1)}, bf16[3,64,1024]{2,1,0:T(8,128)(2,1)}, u32[]{:S(2)}, u32[]{:S(2)}) collective-permute-start(bf16[3,64,1024]{2,1,0:T(8,128)(2,1)} %slice.533), channel_id=1, source_target_pairs={{0,16},{16,0},{1,17},{17,1},{2,18},{18,2},{3,19},{19,3},{4,20},{20... | collective-permute-start | bytes 1179656 | tf_op jit(solution)/shard_map/while/body/ppermute | solution.py:20
  147.3 22.2 %collective-permute-start.19 = (bf16[3,128,1024]{2,1,0:T(8,128)(2,1)}, bf16[3,128,1024]{2,1,0:T(8,128)(2,1)S(1)}, u32[]{:S(2)}, u32[]{:S(2)}) collective-permute-start(bf16[3,128,1024]{2,1,0:T(8,128)(2,1)} %get-tuple-element.793), channel_id=1, source_target_pairs={{0,32},{32,64},{64,96},{96,0},{1,33},{33,65},{65,97},{97,1},{2,34}... | collective-permute-start | bytes 2359304 | tf_op jit(solution)/shard_map/while/body/ppermute | solution.py:20
  147.9 37.3 %collective-permute-start.20 = (bf16[3,128,1024]{2,1,0:T(8,128)(2,1)}, bf16[3,128,1024]{2,1,0:T(8,128)(2,1)S(1)}, u32[]{:S(2)}, u32[]{:S(2)}) collective-permute-start(bf16[3,128,1024]{2,1,0:T(8,128)(2,1)} %get-tuple-element.794), channel_id=1, source_target_pairs={{0,64},{32,96},{64,0},{96,32},{1,65},{33,97},{65,1},{97,33},{2,66}... | collective-permute-start | bytes 2359304 | tf_op jit(solution)/shard_map/while/body/ppermute | solution.py:20
  151.8 33.5 %collective-permute-start.21 = (bf16[3,128,1024]{2,1,0:T(8,128)(2,1)}, bf16[3,128,1024]{2,1,0:T(8,128)(2,1)S(1)}, u32[]{:S(2)}, u32[]{:S(2)}) collective-permute-start(bf16[3,128,1024]{2,1,0:T(8,128)(2,1)} %get-tuple-element.795), channel_id=1, source_target_pairs={{0,96},{32,0},{64,32},{96,64},{1,97},{33,1},{65,33},{97,65},{2,98}... | collective-permute-start | bytes 2359304 | tf_op jit(solution)/shard_map/while/body/ppermute | solution.py:20
  185.9 11.5 %collective-permute-start.24 = (bf16[3,64,1024]{2,1,0:T(8,128)(2,1)S(1)}, bf16[3,64,1024]{2,1,0:T(8,128)(2,1)S(1)}, u32[]{:S(2)}, u32[]{:S(2)}) collective-permute-start(bf16[3,64,1024]{2,1,0:T(8,128)(2,1)S(1)} %get-tuple-element.811), channel_id=1, source_target_pairs={{0,32},{32,64},{64,96},{96,0},{1,33},{33,65},{65,97},{97,1},{2,34}... | collective-permute-start | bytes 1179656 | tf_op jit(solution)/shard_map/while/body/ppermute | solution.py:20
  186.7 20.3 %collective-permute-start.25 = (bf16[3,64,1024]{2,1,0:T(8,128)(2,1)S(1)}, bf16[3,64,1024]{2,1,0:T(8,128)(2,1)S(1)}, u32[]{:S(2)}, u32[]{:S(2)}) collective-permute-start(bf16[3,64,1024]{2,1,0:T(8,128)(2,1)S(1)} %get-tuple-element.812), channel_id=1, source_target_pairs={{0,64},{32,96},{64,0},{96,32},{1,65},{33,97},{65,1},{97,33},{2,66}... | collective-permute-start | bytes 1179656 | tf_op jit(solution)/shard_map/while/body/ppermute | solution.py:20
  189.6 17.4 %collective-permute-start.26 = (bf16[3,64,1024]{2,1,0:T(8,128)(2,1)S(1)}, bf16[3,64,1024]{2,1,0:T(8,128)(2,1)S(1)}, u32[]{:S(2)}, u32[]{:S(2)}) collective-permute-start(bf16[3,64,1024]{2,1,0:T(8,128)(2,1)S(1)} %get-tuple-element.813), channel_id=1, source_target_pairs={{0,96},{32,0},{64,32},{96,64},{1,97},{33,1},{65,33},{97,65},{2,98}... | collective-permute-start | bytes 1179656 | tf_op jit(solution)/shard_map/while/body/ppermute | solution.py:20
  191.1 19.3 %collective-permute-start.23 = (bf16[2,64,1024]{2,1,0:T(8,128)(2,1)S(1)}, bf16[2,64,1024]{2,1,0:T(8,128)(2,1)}, u32[]{:S(2)}, u32[]{:S(2)}) collective-permute-start(bf16[2,64,1024]{2,1,0:T(8,128)(2,1)S(1)} %pad_maximum_fusion.10.refs_0_), channel_id=1, source_target_pairs={{0,16},{16,0},{1,17},{17,1},{2,18},{18,2},{3,19},{19,3},{4,20},{20... | collective-permute-start | bytes 786440 | tf_op jit(solution)/shard_map/while/body/ppermute | solution.py:20
  192.8 20.2 %collective-permute-start.33 = (bf16[3,64,1024]{2,1,0:T(8,128)(2,1)}, bf16[3,64,1024]{2,1,0:T(8,128)(2,1)}, u32[]{:S(2)}, u32[]{:S(2)}) collective-permute-start(bf16[3,64,1024]{2,1,0:T(8,128)(2,1)} %slice.536), channel_id=1, source_target_pairs={{0,16},{16,0},{1,17},{17,1},{2,18},{18,2},{3,19},{19,3},{4,20},{20... | collective-permute-start | bytes 1179656 | tf_op jit(solution)/shard_map/while/body/ppermute | solution.py:20
  208.2 12.2 %collective-permute-start.30 = (bf16[2,64,1024]{2,1,0:T(8,128)(2,1)}, bf16[2,64,1024]{2,1,0:T(8,128)(2,1)}, u32[]{:S(2)}, u32[]{:S(2)}) collective-permute-start(bf16[2,64,1024]{2,1,0:T(8,128)(2,1)} %pad_maximum_fusion.11.refs_0_), channel_id=1, source_target_pairs={{0,96},{32,0},{64,32},{96,64},{1,97},{33,1},{65,33},{97,65},{2,98}... | collective-permute-start | bytes 786440 | tf_op jit(solution)/shard_map/while/body/ppermute | solution.py:20
  215.0 10.8 %collective-permute-start.34 = (bf16[1,192,1024]{2,1,0:T(8,128)(2,1)S(1)}, bf16[1,192,1024]{2,1,0:T(8,128)(2,1)S(1)}, u32[]{:S(2)}, u32[]{:S(2)}) collective-permute-start(bf16[1,192,1024]{2,1,0:T(8,128)(2,1)S(1)} %maximum_bitcast_fusion.2.refs_0_), channel_id=1, source_target_pairs={{0,16},{16,0},{1,17},{17,1},{2,18},{18,2},{3,19},{19,3},{4,20},{20... | collective-permute-start | bytes 1179656 | tf_op jit(solution)/shard_map/while/body/ppermute | solution.py:20
  216.5 13.5 %collective-permute-start.31 = (bf16[2,64,1024]{2,1,0:T(8,128)(2,1)}, bf16[2,64,1024]{2,1,0:T(8,128)(2,1)}, u32[]{:S(2)}, u32[]{:S(2)}) collective-permute-start(bf16[2,64,1024]{2,1,0:T(8,128)(2,1)} %pad_maximum_fusion.11.refs_0_), channel_id=1, source_target_pairs={{0,64},{32,96},{64,0},{96,32},{1,65},{33,97},{65,1},{97,33},{2,66}... | collective-permute-start | bytes 786440 | tf_op jit(solution)/shard_map/while/body/ppermute | solution.py:20
  217.2 16.0 %collective-permute-start.32 = (bf16[2,64,1024]{2,1,0:T(8,128)(2,1)}, bf16[2,64,1024]{2,1,0:T(8,128)(2,1)}, u32[]{:S(2)}, u32[]{:S(2)}) collective-permute-start(bf16[2,64,1024]{2,1,0:T(8,128)(2,1)} %pad_maximum_fusion.11.refs_0_), channel_id=1, source_target_pairs={{0,32},{32,64},{64,96},{96,0},{1,33},{33,65},{65,97},{97,1},{2,34}... | collective-permute-start | bytes 786440 | tf_op jit(solution)/shard_map/while/body/ppermute | solution.py:20
  217.4 26.3 %collective-permute-start.27 = (bf16[2,128,1024]{2,1,0:T(8,128)(2,1)}, bf16[2,128,1024]{2,1,0:T(8,128)(2,1)}, u32[]{:S(2)}, u32[]{:S(2)}) collective-permute-start(bf16[2,128,1024]{2,1,0:T(8,128)(2,1)} %body.83.refs_0_), channel_id=1, source_target_pairs={{0,96},{32,0},{64,32},{96,64},{1,97},{33,1},{65,33},{97,65},{2,98}... | collective-permute-start | bytes 1572872 | tf_op jit(solution)/shard_map/while/body/ppermute | solution.py:20
  220.4 24.1 %collective-permute-start.28 = (bf16[2,128,1024]{2,1,0:T(8,128)(2,1)}, bf16[2,128,1024]{2,1,0:T(8,128)(2,1)}, u32[]{:S(2)}, u32[]{:S(2)}) collective-permute-start(bf16[2,128,1024]{2,1,0:T(8,128)(2,1)} %body.83.refs_0_), channel_id=1, source_target_pairs={{0,64},{32,96},{64,0},{96,32},{1,65},{33,97},{65,1},{97,33},{2,66}... | collective-permute-start | bytes 1572872 | tf_op jit(solution)/shard_map/while/body/ppermute | solution.py:20
  225.9 11.9 %collective-permute-start.36 = (bf16[2,64,1024]{2,1,0:T(8,128)(2,1)S(1)}, bf16[2,64,1024]{2,1,0:T(8,128)(2,1)}, u32[]{:S(2)}, u32[]{:S(2)}) collective-permute-start(bf16[2,64,1024]{2,1,0:T(8,128)(2,1)S(1)} %pad_maximum_fusion.12.refs_0_), channel_id=1, source_target_pairs={{0,16},{16,0},{1,17},{17,1},{2,18},{18,2},{3,19},{19,3},{4,20},{20... | collective-permute-start | bytes 786440 | tf_op jit(solution)/shard_map/while/body/ppermute | solution.py:20
  236.2 40.5 %collective-permute-start.35 = (bf16[2,256,1024]{2,1,0:T(8,128)(2,1)}, bf16[2,256,1024]{2,1,0:T(8,128)(2,1)}, u32[]{:S(2)}, u32[]{:S(2)}) collective-permute-start(bf16[2,256,1024]{2,1,0:T(8,128)(2,1)} %body.85.refs_0_), channel_id=1, source_target_pairs={{0,16},{16,0},{1,17},{17,1},{2,18},{18,2},{3,19},{19,3},{4,20},{20... | collective-permute-start | bytes 3145736 | tf_op jit(solution)/shard_map/while/body/ppermute | solution.py:20
  237.7 27.7 %collective-permute-start.29 = (bf16[2,128,1024]{2,1,0:T(8,128)(2,1)}, bf16[2,128,1024]{2,1,0:T(8,128)(2,1)}, u32[]{:S(2)}, u32[]{:S(2)}) collective-permute-start(bf16[2,128,1024]{2,1,0:T(8,128)(2,1)} %body.83.refs_0_), channel_id=1, source_target_pairs={{0,32},{32,64},{64,96},{96,0},{1,33},{33,65},{65,97},{97,1},{2,34}... | collective-permute-start | bytes 1572872 | tf_op jit(solution)/shard_map/while/body/ppermute | solution.py:20
  240.4 25.0 %collective-permute-start.37 = (bf16[2,128,1024]{2,1,0:T(8,128)(2,1)}, bf16[2,128,1024]{2,1,0:T(8,128)(2,1)}, u32[]{:S(2)}, u32[]{:S(2)}) collective-permute-start(bf16[2,128,1024]{2,1,0:T(8,128)(2,1)} %body.86.refs_2_), channel_id=1, source_target_pairs={{0,96},{32,0},{64,32},{96,64},{1,97},{33,1},{65,33},{97,65},{2,98}... | collective-permute-start | bytes 1572872 | tf_op jit(solution)/shard_map/while/body/ppermute | solution.py:20
  243.7 23.3 %collective-permute-start.38 = (bf16[2,128,1024]{2,1,0:T(8,128)(2,1)}, bf16[2,128,1024]{2,1,0:T(8,128)(2,1)}, u32[]{:S(2)}, u32[]{:S(2)}) collective-permute-start(bf16[2,128,1024]{2,1,0:T(8,128)(2,1)} %body.86.refs_2_), channel_id=1, source_target_pairs={{0,64},{32,96},{64,0},{96,32},{1,65},{33,97},{65,1},{97,33},{2,66}... | collective-permute-start | bytes 1572872 | tf_op jit(solution)/shard_map/while/body/ppermute | solution.py:20
  244.5 32.2 %collective-permute-start.39 = (bf16[2,128,1024]{2,1,0:T(8,128)(2,1)}, bf16[2,128,1024]{2,1,0:T(8,128)(2,1)}, u32[]{:S(2)}, u32[]{:S(2)}) collective-permute-start(bf16[2,128,1024]{2,1,0:T(8,128)(2,1)} %body.86.refs_2_), channel_id=1, source_target_pairs={{0,32},{32,64},{64,96},{96,0},{1,33},{33,65},{65,97},{97,1},{2,34}... | collective-permute-start | bytes 1572872 | tf_op jit(solution)/shard_map/while/body/ppermute | solution.py:20
  289.8 11.8 %collective-permute-start.41 = (bf16[768,1024]{1,0:T(8,128)(2,1)}, bf16[768,1024]{1,0:T(8,128)(2,1)S(1)}, u32[]{:S(2)}, u32[]{:S(2)}) collective-permute-start(bf16[768,1024]{1,0:T(8,128)(2,1)} %get-tuple-element.850), channel_id=1, source_target_pairs={{0,1},{1,0},{2,3},{3,2},{4,5},{5,4},{6,7},{7,6},{8,9},{9,8},{10,11... | collective-permute-start | bytes 4718600 | tf_op jit(solution)/shard_map/while/body/ppermute | solution.py:20
  293.0 25.6 %collective-permute-start.54 = (bf16[1,384,1024]{2,1,0:T(8,128)(2,1)}, bf16[1,384,1024]{2,1,0:T(8,128)(2,1)}, u32[]{:S(2)}, u32[]{:S(2)}) collective-permute-start(bf16[1,384,1024]{2,1,0:T(8,128)(2,1)} %body.84.refs_0_), channel_id=1, source_target_pairs={{0,96},{32,0},{64,32},{96,64},{1,97},{33,1},{65,33},{97,65},{2,98}... | collective-permute-start | bytes 2359304 | tf_op jit(solution)/shard_map/while/body/ppermute | solution.py:20
  293.5 25.1 %collective-permute-start.55 = (bf16[1,384,1024]{2,1,0:T(8,128)(2,1)}, bf16[1,384,1024]{2,1,0:T(8,128)(2,1)}, u32[]{:S(2)}, u32[]{:S(2)}) collective-permute-start(bf16[1,384,1024]{2,1,0:T(8,128)(2,1)} %body.84.refs_0_), channel_id=1, source_target_pairs={{0,64},{32,96},{64,0},{96,32},{1,65},{33,97},{65,1},{97,33},{2,66}... | collective-permute-start | bytes 2359304 | tf_op jit(solution)/shard_map/while/body/ppermute | solution.py:20
  294.2 37.6 %collective-permute-start.56 = (bf16[1,384,1024]{2,1,0:T(8,128)(2,1)}, bf16[1,384,1024]{2,1,0:T(8,128)(2,1)}, u32[]{:S(2)}, u32[]{:S(2)}) collective-permute-start(bf16[1,384,1024]{2,1,0:T(8,128)(2,1)} %body.84.refs_0_), channel_id=1, source_target_pairs={{0,32},{32,64},{64,96},{96,0},{1,33},{33,65},{65,97},{97,1},{2,34}... | collective-permute-start | bytes 2359304 | tf_op jit(solution)/shard_map/while/body/ppermute | solution.py:20
  301.3 38.3 %collective-permute-start.40 = (bf16[256,1024]{1,0:T(8,128)(2,1)}, bf16[256,1024]{1,0:T(8,128)(2,1)}, u32[]{:S(2)}, u32[]{:S(2)}) collective-permute-start(bf16[256,1024]{1,0:T(8,128)(2,1)} %get-tuple-element.848), channel_id=1, source_target_pairs={{0,1},{1,0},{2,3},{3,2},{4,5},{5,4},{6,7},{7,6},{8,9},{9,8},{10,11... | collective-permute-start | bytes 1572872 | tf_op jit(solution)/shard_map/while/body/ppermute | solution.py:20
  309.1 30.6 %collective-permute-start.42 = (bf16[4,96,512]{2,1,0:T(8,128)(2,1)}, bf16[4,96,512]{2,1,0:T(8,128)(2,1)S(1)}, u32[]{:S(2)}, u32[]{:S(2)}) collective-permute-start(bf16[4,96,512]{2,1,0:T(8,128)(2,1)} %slice_bitcast_fusion.14), channel_id=1, source_target_pairs={{0,8},{8,0},{1,9},{9,1},{2,10},{10,2},{3,11},{11,3},{4,12},{12,4},... | collective-permute-start | bytes 1179656 | tf_op jit(solution)/shard_map/while/body/ppermute | solution.py:20
  318.6 21.0 %collective-permute-start.43 = (bf16[2,96,512]{2,1,0:T(8,128)(2,1)}, bf16[2,96,512]{2,1,0:T(8,128)(2,1)}, u32[]{:S(2)}, u32[]{:S(2)}) collective-permute-start(bf16[2,96,512]{2,1,0:T(8,128)(2,1)} %get-tuple-element.853), channel_id=1, source_target_pairs={{0,2},{2,4},{4,6},{6,0},{1,3},{3,5},{5,7},{7,1},{8,10},{10,12},{12... | collective-permute-start | bytes 589832 | tf_op jit(solution)/shard_map/while/body/ppermute | solution.py:20
  318.6 21.0 %collective-permute-start.44 = (bf16[2,96,512]{2,1,0:T(8,128)(2,1)}, bf16[2,96,512]{2,1,0:T(8,128)(2,1)}, u32[]{:S(2)}, u32[]{:S(2)}) collective-permute-start(bf16[2,96,512]{2,1,0:T(8,128)(2,1)} %get-tuple-element.854), channel_id=1, source_target_pairs={{0,4},{2,6},{4,0},{6,2},{1,5},{3,7},{5,1},{7,3},{8,12},{10,14},{12... | collective-permute-start | bytes 589832 | tf_op jit(solution)/shard_map/while/body/ppermute | solution.py:20
  339.8 14.0 %collective-permute-start.48 = (bf16[96,512]{1,0:T(8,128)(2,1)S(1)}, bf16[96,512]{1,0:T(8,128)(2,1)S(1)}, u32[]{:S(2)}, u32[]{:S(2)}) collective-permute-start(bf16[96,512]{1,0:T(8,128)(2,1)S(1)} %get-tuple-element.865), channel_id=1, source_target_pairs={{0,2},{2,4},{4,6},{6,0},{1,3},{3,5},{5,7},{7,1},{8,10},{10,12},{12... | collective-permute-start | bytes 294920 | tf_op jit(solution)/shard_map/while/body/ppermute | solution.py:20
  341.3 12.5 %collective-permute-start.49 = (bf16[96,512]{1,0:T(8,128)(2,1)S(1)}, bf16[96,512]{1,0:T(8,128)(2,1)S(1)}, u32[]{:S(2)}, u32[]{:S(2)}) collective-permute-start(bf16[96,512]{1,0:T(8,128)(2,1)S(1)} %get-tuple-element.866), channel_id=1, source_target_pairs={{0,4},{2,6},{4,0},{6,2},{1,5},{3,7},{5,1},{7,3},{8,12},{10,14},{12... | collective-permute-start | bytes 294920 | tf_op jit(solution)/shard_map/while/body/ppermute | solution.py:20
  342.5 11.3 %collective-permute-start.50 = (bf16[96,512]{1,0:T(8,128)(2,1)S(1)}, bf16[96,512]{1,0:T(8,128)(2,1)S(1)}, u32[]{:S(2)}, u32[]{:S(2)}) collective-permute-start(bf16[96,512]{1,0:T(8,128)(2,1)S(1)} %get-tuple-element.867), channel_id=1, source_target_pairs={{0,6},{2,0},{4,2},{6,4},{1,7},{3,1},{5,3},{7,5},{8,14},{10,8},{12,... | collective-permute-start | bytes 294920 | tf_op jit(solution)/shard_map/while/body/ppermute | solution.py:20
  348.3 9.3 %collective-permute-start.46 = (bf16[128,1024]{1,0:T(8,128)(2,1)S(1)}, bf16[128,1024]{1,0:T(8,128)(2,1)S(1)}, u32[]{:S(2)}, u32[]{:S(2)}) collective-permute-start(bf16[128,1024]{1,0:T(8,128)(2,1)S(1)} %slice.537), channel_id=1, source_target_pairs={{0,8},{8,0},{1,9},{9,1},{2,10},{10,2},{3,11},{11,3},{4,12},{12,4},... | collective-permute-start | bytes 786440 | tf_op jit(solution)/shard_map/while/body/ppermute | solution.py:20
  (63 other events, 555.1 us)

commit v4 on v0

--- a/solution.py
+++ b/solution.py
@@ -270,7 +270,7 @@
 
     dgd, dud, *halves = unproject(place, after(pair_b, *pieces0[1:], *pieces_a, *all_b)[3:], jobs1, cap, weights[:2], rank[:, None])
     swap1 = shift(halves[1], "c", 2, 1)
-    dg0, du0, *halves0 = unproject(place, after(dgd, *pieces0), jobs0, 8 * r0, weights[:2], None)
+    dg0, du0, *halves0 = unproject(place, after(dgd, all_h[1], all_h[3], *pieces0)[2:], jobs0, 8 * r0, weights[:2], None)
     swap0 = shift(halves0[1], "c", 2, 1)
     xd, gd = jnp.concatenate([xa, xb], axis=0), jnp.concatenate([ga, gb], axis=0)
 

time: 374 us -> 396 us (1.059)
  waiting for transfers between devices: 137 us -> 159 us
    ppermute x57, waiting for transfers between devices: 137 us -> 159 us  [shift(): lax.ppermute(value, axis, [(i, (i + step) % size) for i in range(size)])]
    while x104 -> x108, local copies, waits for them, and re-layouts: 7.65 us -> 8.23 us
  transfers between devices with their start and end apart: 57 -> 57, of which waited for: 23 -> 25; matrix products, arithmetic and copies ran while one was open for 13% -> 11% of each run, Pallas kernels for 19% -> 18%
where the time goes in v4:
time: 396 us; the launch traced here: 394 us
  waiting for transfers between devices  159 us (40%)
  Pallas kernels  91.9 us (23%)
  starting transfers between devices  77.8 us (20%)
  other arithmetic  30.4 us (8%)
  local copies, waits for them, and re-layouts  17.1 us (4%)
  matrix products  13.7 us (3%)
    ppermute x57, waiting for transfers between devices, shift(): lax.ppermute(value, axis, [(i, (i + step) % size) for i in range(size)])  159 us
    ppermute x57, starting transfers between devices, shift(): lax.ppermute(value, axis, [(i, (i + step) % size) for i in range(size)])  77.8 us
    pallas_call x3, Pallas kernels, project(): pl.pallas_call(kernel, out_shape=[jax.ShapeDtypeStruct(s, BF) for s in sh...  37.2 us
    pallas_call x12, Pallas kernels, move(): pl.pallas_call(kernel, out_shape=[jax.ShapeDtypeStruct(s, BF) for s in sh...  35.5 us
    pallas_call x2, Pallas kernels, unproject(): pl.pallas_call(kernel, out_shape=[jax.ShapeDtypeStruct(s, BF) for s in sh...  19.3 us
    dot_general x6, matrix products, dot(): lax.dot_general(left, right, ((dims[:1], dims[1:]), ((), ())), preferred_...  13.7 us
    while x108, local copies, waits for them, and re-layouts  8.23 us
  transfers between devices with their start and end apart: 57, of which 25 were waited for; matrix products, arithmetic and copies ran while one was open for 11% of the time, Pallas kernels for 18%

profile of v4, /device:TPU:0, one launch (start us, length us, event | category | flops | bytes accessed | tf_op | source)
XLA Modules:
  0.0 394.4 jit_solution(17652040384447045068)
XLA Ops:
  5.0 387.5 %while.21 = (s32[]{:T(128)}, bf16[32,1024]{1,0:T(8,128)(2,1)}, bf16[96,1024]{1,0:T(8,128)(2,1)}, bf16[960,1024]{1,0:T(8,128)(2,1)}, bf16[960,1024]{1,0:T(8,128)(...) while((s32[]{:T(128)}, bf16[32,1024]{1,0:T(8,128)(2,1)}, ...), condition=%wide.region_4.5_spmd, body=%wide.region_1.4_spmd.sunk | while | flops 9105185792 | bytes 420481024 | solution.py:377
  6.3 3.2 collective-permute-start
  9.5 3.5 collective-permute-done.refs_1_
  15.8 4.3 %collective-permute-start.1 = (bf16[128,1024]{1,0:T(8,128)(2,1)}, bf16[128,1024]{1,0:T(8,128)(2,1)S(1)}, u32[]{:S(2)}, u32[]{:S(2)}) collective-permute-start(bf16[128,1024]{1,0:T(8,128)(2,1)} %body.73.refs_0_), channel_id=1, source_target_pairs={{0,6},{2,0},{4,2},{6,4},{1,7},{3,1},{5,3},{7,5},{8,14},{10,8},{12,... | collective-permute-start | bytes 786440 | tf_op jit(solution)/shard_map/while/body/ppermute | solution.py:20
  21.4 9.4 %collective-permute-done.1.refs_1_ = bf16[128,1024]{1,0:T(8,128)(2,1)S(1)} collective-permute-done((bf16[128,1024]{1,0:T(8,128)(2,1)}, bf16[128,1024]{1,0:T(8,128)(2,1)S(1)}, u32[]{:S(2)}, u32[]{:S(2)}) %collective-permute-start.1) | collective-permute-done | bytes 262176 | tf_op jit(solution)/shard_map/while/body/ppermute | solution.py:20
  31.1 3.0 collective-permute-done.3.refs_3_
  34.8 2.9 body.74.refs_0_
  37.9 3.1 collective-permute-start.5
  43.1 3.8 collective-permute-done.5.refs_1_
  51.5 3.7 body.76
  55.2 2.7 body.77.refs_0_
  58.0 10.9 %body.78 = (bf16[3,128,1024]{2,1,0:T(8,128)(2,1)}, bf16[3,128,1024]{2,1,0:T(8,128)(2,1)}, bf16[3,128,1024]{2,1,0:T(8,128)(2,1)}, bf16[3,128,1024]{2,1,0:T(8,128)(2,1)}) custom-call(s32[2]{0:T(128)S(1)} %get-tuple-element.943.place_ref, bf16[512,1024]{1,0:T(8,128)(2,1)} %get-tuple-element.774.refs_0_, bf16[512,1024]{1,0:T(8,128)(2,1)} %get-tuple-element.775.refs_1_, ...), custom_call_target="tpu_custom_call" | custom-call | tf_op jit(solution)/shard_map/while/body/pallas_call | solution.py:141
  68.9 3.1 collective-permute-start.11
  72.0 3.0 collective-permute-start.12
  76.0 12.5 %collective-permute-done.14.refs_2_ = bf16[192,1024]{1,0:T(8,128)(2,1)S(1)} collective-permute-done((bf16[192,1024]{1,0:T(8,128)(2,1)S(1)}, bf16[192,1024]{1,0:T(8,128)(2,1)S(1)}, u32[]{:S(2)}, u32[]{:S(2)}) %collective-permute-start.14) | collective-permute-done | bytes 393248 | tf_op jit(solution)/shard_map/while/body/ppermute | solution.py:20
  88.6 6.3 %collective-permute-done.15.refs_3_ = bf16[192,1024]{1,0:T(8,128)(2,1)S(1)} collective-permute-done((bf16[192,1024]{1,0:T(8,128)(2,1)S(1)}, bf16[192,1024]{1,0:T(8,128)(2,1)S(1)}, u32[]{:S(2)}, u32[]{:S(2)}) %collective-permute-start.15) | collective-permute-done | bytes 393248 | tf_op jit(solution)/shard_map/while/body/ppermute | solution.py:20
  95.6 3.3 body.79.refs_3_
  98.9 3.1 body.80.refs_1_
  111.0 11.3 %body.81 = (bf16[512,1024]{1,0:T(8,128)(2,1)}, bf16[512,1024]{1,0:T(8,128)(2,1)}, bf16[3,256,1024]{2,1,0:T(8,128)(2,1)}, bf16[3,256,1024]{2,1,0:T(8,128)(2,1)}) custom-call(s32[2]{0:T(128)} %copy-done.32, s32[1,1536]{1,0:T(1,128)} %fusion.144.refs_0_, bf16[768,1024]{1,0:T(8,128)(2,1)} %body.80.refs_1_, bf16[768,1024]{1,0:T(8,128)(2,1)} %collective-permute-done.16.refs_2_, ...), custom_call_target="tpu_custom_call" | custom-call | tf_op jit(solution)/shard_map/while/body/pallas_call | solution.py:141
  123.9 5.1 %collective-permute-done.10 = bf16[3,128,1024]{2,1,0:T(8,128)(2,1)} collective-permute-done((bf16[3,128,1024]{2,1,0:T(8,128)(2,1)}, bf16[3,128,1024]{2,1,0:T(8,128)(2,1)}, u32[]{:S(2)}, u32[]{:S(2)}) %collective-permute-start.10) | collective-permute-done | bytes 786464 | tf_op jit(solution)/shard_map/while/body/ppermute | solution.py:20
  134.0 14.9 %body.82 = (bf16[512,1024]{1,0:T(8,128)(2,1)}, bf16[512,1024]{1,0:T(8,128)(2,1)}, bf16[3,128,1024]{2,1,0:T(8,128)(2,1)}, bf16[3,128,1024]{2,1,0:T(8,128)(2,1)}, ...) custom-call(s32[2]{0:T(128)} %copy-done.32, s32[1,1536]{1,0:T(1,128)} %sub.274.refs_0_, ...), custom_call_target="tpu_custom_call" | custom-call | tf_op jit(solution)/shard_map/while/body/pallas_call | solution.py:141
  149.6 3.8 collective-permute-start.19
  153.6 13.7 %collective-permute-done.23 = bf16[3,64,1024]{2,1,0:T(8,128)(2,1)} collective-permute-done((bf16[3,64,1024]{2,1,0:T(8,128)(2,1)}, bf16[3,64,1024]{2,1,0:T(8,128)(2,1)}, u32[]{:S(2)}, u32[]{:S(2)}) %collective-permute-start.23) | collective-permute-done | bytes 393248 | tf_op jit(solution)/shard_map/while/body/ppermute | solution.py:20
  168.3 2.7 fusion.145
  171.1 15.8 %collective-permute-done.19 = bf16[3,128,1024]{2,1,0:T(8,128)(2,1)S(1)} collective-permute-done((bf16[3,128,1024]{2,1,0:T(8,128)(2,1)}, bf16[3,128,1024]{2,1,0:T(8,128)(2,1)S(1)}, u32[]{:S(2)}, u32[]{:S(2)}) %collective-permute-start.19) | collective-permute-done | bytes 786464 | tf_op jit(solution)/shard_map/while/body/ppermute | solution.py:20
  188.4 2.9 collective-permute-start.26
  195.8 3.3 collective-permute-done.25
  199.1 9.6 %collective-permute-done.26 = bf16[3,64,1024]{2,1,0:T(8,128)(2,1)S(1)} collective-permute-done((bf16[3,64,1024]{2,1,0:T(8,128)(2,1)S(1)}, bf16[3,64,1024]{2,1,0:T(8,128)(2,1)S(1)}, u32[]{:S(2)}, u32[]{:S(2)}) %collective-permute-start.26) | collective-permute-done | bytes 393248 | tf_op jit(solution)/shard_map/while/body/ppermute | solution.py:20
  219.0 3.0 collective-permute-start.31
  223.9 3.6 collective-permute-done.28.refs_1_
  228.9 2.8 body.84.refs_0_
  231.7 3.1 collective-permute-done.36.refs_3_
  234.8 3.0 body.85.refs_0_
  242.0 3.3 collective-permute-start.39
  246.1 5.7 %collective-permute-start.41 = (bf16[2,128,1024]{2,1,0:T(8,128)(2,1)}, bf16[2,128,1024]{2,1,0:T(8,128)(2,1)}, u32[]{:S(2)}, u32[]{:S(2)}) collective-permute-start(bf16[2,128,1024]{2,1,0:T(8,128)(2,1)} %body.86.refs_2_), channel_id=1, source_target_pairs={{0,32},{32,64},{64,96},{96,0},{1,33},{33,65},{65,97},{97,1},{2,34}... | collective-permute-start | bytes 1572872 | tf_op jit(solution)/shard_map/while/body/ppermute | solution.py:20
  251.8 3.4 fusion.149.refs_8_
  255.2 11.8 %collective-permute-done.33.refs_3_ = bf16[2,128,1024]{2,1,0:T(8,128)(2,1)} collective-permute-done((bf16[2,128,1024]{2,1,0:T(8,128)(2,1)}, bf16[2,128,1024]{2,1,0:T(8,128)(2,1)}, u32[]{:S(2)}, u32[]{:S(2)}) %collective-permute-start.33) | collective-permute-done | bytes 524320 | tf_op jit(solution)/shard_map/while/body/ppermute | solution.py:20
  268.6 9.7 %collective-permute-done.41.refs_5_ = bf16[2,128,1024]{2,1,0:T(8,128)(2,1)} collective-permute-done((bf16[2,128,1024]{2,1,0:T(8,128)(2,1)}, bf16[2,128,1024]{2,1,0:T(8,128)(2,1)}, u32[]{:S(2)}, u32[]{:S(2)}) %collective-permute-start.41) | collective-permute-done | bytes 524320 | tf_op jit(solution)/shard_map/while/body/ppermute | solution.py:20
  278.3 13.1 %body.87 = (bf16[1024,1024]{1,0:T(8,128)(2,1)}, bf16[1024,1024]{1,0:T(8,128)(2,1)}, bf16[768,1024]{1,0:T(8,128)(2,1)}, bf16[768,1024]{1,0:T(8,128)(2,1)}) custom-call(s32[2]{0:T(128)} %copy-done.32, bf16[2,256,1024]{2,1,0:T(8,128)(2,1)} %body.85.refs_0_, bf16[2,256,1024]{2,1,0:T(8,128)(2,1)} %collective-permute-done.37.refs_1_, ...), custom_call_target="tpu_custom_call" | custom-call | tf_op jit(solution)/shard_map/while/body/pallas_call | solution.py:186
  293.6 3.1 pad_maximum_fusion.13
  297.3 14.6 %collective-permute-done.29.refs_1_ = bf16[1,384,1024]{2,1,0:T(8,128)(2,1)S(1)} collective-permute-done((bf16[1,384,1024]{2,1,0:T(8,128)(2,1)S(1)}, bf16[1,384,1024]{2,1,0:T(8,128)(2,1)S(1)}, u32[]{:S(2)}, u32[]{:S(2)}) %collective-permute-start.29) | collective-permute-done | bytes 786464 | tf_op jit(solution)/shard_map/while/body/ppermute | solution.py:20
  312.0 17.9 %collective-permute-done.30.refs_3_ = bf16[1,384,1024]{2,1,0:T(8,128)(2,1)} collective-permute-done((bf16[1,384,1024]{2,1,0:T(8,128)(2,1)S(1)}, bf16[1,384,1024]{2,1,0:T(8,128)(2,1)}, u32[]{:S(2)}, u32[]{:S(2)}) %collective-permute-start.30) | collective-permute-done | bytes 786464 | tf_op jit(solution)/shard_map/while/body/ppermute | solution.py:20
  329.9 6.2 %body.88 = (bf16[512,1024]{1,0:T(8,128)(2,1)}, bf16[512,1024]{1,0:T(8,128)(2,1)}, bf16[256,1024]{1,0:T(8,128)(2,1)}, bf16[256,1024]{1,0:T(8,128)(2,1)}) custom-call(s32[2]{0:T(128)S(1)} %copy-done.33, bf16[2,128,1024]{2,1,0:T(8,128)(2,1)} %body.83.refs_0_, bf16[2,128,1024]{2,1,0:T(8,128)(2,1)} %collective-permute-done.31.refs_1_, ...), custom_call_target="tpu_custom_call" | custom-call | tf_op jit(solution)/shard_map/while/body/pallas_call | solution.py:186
  336.5 2.7 convert_add_fusion.11
  354.9 4.3 %body.89 = (bf16[512,1024]{1,0:T(8,128)(2,1)}, bf16[1024,1024]{1,0:T(8,128)(2,1)}) custom-call(s32[2]{0:T(128)S(1)} %copy-done.33, bf16[1,384,1024]{2,1,0:T(8,128)(2,1)} %body.84.refs_0_, bf16[1,384,1024]{2,1,0:T(8,128)(2,1)} %copy-done.17, bf16[1,384,1024]{2,1,0:T(8,128)(2,1)} %collective-permute-done.56.refs_2_, ...), custom_call_target="tpu_custom_call" | custom-call | tf_op jit(solution)/shard_map/while/body/pallas_call | solution.py:38
  370.9 2.9 collective-permute-start.49
  375.3 3.0 add_convert_fusion.8
  378.6 4.5 %collective-permute-done.48 = bf16[128,1024]{1,0:T(8,128)(2,1)S(1)} collective-permute-done((bf16[128,1024]{1,0:T(8,128)(2,1)S(1)}, bf16[128,1024]{1,0:T(8,128)(2,1)S(1)}, u32[]{:S(2)}, u32[]{:S(2)}) %collective-permute-start.48) | collective-permute-done | bytes 262176 | tf_op jit(solution)/shard_map/while/body/ppermute | solution.py:20
  (266 shorter events, 104.0 us)
Async XLA Ops:
  15.8 15.0 %collective-permute-start.1 = (bf16[128,1024]{1,0:T(8,128)(2,1)}, bf16[128,1024]{1,0:T(8,128)(2,1)S(1)}, u32[]{:S(2)}, u32[]{:S(2)}) collective-permute-start(bf16[128,1024]{1,0:T(8,128)(2,1)} %body.73.refs_0_), channel_id=1, source_target_pairs={{0,6},{2,0},{4,2},{6,4},{1,7},{3,1},{5,3},{7,5},{8,14},{10,8},{12,... | collective-permute-start | bytes 786440 | tf_op jit(solution)/shard_map/while/body/ppermute | solution.py:20
  20.2 11.0 %collective-permute-start.2 = (bf16[128,1024]{1,0:T(8,128)(2,1)}, bf16[128,1024]{1,0:T(8,128)(2,1)S(1)}, u32[]{:S(2)}, u32[]{:S(2)}) collective-permute-start(bf16[128,1024]{1,0:T(8,128)(2,1)} %body.73.refs_0_), channel_id=1, source_target_pairs={{0,4},{2,6},{4,0},{6,2},{1,5},{3,7},{5,1},{7,3},{8,12},{10,14},{12... | collective-permute-start | bytes 786440 | tf_op jit(solution)/shard_map/while/body/ppermute | solution.py:20
  20.2 13.9 %collective-permute-start.3 = (bf16[128,1024]{1,0:T(8,128)(2,1)}, bf16[128,1024]{1,0:T(8,128)(2,1)S(1)}, u32[]{:S(2)}, u32[]{:S(2)}) collective-permute-start(bf16[128,1024]{1,0:T(8,128)(2,1)} %body.73.refs_0_), channel_id=1, source_target_pairs={{0,2},{2,4},{4,6},{6,0},{1,3},{3,5},{5,7},{7,1},{8,10},{10,12},{12... | collective-permute-start | bytes 786440 | tf_op jit(solution)/shard_map/while/body/ppermute | solution.py:20
  37.7 12.7 %collective-permute-start.4 = (bf16[512,1024]{1,0:T(8,128)(2,1)}, bf16[512,1024]{1,0:T(8,128)(2,1)S(1)}, u32[]{:S(2)}, u32[]{:S(2)}) collective-permute-start(bf16[512,1024]{1,0:T(8,128)(2,1)} %body.74.refs_0_), channel_id=1, source_target_pairs={{0,1},{1,0},{2,3},{3,2},{4,5},{5,4},{6,7},{7,6},{8,9},{9,8},{10,11... | collective-permute-start | bytes 3145736 | tf_op jit(solution)/shard_map/while/body/ppermute | solution.py:20
  41.0 14.2 %collective-permute-start.6 = (bf16[96,1024]{1,0:T(8,128)(2,1)S(1)}, bf16[96,1024]{1,0:T(8,128)(2,1)}, u32[]{:S(2)}, u32[]{:S(2)}) collective-permute-start(bf16[96,1024]{1,0:T(8,128)(2,1)S(1)} %bitcast.161), channel_id=1, source_target_pairs={{0,6},{2,0},{4,2},{6,4},{1,7},{3,1},{5,3},{7,5},{8,14},{10,8},{12,... | collective-permute-start | bytes 589832 | tf_op jit(solution)/shard_map/while/body/ppermute | solution.py:20
  42.1 13.1 %collective-permute-start.7 = (bf16[96,1024]{1,0:T(8,128)(2,1)S(1)}, bf16[96,1024]{1,0:T(8,128)(2,1)}, u32[]{:S(2)}, u32[]{:S(2)}) collective-permute-start(bf16[96,1024]{1,0:T(8,128)(2,1)S(1)} %bitcast.162), channel_id=1, source_target_pairs={{0,4},{2,6},{4,0},{6,2},{1,5},{3,7},{5,1},{7,3},{8,12},{10,14},{12... | collective-permute-start | bytes 589832 | tf_op jit(solution)/shard_map/while/body/ppermute | solution.py:20
  42.2 13.0 %collective-permute-start.8 = (bf16[96,1024]{1,0:T(8,128)(2,1)S(1)}, bf16[96,1024]{1,0:T(8,128)(2,1)}, u32[]{:S(2)}, u32[]{:S(2)}) collective-permute-start(bf16[96,1024]{1,0:T(8,128)(2,1)S(1)} %bitcast.163), channel_id=1, source_target_pairs={{0,2},{2,4},{4,6},{6,0},{1,3},{3,5},{5,7},{7,1},{8,10},{10,12},{12... | collective-permute-start | bytes 589832 | tf_op jit(solution)/shard_map/while/body/ppermute | solution.py:20
  49.3 25.9 %collective-permute-start.13 = (bf16[192,1024]{1,0:T(8,128)(2,1)}, bf16[192,1024]{1,0:T(8,128)(2,1)}, u32[]{:S(2)}, u32[]{:S(2)}) collective-permute-start(bf16[192,1024]{1,0:T(8,128)(2,1)} %body.75.refs_0_), channel_id=1, source_target_pairs={{0,6},{2,0},{4,2},{6,4},{1,7},{3,1},{5,3},{7,5},{8,14},{10,8},{12,... | collective-permute-start | bytes 1179656 | tf_op jit(solution)/shard_map/while/body/ppermute | solution.py:20
  68.9 25.9 %collective-permute-start.11 = (bf16[3,128,1024]{2,1,0:T(8,128)(2,1)}, bf16[3,128,1024]{2,1,0:T(8,128)(2,1)}, u32[]{:S(2)}, u32[]{:S(2)}) collective-permute-start(bf16[3,128,1024]{2,1,0:T(8,128)(2,1)} %get-tuple-element.779), channel_id=1, source_target_pairs={{0,96},{32,0},{64,32},{96,64},{1,97},{33,1},{65,33},{97,65},{2,98}... | collective-permute-start | bytes 2359304 | tf_op jit(solution)/shard_map/while/body/ppermute | solution.py:20
  72.0 22.9 %collective-permute-start.9 = (bf16[3,128,1024]{2,1,0:T(8,128)(2,1)}, bf16[3,128,1024]{2,1,0:T(8,128)(2,1)}, u32[]{:S(2)}, u32[]{:S(2)}) collective-permute-start(bf16[3,128,1024]{2,1,0:T(8,128)(2,1)} %get-tuple-element.777), channel_id=1, source_target_pairs={{0,32},{32,64},{64,96},{96,0},{1,33},{33,65},{65,97},{97,1},{2,34}... | collective-permute-start | bytes 2359304 | tf_op jit(solution)/shard_map/while/body/ppermute | solution.py:20
  72.0 26.9 %collective-permute-start.12 = (bf16[384,1024]{1,0:T(8,128)(2,1)}, bf16[384,1024]{1,0:T(8,128)(2,1)}, u32[]{:S(2)}, u32[]{:S(2)}) collective-permute-start(bf16[384,1024]{1,0:T(8,128)(2,1)} %body.77.refs_0_), channel_id=1, source_target_pairs={{0,8},{8,0},{1,9},{9,1},{2,10},{10,2},{3,11},{11,3},{4,12},{12,4},... | collective-permute-start | bytes 2359304 | tf_op jit(solution)/shard_map/while/body/ppermute | solution.py:20
  75.0 13.6 %collective-permute-start.14 = (bf16[192,1024]{1,0:T(8,128)(2,1)S(1)}, bf16[192,1024]{1,0:T(8,128)(2,1)S(1)}, u32[]{:S(2)}, u32[]{:S(2)}) collective-permute-start(bf16[192,1024]{1,0:T(8,128)(2,1)S(1)} %copy-done.9), channel_id=1, source_target_pairs={{0,4},{2,6},{4,0},{6,2},{1,5},{3,7},{5,1},{7,3},{8,12},{10,14},{12... | collective-permute-start | bytes 1179656 | tf_op jit(solution)/shard_map/while/body/ppermute | solution.py:20
  75.1 19.7 %collective-permute-start.15 = (bf16[192,1024]{1,0:T(8,128)(2,1)S(1)}, bf16[192,1024]{1,0:T(8,128)(2,1)S(1)}, u32[]{:S(2)}, u32[]{:S(2)}) collective-permute-start(bf16[192,1024]{1,0:T(8,128)(2,1)S(1)} %copy-done.9), channel_id=1, source_target_pairs={{0,2},{2,4},{4,6},{6,0},{1,3},{3,5},{5,7},{7,1},{8,10},{10,12},{12... | collective-permute-start | bytes 1179656 | tf_op jit(solution)/shard_map/while/body/ppermute | solution.py:20
  107.3 21.7 %collective-permute-start.10 = (bf16[3,128,1024]{2,1,0:T(8,128)(2,1)}, bf16[3,128,1024]{2,1,0:T(8,128)(2,1)}, u32[]{:S(2)}, u32[]{:S(2)}) collective-permute-start(bf16[3,128,1024]{2,1,0:T(8,128)(2,1)} %get-tuple-element.778), channel_id=1, source_target_pairs={{0,64},{32,96},{64,0},{96,32},{1,65},{33,97},{65,1},{97,33},{2,66}... | collective-permute-start | bytes 2359304 | tf_op jit(solution)/shard_map/while/body/ppermute | solution.py:20
  122.3 46.0 %collective-permute-start.21 = (bf16[3,256,1024]{2,1,0:T(8,128)(2,1)}, bf16[3,256,1024]{2,1,0:T(8,128)(2,1)}, u32[]{:S(2)}, u32[]{:S(2)}) collective-permute-start(bf16[3,256,1024]{2,1,0:T(8,128)(2,1)} %get-tuple-element.797), channel_id=1, source_target_pairs={{0,16},{16,0},{1,17},{17,1},{2,18},{18,2},{3,19},{19,3},{4,20},{20... | collective-permute-start | bytes 4718600 | tf_op jit(solution)/shard_map/while/body/ppermute | solution.py:20
  132.2 35.0 %collective-permute-start.23 = (bf16[3,64,1024]{2,1,0:T(8,128)(2,1)}, bf16[3,64,1024]{2,1,0:T(8,128)(2,1)}, u32[]{:S(2)}, u32[]{:S(2)}) collective-permute-start(bf16[3,64,1024]{2,1,0:T(8,128)(2,1)} %slice.536), channel_id=1, source_target_pairs={{0,16},{16,0},{1,17},{17,1},{2,18},{18,2},{3,19},{19,3},{4,20},{20... | collective-permute-start | bytes 1179656 | tf_op jit(solution)/shard_map/while/body/ppermute | solution.py:20
  148.9 22.1 %collective-permute-start.18 = (bf16[3,128,1024]{2,1,0:T(8,128)(2,1)}, bf16[3,128,1024]{2,1,0:T(8,128)(2,1)S(1)}, u32[]{:S(2)}, u32[]{:S(2)}) collective-permute-start(bf16[3,128,1024]{2,1,0:T(8,128)(2,1)} %get-tuple-element.793), channel_id=1, source_target_pairs={{0,32},{32,64},{64,96},{96,0},{1,33},{33,65},{65,97},{97,1},{2,34}... | collective-permute-start | bytes 2359304 | tf_op jit(solution)/shard_map/while/body/ppermute | solution.py:20
  149.6 37.3 %collective-permute-start.19 = (bf16[3,128,1024]{2,1,0:T(8,128)(2,1)}, bf16[3,128,1024]{2,1,0:T(8,128)(2,1)S(1)}, u32[]{:S(2)}, u32[]{:S(2)}) collective-permute-start(bf16[3,128,1024]{2,1,0:T(8,128)(2,1)} %get-tuple-element.794), channel_id=1, source_target_pairs={{0,64},{32,96},{64,0},{96,32},{1,65},{33,97},{65,1},{97,33},{2,66}... | collective-permute-start | bytes 2359304 | tf_op jit(solution)/shard_map/while/body/ppermute | solution.py:20
  153.4 33.5 %collective-permute-start.20 = (bf16[3,128,1024]{2,1,0:T(8,128)(2,1)}, bf16[3,128,1024]{2,1,0:T(8,128)(2,1)S(1)}, u32[]{:S(2)}, u32[]{:S(2)}) collective-permute-start(bf16[3,128,1024]{2,1,0:T(8,128)(2,1)} %get-tuple-element.795), channel_id=1, source_target_pairs={{0,96},{32,0},{64,32},{96,64},{1,97},{33,1},{65,33},{97,65},{2,98}... | collective-permute-start | bytes 2359304 | tf_op jit(solution)/shard_map/while/body/ppermute | solution.py:20
  187.6 11.5 %collective-permute-start.25 = (bf16[3,64,1024]{2,1,0:T(8,128)(2,1)S(1)}, bf16[3,64,1024]{2,1,0:T(8,128)(2,1)S(1)}, u32[]{:S(2)}, u32[]{:S(2)}) collective-permute-start(bf16[3,64,1024]{2,1,0:T(8,128)(2,1)S(1)} %get-tuple-element.811), channel_id=1, source_target_pairs={{0,32},{32,64},{64,96},{96,0},{1,33},{33,65},{65,97},{97,1},{2,34}... | collective-permute-start | bytes 1179656 | tf_op jit(solution)/shard_map/while/body/ppermute | solution.py:20
  188.4 20.3 %collective-permute-start.26 = (bf16[3,64,1024]{2,1,0:T(8,128)(2,1)S(1)}, bf16[3,64,1024]{2,1,0:T(8,128)(2,1)S(1)}, u32[]{:S(2)}, u32[]{:S(2)}) collective-permute-start(bf16[3,64,1024]{2,1,0:T(8,128)(2,1)S(1)} %get-tuple-element.812), channel_id=1, source_target_pairs={{0,64},{32,96},{64,0},{96,32},{1,65},{33,97},{65,1},{97,33},{2,66}... | collective-permute-start | bytes 1179656 | tf_op jit(solution)/shard_map/while/body/ppermute | solution.py:20
  191.3 17.4 %collective-permute-start.27 = (bf16[3,64,1024]{2,1,0:T(8,128)(2,1)S(1)}, bf16[3,64,1024]{2,1,0:T(8,128)(2,1)S(1)}, u32[]{:S(2)}, u32[]{:S(2)}) collective-permute-start(bf16[3,64,1024]{2,1,0:T(8,128)(2,1)S(1)} %get-tuple-element.813), channel_id=1, source_target_pairs={{0,96},{32,0},{64,32},{96,64},{1,97},{33,1},{65,33},{97,65},{2,98}... | collective-permute-start | bytes 1179656 | tf_op jit(solution)/shard_map/while/body/ppermute | solution.py:20
  192.8 19.2 %collective-permute-start.24 = (bf16[2,64,1024]{2,1,0:T(8,128)(2,1)S(1)}, bf16[2,64,1024]{2,1,0:T(8,128)(2,1)}, u32[]{:S(2)}, u32[]{:S(2)}) collective-permute-start(bf16[2,64,1024]{2,1,0:T(8,128)(2,1)S(1)} %pad_maximum_fusion.10.refs_0_), channel_id=1, source_target_pairs={{0,16},{16,0},{1,17},{17,1},{2,18},{18,2},{3,19},{19,3},{4,20},{20... | collective-permute-start | bytes 786440 | tf_op jit(solution)/shard_map/while/body/ppermute | solution.py:20
  194.5 20.1 %collective-permute-start.22 = (bf16[3,64,1024]{2,1,0:T(8,128)(2,1)}, bf16[3,64,1024]{2,1,0:T(8,128)(2,1)}, u32[]{:S(2)}, u32[]{:S(2)}) collective-permute-start(bf16[3,64,1024]{2,1,0:T(8,128)(2,1)} %slice.535), channel_id=1, source_target_pairs={{0,16},{16,0},{1,17},{17,1},{2,18},{18,2},{3,19},{19,3},{4,20},{20... | collective-permute-start | bytes 1179656 | tf_op jit(solution)/shard_map/while/body/ppermute | solution.py:20
  209.8 12.2 %collective-permute-start.34 = (bf16[2,64,1024]{2,1,0:T(8,128)(2,1)}, bf16[2,64,1024]{2,1,0:T(8,128)(2,1)}, u32[]{:S(2)}, u32[]{:S(2)}) collective-permute-start(bf16[2,64,1024]{2,1,0:T(8,128)(2,1)} %pad_maximum_fusion.11.refs_0_), channel_id=1, source_target_pairs={{0,96},{32,0},{64,32},{96,64},{1,97},{33,1},{65,33},{97,65},{2,98}... | collective-permute-start | bytes 786440 | tf_op jit(solution)/shard_map/while/body/ppermute | solution.py:20
  216.6 10.8 %collective-permute-start.28 = (bf16[1,192,1024]{2,1,0:T(8,128)(2,1)S(1)}, bf16[1,192,1024]{2,1,0:T(8,128)(2,1)S(1)}, u32[]{:S(2)}, u32[]{:S(2)}) collective-permute-start(bf16[1,192,1024]{2,1,0:T(8,128)(2,1)S(1)} %maximum_bitcast_fusion.2.refs_0_), channel_id=1, source_target_pairs={{0,16},{16,0},{1,17},{17,1},{2,18},{18,2},{3,19},{19,3},{4,20},{20... | collective-permute-start | bytes 1179656 | tf_op jit(solution)/shard_map/while/body/ppermute | solution.py:20
  218.2 13.5 %collective-permute-start.35 = (bf16[2,64,1024]{2,1,0:T(8,128)(2,1)}, bf16[2,64,1024]{2,1,0:T(8,128)(2,1)}, u32[]{:S(2)}, u32[]{:S(2)}) collective-permute-start(bf16[2,64,1024]{2,1,0:T(8,128)(2,1)} %pad_maximum_fusion.11.refs_0_), channel_id=1, source_target_pairs={{0,64},{32,96},{64,0},{96,32},{1,65},{33,97},{65,1},{97,33},{2,66}... | collective-permute-start | bytes 786440 | tf_op jit(solution)/shard_map/while/body/ppermute | solution.py:20
  218.8 16.0 %collective-permute-start.36 = (bf16[2,64,1024]{2,1,0:T(8,128)(2,1)}, bf16[2,64,1024]{2,1,0:T(8,128)(2,1)}, u32[]{:S(2)}, u32[]{:S(2)}) collective-permute-start(bf16[2,64,1024]{2,1,0:T(8,128)(2,1)} %pad_maximum_fusion.11.refs_0_), channel_id=1, source_target_pairs={{0,32},{32,64},{64,96},{96,0},{1,33},{33,65},{65,97},{97,1},{2,34}... | collective-permute-start | bytes 786440 | tf_op jit(solution)/shard_map/while/body/ppermute | solution.py:20
  219.0 26.3 %collective-permute-start.31 = (bf16[2,128,1024]{2,1,0:T(8,128)(2,1)}, bf16[2,128,1024]{2,1,0:T(8,128)(2,1)}, u32[]{:S(2)}, u32[]{:S(2)}) collective-permute-start(bf16[2,128,1024]{2,1,0:T(8,128)(2,1)} %body.83.refs_0_), channel_id=1, source_target_pairs={{0,96},{32,0},{64,32},{96,64},{1,97},{33,1},{65,33},{97,65},{2,98}... | collective-permute-start | bytes 1572872 | tf_op jit(solution)/shard_map/while/body/ppermute | solution.py:20
  222.0 24.1 %collective-permute-start.32 = (bf16[2,128,1024]{2,1,0:T(8,128)(2,1)}, bf16[2,128,1024]{2,1,0:T(8,128)(2,1)}, u32[]{:S(2)}, u32[]{:S(2)}) collective-permute-start(bf16[2,128,1024]{2,1,0:T(8,128)(2,1)} %body.83.refs_0_), channel_id=1, source_target_pairs={{0,64},{32,96},{64,0},{96,32},{1,65},{33,97},{65,1},{97,33},{2,66}... | collective-permute-start | bytes 1572872 | tf_op jit(solution)/shard_map/while/body/ppermute | solution.py:20
  227.5 11.9 %collective-permute-start.38 = (bf16[2,64,1024]{2,1,0:T(8,128)(2,1)S(1)}, bf16[2,64,1024]{2,1,0:T(8,128)(2,1)}, u32[]{:S(2)}, u32[]{:S(2)}) collective-permute-start(bf16[2,64,1024]{2,1,0:T(8,128)(2,1)S(1)} %pad_maximum_fusion.12.refs_0_), channel_id=1, source_target_pairs={{0,16},{16,0},{1,17},{17,1},{2,18},{18,2},{3,19},{19,3},{4,20},{20... | collective-permute-start | bytes 786440 | tf_op jit(solution)/shard_map/while/body/ppermute | solution.py:20
  237.8 40.5 %collective-permute-start.37 = (bf16[2,256,1024]{2,1,0:T(8,128)(2,1)}, bf16[2,256,1024]{2,1,0:T(8,128)(2,1)}, u32[]{:S(2)}, u32[]{:S(2)}) collective-permute-start(bf16[2,256,1024]{2,1,0:T(8,128)(2,1)} %body.85.refs_0_), channel_id=1, source_target_pairs={{0,16},{16,0},{1,17},{17,1},{2,18},{18,2},{3,19},{19,3},{4,20},{20... | collective-permute-start | bytes 3145736 | tf_op jit(solution)/shard_map/while/body/ppermute | solution.py:20
  239.3 27.7 %collective-permute-start.33 = (bf16[2,128,1024]{2,1,0:T(8,128)(2,1)}, bf16[2,128,1024]{2,1,0:T(8,128)(2,1)}, u32[]{:S(2)}, u32[]{:S(2)}) collective-permute-start(bf16[2,128,1024]{2,1,0:T(8,128)(2,1)} %body.83.refs_0_), channel_id=1, source_target_pairs={{0,32},{32,64},{64,96},{96,0},{1,33},{33,65},{65,97},{97,1},{2,34}... | collective-permute-start | bytes 1572872 | tf_op jit(solution)/shard_map/while/body/ppermute | solution.py:20
  242.0 25.0 %collective-permute-start.39 = (bf16[2,128,1024]{2,1,0:T(8,128)(2,1)}, bf16[2,128,1024]{2,1,0:T(8,128)(2,1)}, u32[]{:S(2)}, u32[]{:S(2)}) collective-permute-start(bf16[2,128,1024]{2,1,0:T(8,128)(2,1)} %body.86.refs_2_), channel_id=1, source_target_pairs={{0,96},{32,0},{64,32},{96,64},{1,97},{33,1},{65,33},{97,65},{2,98}... | collective-permute-start | bytes 1572872 | tf_op jit(solution)/shard_map/while/body/ppermute | solution.py:20
  245.3 23.3 %collective-permute-start.40 = (bf16[2,128,1024]{2,1,0:T(8,128)(2,1)}, bf16[2,128,1024]{2,1,0:T(8,128)(2,1)}, u32[]{:S(2)}, u32[]{:S(2)}) collective-permute-start(bf16[2,128,1024]{2,1,0:T(8,128)(2,1)} %body.86.refs_2_), channel_id=1, source_target_pairs={{0,64},{32,96},{64,0},{96,32},{1,65},{33,97},{65,1},{97,33},{2,66}... | collective-permute-start | bytes 1572872 | tf_op jit(solution)/shard_map/while/body/ppermute | solution.py:20
  246.1 32.2 %collective-permute-start.41 = (bf16[2,128,1024]{2,1,0:T(8,128)(2,1)}, bf16[2,128,1024]{2,1,0:T(8,128)(2,1)}, u32[]{:S(2)}, u32[]{:S(2)}) collective-permute-start(bf16[2,128,1024]{2,1,0:T(8,128)(2,1)} %body.86.refs_2_), channel_id=1, source_target_pairs={{0,32},{32,64},{64,96},{96,0},{1,33},{33,65},{65,97},{97,1},{2,34}... | collective-permute-start | bytes 1572872 | tf_op jit(solution)/shard_map/while/body/ppermute | solution.py:20
  291.4 45.0 %collective-permute-start.43 = (bf16[768,1024]{1,0:T(8,128)(2,1)}, bf16[768,1024]{1,0:T(8,128)(2,1)}, u32[]{:S(2)}, u32[]{:S(2)}) collective-permute-start(bf16[768,1024]{1,0:T(8,128)(2,1)} %get-tuple-element.850), channel_id=1, source_target_pairs={{0,1},{1,0},{2,3},{3,2},{4,5},{5,4},{6,7},{7,6},{8,9},{9,8},{10,11... | collective-permute-start | bytes 4718600 | tf_op jit(solution)/shard_map/while/body/ppermute | solution.py:20
  291.5 20.4 %collective-permute-start.29 = (bf16[1,384,1024]{2,1,0:T(8,128)(2,1)S(1)}, bf16[1,384,1024]{2,1,0:T(8,128)(2,1)S(1)}, u32[]{:S(2)}, u32[]{:S(2)}) collective-permute-start(bf16[1,384,1024]{2,1,0:T(8,128)(2,1)S(1)} %copy-done.6), channel_id=1, source_target_pairs={{0,96},{32,0},{64,32},{96,64},{1,97},{33,1},{65,33},{97,65},{2,98}... | collective-permute-start | bytes 2359304 | tf_op jit(solution)/shard_map/while/body/ppermute | solution.py:20
  292.1 37.8 %collective-permute-start.30 = (bf16[1,384,1024]{2,1,0:T(8,128)(2,1)S(1)}, bf16[1,384,1024]{2,1,0:T(8,128)(2,1)}, u32[]{:S(2)}, u32[]{:S(2)}) collective-permute-start(bf16[1,384,1024]{2,1,0:T(8,128)(2,1)S(1)} %copy-done.6), channel_id=1, source_target_pairs={{0,32},{32,64},{64,96},{96,0},{1,33},{33,65},{65,97},{97,1},{2,34}... | collective-permute-start | bytes 2359304 | tf_op jit(solution)/shard_map/while/body/ppermute | solution.py:20
  296.7 55.7 %collective-permute-start.56 = (bf16[1,384,1024]{2,1,0:T(8,128)(2,1)S(1)}, bf16[1,384,1024]{2,1,0:T(8,128)(2,1)}, u32[]{:S(2)}, u32[]{:S(2)}) collective-permute-start(bf16[1,384,1024]{2,1,0:T(8,128)(2,1)S(1)} %copy-done.6), channel_id=1, source_target_pairs={{0,64},{32,96},{64,0},{96,32},{1,65},{33,97},{65,1},{97,33},{2,66}... | collective-permute-start | bytes 2359304 | tf_op jit(solution)/shard_map/while/body/ppermute | solution.py:20
  336.1 25.5 %collective-permute-start.42 = (bf16[256,1024]{1,0:T(8,128)(2,1)}, bf16[256,1024]{1,0:T(8,128)(2,1)S(1)}, u32[]{:S(2)}, u32[]{:S(2)}) collective-permute-start(bf16[256,1024]{1,0:T(8,128)(2,1)} %get-tuple-element.848), channel_id=1, source_target_pairs={{0,1},{1,0},{2,3},{3,2},{4,5},{5,4},{6,7},{7,6},{8,9},{9,8},{10,11... | collective-permute-start | bytes 1572872 | tf_op jit(solution)/shard_map/while/body/ppermute | solution.py:20
  342.8 18.8 %collective-permute-start.45 = (bf16[2,96,512]{2,1,0:T(8,128)(2,1)}, bf16[2,96,512]{2,1,0:T(8,128)(2,1)}, u32[]{:S(2)}, u32[]{:S(2)}) collective-permute-start(bf16[2,96,512]{2,1,0:T(8,128)(2,1)} %get-tuple-element.854), channel_id=1, source_target_pairs={{0,2},{2,4},{4,6},{6,0},{1,3},{3,5},{5,7},{7,1},{8,10},{10,12},{12... | collective-permute-start | bytes 589832 | tf_op jit(solution)/shard_map/while/body/ppermute | solution.py:20
  342.9 18.8 %collective-permute-start.46 = (bf16[2,96,512]{2,1,0:T(8,128)(2,1)}, bf16[2,96,512]{2,1,0:T(8,128)(2,1)}, u32[]{:S(2)}, u32[]{:S(2)}) collective-permute-start(bf16[2,96,512]{2,1,0:T(8,128)(2,1)} %get-tuple-element.855), channel_id=1, source_target_pairs={{0,4},{2,6},{4,0},{6,2},{1,5},{3,7},{5,1},{7,3},{8,12},{10,14},{12... | collective-permute-start | bytes 589832 | tf_op jit(solution)/shard_map/while/body/ppermute | solution.py:20
  345.0 16.7 %collective-permute-start.44 = (bf16[4,96,512]{2,1,0:T(8,128)(2,1)S(1)}, bf16[4,96,512]{2,1,0:T(8,128)(2,1)S(1)}, u32[]{:S(2)}, u32[]{:S(2)}) collective-permute-start(bf16[4,96,512]{2,1,0:T(8,128)(2,1)S(1)} %slice_bitcast_fusion.14), channel_id=1, source_target_pairs={{0,8},{8,0},{1,9},{9,1},{2,10},{10,2},{3,11},{11,3},{4,12},{12,4},... | collective-permute-start | bytes 1179656 | tf_op jit(solution)/shard_map/while/body/ppermute | solution.py:20
  364.0 14.4 %collective-permute-start.50 = (bf16[96,512]{1,0:T(8,128)(2,1)S(1)}, bf16[96,512]{1,0:T(8,128)(2,1)S(1)}, u32[]{:S(2)}, u32[]{:S(2)}) collective-permute-start(bf16[96,512]{1,0:T(8,128)(2,1)S(1)} %get-tuple-element.865), channel_id=1, source_target_pairs={{0,2},{2,4},{4,6},{6,0},{1,3},{3,5},{5,7},{7,1},{8,10},{10,12},{12... | collective-permute-start | bytes 294920 | tf_op jit(solution)/shard_map/while/body/ppermute | solution.py:20
  365.0 13.4 %collective-permute-start.51 = (bf16[96,512]{1,0:T(8,128)(2,1)S(1)}, bf16[96,512]{1,0:T(8,128)(2,1)S(1)}, u32[]{:S(2)}, u32[]{:S(2)}) collective-permute-start(bf16[96,512]{1,0:T(8,128)(2,1)S(1)} %get-tuple-element.866), channel_id=1, source_target_pairs={{0,4},{2,6},{4,0},{6,2},{1,5},{3,7},{5,1},{7,3},{8,12},{10,14},{12... | collective-permute-start | bytes 294920 | tf_op jit(solution)/shard_map/while/body/ppermute | solution.py:20
  367.1 11.3 %collective-permute-start.52 = (bf16[96,512]{1,0:T(8,128)(2,1)S(1)}, bf16[96,512]{1,0:T(8,128)(2,1)S(1)}, u32[]{:S(2)}, u32[]{:S(2)}) collective-permute-start(bf16[96,512]{1,0:T(8,128)(2,1)S(1)} %get-tuple-element.867), channel_id=1, source_target_pairs={{0,6},{2,0},{4,2},{6,4},{1,7},{3,1},{5,3},{7,5},{8,14},{10,8},{12,... | collective-permute-start | bytes 294920 | tf_op jit(solution)/shard_map/while/body/ppermute | solution.py:20
  374.0 9.1 %collective-permute-start.48 = (bf16[128,1024]{1,0:T(8,128)(2,1)S(1)}, bf16[128,1024]{1,0:T(8,128)(2,1)S(1)}, u32[]{:S(2)}, u32[]{:S(2)}) collective-permute-start(bf16[128,1024]{1,0:T(8,128)(2,1)S(1)} %slice.537), channel_id=1, source_target_pairs={{0,8},{8,0},{1,9},{9,1},{2,10},{10,2},{3,11},{11,3},{4,12},{12,4},... | collective-permute-start | bytes 786440 | tf_op jit(solution)/shard_map/while/body/ppermute | solution.py:20
  (65 other events, 657.5 us)
